TPU v7x, 512 devices: a whole 4x4x16 slice. The times are simulated.
512 devices in a mesh: lat: 64 (over y, z), wid: 8 (over x, core).
Axes of the slice: x: 4, y: 4, z: 16, core: 2. Of those that a mesh axis runs over, the one named last changes fastest.
Arguments:
- activations: bfloat16 [128, 3584], P(None, 'wid'), may hold values from -6 to 6
- encoder: bfloat16 [3584, 32768], P('wid', 'lat'), may hold values from -0.09375 to 0.09375
- encoder_bias: float32 [32768], P('lat'), may hold values from -3 to 3
- decoder: bfloat16 [32768, 3584], P('lat', 'wid'), may hold values from -0.75 to 0.75
- decoder_bias: float32 [3584], P('wid'), may hold values from -3 to 3
- kept_mask: int32 [128, 32768], P(None, 'lat'), may hold values 0 or 1
- boundaries: int32 [8], replicated, may hold values from 4097 to 32768, as said below
Outputs:
- encoder_grad: bfloat16 [3584, 32768], P('wid', 'lat')
- encoder_bias_grad: float32 [32768], P('lat')
- decoder_grad: bfloat16 [32768, 3584], P('lat', 'wid')
- decoder_bias_grad: float32 [3584], P('wid')
Inputs may be any that keep to these rules, and one draw needn't show every extreme that they name: `boundaries`: Rising; for k below 7, boundary k lies among the 512 latents that follow (k + 1) * 4096; the last equals 32768.
All inputs are finite; a program needn't handle non-finite values. No bound on the sum of `kept_mask` on one device may be relied on, other than what follows from the above.
Results may differ from a plain program's by a relative error of at most 0.006.
Values may be sent and summed in bfloat16 or wider, within the bound.
No kernel may reach another device: no remote copies, remote signals or barrier semaphores. Data moves between devices by JAX's collectives and lax.ppermute only.
A program may use at most 128 MiB of HBM per device.

v0:
```python
import jax
import jax.numpy as jnp
from jax import lax
from jax.sharding import PartitionSpec as P

GROUPS = 8


def prefix(part, axis, combine, identity, reverse):
    count = lax.axis_size(axis)
    place = lax.axis_index(axis)
    ahead = count - 1 - place if reverse else place
    gathered = lax.all_gather(part, axis)
    state = jnp.zeros_like(part) + jnp.asarray(identity, part.dtype)

    def one(step, state):
        source = count - 1 - step if reverse else step
        return combine(state, lax.dynamic_index_in_dim(gathered, source, 0, False))

    return lax.fori_loop(0, ahead, one, state)


def add_terms(earlier, later):
    return earlier + later


def body(activations, encoder, encoder_bias, decoder, decoder_bias, kept_mask, boundaries):
    latent_width = encoder.shape[1]
    first_latent = lax.axis_index("lat") * latent_width
    latent_ids = first_latent + jnp.arange(latent_width, dtype=jnp.int32)
    kept_float = kept_mask.astype(jnp.float32)
    encoder_part = jnp.dot(activations, encoder, preferred_element_type=jnp.float32)
    preacts = lax.psum(encoder_part, "wid") + encoder_bias
    codes = (kept_float * preacts).astype(jnp.bfloat16)
    inside_rows = (boundaries > first_latent) & (boundaries <= first_latent + latent_width)
    holds_cut = jnp.any(inside_rows)
    cut_point = jnp.sum(jnp.where(inside_rows, boundaries, 0))
    below_cut = latent_ids < cut_point
    zero_code = jnp.zeros((), jnp.bfloat16)
    masked_codes = jnp.stack(
        [
            jnp.where(below_cut[None, :], codes, zero_code),
            jnp.where(below_cut[None, :], zero_code, codes),
        ]
    )
    decoded_pieces = jnp.einsum(
        "sbj,jd->sbd", masked_codes, decoder, preferred_element_type=jnp.float32
    )
    local_total = decoded_pieces[0] + decoded_pieces[1]
    zero_rows = jnp.zeros_like(local_total)
    prefix_sum = prefix(local_total, "lat", add_terms, zero_rows, False)
    target_rows = activations.astype(jnp.float32)
    scaled_error = jnp.where(
        holds_cut, (decoder_bias + prefix_sum + decoded_pieces[0] - target_rows) / GROUPS, 0.0
    )
    suffix_sum = prefix(scaled_error, "lat", add_terms, zero_rows, True)
    below_suffix = suffix_sum + scaled_error
    suffix_pair = jnp.stack([below_suffix, suffix_sum]).astype(jnp.bfloat16)
    back_grads = jnp.einsum("sbd,jd->sbj", suffix_pair, decoder, preferred_element_type=jnp.float32)
    partial_grads = jnp.where(below_cut[None, :], back_grads[0], back_grads[1])
    coded_grads = lax.psum(partial_grads, "wid")
    pre_grads = kept_float * coded_grads
    encoder_bias_grad = jnp.sum(pre_grads, axis=0)
    pre_low = pre_grads.astype(jnp.bfloat16)
    encoder_grad = lax.dot_general(
        activations, pre_low, (((0,), (0,)), ((), ())), preferred_element_type=jnp.float32
    ).astype(jnp.bfloat16)
    decoder_grad = jnp.einsum(
        "sbj,sbd->jd", masked_codes, suffix_pair, preferred_element_type=jnp.float32
    ).astype(jnp.bfloat16)
    decoder_bias_grad = lax.psum(jnp.sum(scaled_error, axis=0), "lat")
    return (encoder_grad, encoder_bias_grad, decoder_grad, decoder_bias_grad)


def solution(mesh):
    placed = (
        P(None, "wid"),
        P("wid", "lat"),
        P("lat"),
        P("lat", "wid"),
        P("wid"),
        P(None, "lat"),
        P(),
    )
    return jax.shard_map(
        body,
        mesh=mesh,
        in_specs=placed,
        out_specs=(P("wid", "lat"), P("lat"), P("lat", "wid"), P("wid")),
        check_vma=False,
    )
```

profile of v0, /device:TPU:6, one launch (start us, length us, event | category | flops | bytes accessed | tf_op | source)
XLA Modules:
  0.0 781.7 jit_solution(4494470858266741804)
XLA Ops:
  7.2 2.1 fusion.19
  9.4 1.3 select_reduce_fusion
  11.3 77.0 %all-reduce.3.cloned.1.call-done = f32[128,512]{1,0:T(8,128)} async-done(((f32[128,512]{1,0:T(8,128)}), f32[128,512]{1,0:T(8,128)}) %all-reduce.3.cloned.1.call-update) | async-done | bytes 262160 | tf_op jit(solution)/shard_map/psum | solution.py:33
  88.3 1.1 select_bitcast_fusion.1
  90.5 1.3 fusion.16
  91.8 183.6 %all-gather.4.cloned.1.call-done = f32[64,128,448]{1,2,0:T(8,128)} async-done(((f32[1,128,448]{1,2,0:T(8,128)}), f32[64,128,448]{1,2,0:T(8,128)}) %all-gather.4.cloned.1.call-update) | async-done | bytes 14680080 | tf_op jit(solution)/shard_map/all_gather | solution.py:13
  275.6 2.4 fusion.17
  278.1 269.8 %all-gather.6.cloned.1.call-done = f32[8192,448]{0,1:T(8,128)} async-done(((f32[128,448]{0,1:T(8,128)}), f32[8192,448]{0,1:T(8,128)}) %all-gather.6.cloned.1.call-update) | async-done | bytes 14680080 | tf_op jit(solution)/shard_map/all_gather | solution.py:13
  547.8 16.6 %copy.25 = f32[8192,448]{1,0:T(8,128)} copy(f32[8192,448]{0,1:T(8,128)} %all-gather.6.cloned.1.call-done) | data formatting | bytes 29360128 | tf_op jit(solution)/shard_map/while | solution.py:20
  564.4 66.1 %while.23 = (s32[]{:T(128)}, f32[128,448]{1,0:T(8,128)S(1)}, s32[]{:T(128)}, f32[64,128,448]{2,1,0:T(8,128)}, s32[]{:T(128)}, /*index=5*/s32[]{:T(128)}, s32[]{:T(128)}, s32[]{:T(128)}) while((s32[]{:T(128)}, f32[128,448]{1,0:T(8,128)S(1)}, s32[]{:T(128)}, f32[64,128,448]{2,1,0:T(8,128)}, s32[]{:T(128)}, /*index=5*/s32[]{:T(128)}, s32[]{:T(128)}, ...), condition=%wide.region_6.7_spmd, body=%wide.region_5.6_spmd.sunk | while | flops 57350 | bytes 688263 | solution.py:20
  564.5 1.0 bitcast_add_fusion.6
  565.5 1.0 bitcast_add_fusion.6
  566.6 1.0 bitcast_add_fusion.6
  567.6 1.0 bitcast_add_fusion.6
  568.7 1.0 bitcast_add_fusion.6
  569.7 1.0 bitcast_add_fusion.6
  570.8 1.0 bitcast_add_fusion.6
  571.8 1.0 bitcast_add_fusion.6
  572.9 1.0 bitcast_add_fusion.6
  573.9 1.0 bitcast_add_fusion.6
  575.0 1.0 bitcast_add_fusion.6
  576.0 1.0 bitcast_add_fusion.6
  577.1 1.0 bitcast_add_fusion.6
  578.1 1.0 bitcast_add_fusion.6
  579.2 1.0 bitcast_add_fusion.6
  580.2 1.0 bitcast_add_fusion.6
  581.3 1.0 bitcast_add_fusion.6
  582.3 1.0 bitcast_add_fusion.6
  583.4 1.0 bitcast_add_fusion.6
  584.4 1.0 bitcast_add_fusion.6
  585.5 1.0 bitcast_add_fusion.6
  586.5 1.0 bitcast_add_fusion.6
  587.6 1.0 bitcast_add_fusion.6
  588.6 1.0 bitcast_add_fusion.6
  589.7 1.0 bitcast_add_fusion.6
  590.7 1.0 bitcast_add_fusion.6
  591.8 1.0 bitcast_add_fusion.6
  592.8 1.0 bitcast_add_fusion.6
  593.9 1.0 bitcast_add_fusion.6
  594.9 1.0 bitcast_add_fusion.6
  596.0 1.0 bitcast_add_fusion.6
  597.0 1.0 bitcast_add_fusion.6
  598.1 1.0 bitcast_add_fusion.6
  599.1 1.0 bitcast_add_fusion.6
  600.1 1.0 bitcast_add_fusion.6
  601.2 1.0 bitcast_add_fusion.6
  602.2 1.0 bitcast_add_fusion.6
  603.3 1.0 bitcast_add_fusion.6
  604.3 1.0 bitcast_add_fusion.6
  605.4 1.0 bitcast_add_fusion.6
  606.4 1.0 bitcast_add_fusion.6
  607.5 1.0 bitcast_add_fusion.6
  608.5 1.0 bitcast_add_fusion.6
  609.6 1.0 bitcast_add_fusion.6
  610.6 1.0 bitcast_add_fusion.6
  613.8 1.0 bitcast_add_fusion.6
  616.9 1.0 bitcast_add_fusion.6
  620.1 1.0 bitcast_add_fusion.6
  623.2 1.0 bitcast_add_fusion.6
  626.4 1.0 bitcast_add_fusion.6
  631.8 138.7 %psum.23 = f32[448]{0:T(512)} all-reduce(f32[448]{0:T(512)S(1)} %get-tuple-element.117), channel_id=1, replica_groups=mesh['lat'=64,'wid'=8] {'lat'}, use_global_device_ids=true, to_apply=%region_10.11 | all-reduce | flops 448 | bytes 3584 | tf_op jit(solution)/shard_map/psum | solution.py:71
  770.5 1.1 fusion
  771.6 2.0 fusion.1
  773.5 1.6 fusion.11
  (42 shorter events, 16.6 us)
Async XLA Ops:
  7.2 82.3 %copy-start = (bf16[512,448]{0,1:T(8,128)(2,1)S(1)}, bf16[512,448]{0,1:T(8,128)(2,1)}, u32[]{:S(2)}) copy-start(bf16[512,448]{0,1:T(8,128)(2,1)} %param.14) | copy-start | bytes 1376260
  7.2 81.1 %all-reduce.3.cloned.1.call-start = ((), (), s32[]{:S(2)}) async-start(), calls=%async_computation | async-start | bytes 524288 | tf_op jit(solution)/shard_map/psum | solution.py:33
  9.3 266.1 %all-gather.4.cloned.1.call-start = ((), (), s32[]{:S(2)}) async-start(), calls=%async_computation.1 | async-start | bytes 14909440 | tf_op jit(solution)/shard_map/all_gather | solution.py:13
  90.5 457.4 %all-gather.6.cloned.1.call-start = ((), (), s32[]{:S(2)}) async-start(), calls=%async_computation.3 | async-start | bytes 14909440 | tf_op jit(solution)/shard_map/all_gather | solution.py:13
  278.0 493.6 %all-reduce.5.cloned.1.call-start = ((), (), s32[]{:S(2)}) async-start(), calls=%async_computation.2 | async-start | bytes 524288 | tf_op jit(solution)/shard_map/psum | solution.py:61
  278.1 352.6 %copy-start.2 = (f32[128,448]{0,1:T(8,128)S(1)}, f32[128,448]{0,1:T(8,128)}, u32[]{:S(2)}) copy-start(f32[128,448]{0,1:T(8,128)} %get-tuple-element.118) | copy-start | bytes 688132
  278.1 493.5 %copy-start.1 = (s32[128,512]{1,0:T(8,128)S(1)}, s32[128,512]{1,0:T(8,128)}, u32[]{:S(2)}) copy-start(s32[128,512]{1,0:T(8,128)} %param.16) | copy-start | bytes 786436
  278.1 493.5 %copy-start.3 = (bf16[128,448]{0,1:T(8,128)(2,1)S(1)}, bf16[128,448]{0,1:T(8,128)(2,1)}, u32[]{:S(2)}) copy-start(bf16[128,448]{0,1:T(8,128)(2,1)} %param.11) | copy-start | bytes 344068
Sparse Core Ops, SparseCore 0:
  10.9 77.3 all-reduce.2
  92.2 183.1 all-gather.3
  279.3 268.4 all-gather.5
  632.0 61.8 all-reduce.4
where the time goes:
time: 784 us; the launch traced here: 782 us
  waiting for transfers between devices  530 us (68%)
  blocking collectives  139 us (18%)
  other arithmetic  74.2 us (9%)
  local copies, waits for them, and re-layouts  16.9 us (2%)
  between operations  13.9 us (2%)
    all_gather x2, waiting for transfers between devices, prefix(): gathered = lax.all_gather(part, axis)  453 us
    psum x1, blocking collectives, body(): decoder_bias_grad = lax.psum(jnp.sum(scaled_error, axis=0), 'lat')  139 us
    psum x1, waiting for transfers between devices, body(): preacts = lax.psum(encoder_part, 'wid') + encoder_bias  77 us
    add x63, other arithmetic, add_terms(): return earlier + later  64.4 us
    while x3, local copies, waits for them, and re-layouts, prefix(): return lax.fori_loop(0, ahead, one, state)  16.8 us
  transfers between devices with their start and end apart: 4, of which 3 were waited for; matrix products, arithmetic and copies ran while one was open for 1% of the time, Pallas kernels for 0%

commit v1 on v0

v1 whole, which is shorter than its diff:
```python
import jax
import jax.numpy as jnp
from jax import lax
from jax.sharding import PartitionSpec as P

GROUPS = 8
BF = jnp.bfloat16
F32 = jnp.float32
LANES = 128


def swap(x, axis):
    return lax.all_to_all(x, axis, 0, 0, tiled=False)


def spread(x, axis):
    count = lax.axis_size(axis)
    return swap(jnp.broadcast_to(x[None], (count,) + x.shape), axis)


def split_high_low(x):
    high = x.astype(BF)
    low = (x - high.astype(F32)).astype(BF)
    return high, low


def body(activations, encoder, encoder_bias, decoder, decoder_bias, kept_mask, boundaries):
    tokens, width = activations.shape
    latents = encoder.shape[1]
    n_lat, n_wid = lax.axis_size("lat"), lax.axis_size("wid")
    place = lax.axis_index("lat")
    part = lax.axis_index("wid")
    rows = tokens // n_wid
    own = tokens // n_lat
    span = n_lat // GROUPS
    group = place // span
    spare = -width % LANES
    share = width // n_lat

    has_cut = (place % span == 0) & (group > 0)
    cut_point = jnp.where(has_cut, boundaries[jnp.maximum(group - 1, 0)], 0)
    latent_ids = place * latents + jnp.arange(latents, dtype=jnp.int32)
    below_cut = (latent_ids < cut_point)[None, :]
    kept_rows = lax.dynamic_slice_in_dim(kept_mask, part * rows, rows, 0).astype(F32)

    enc_part = jnp.dot(activations, encoder, preferred_element_type=F32).astype(BF)
    pieces = swap(enc_part.reshape(n_wid, rows, latents), "wid")
    preacts = jnp.sum(pieces.astype(F32), axis=0) + encoder_bias
    my_codes = (kept_rows * preacts).astype(BF)
    codes = spread(my_codes, "wid").reshape(tokens, latents)

    zero = jnp.zeros((), BF)
    both_codes = jnp.stack([jnp.where(below_cut, codes, zero), jnp.where(below_cut, zero, codes)])
    decoded = jnp.einsum("sbj,jd->sbd", both_codes, decoder, preferred_element_type=F32)
    weight = (GROUPS - group).astype(F32) / GROUPS
    token_sums = jnp.sum(decoded, axis=1)
    bias_part = token_sums[0] * (weight + 1 / GROUPS) + token_sums[1] * weight
    tags = jnp.stack(split_high_low(bias_part.reshape(n_lat, share)), axis=1)
    sent = jnp.transpose(decoded.astype(BF).reshape(2, n_lat, own, width), (1, 0, 2, 3)).reshape(n_lat, 2 * own, width)
    tags = jnp.pad(tags, ((0, 0), (0, 2 * own - 2), (0, spare - share)))
    got = swap(jnp.concatenate([sent, tags], axis=2), "lat")
    bias_share = jnp.sum(got[:, :2, width : width + share].astype(F32), axis=(0, 1))

    pieces = got[:, :, :width].astype(F32).reshape(GROUPS, span, 2, own, width)
    high_sum = jnp.sum(pieces[:, :, 1], axis=1)
    low_sum = pieces[:, 0, 0]
    segment = high_sum + jnp.concatenate([low_sum[1:], jnp.zeros_like(low_sum[:1])], axis=0)
    target = lax.dynamic_slice_in_dim(activations, place * own, own, 0).astype(F32)
    run = decoder_bias - target
    errors = []
    for k in range(GROUPS):
        run = run + segment[k]
        errors.append(run)
    tail = jnp.zeros_like(run)
    suffixes = []
    for error in reversed(errors):
        tail = tail + error
        suffixes.append(tail / GROUPS)
    suffix = jnp.stack(suffixes[::-1]).astype(BF)
    before = jnp.concatenate([suffix[:1], suffix[:-1]], axis=0)
    pair = jnp.concatenate([before, suffix], axis=1)
    tags = jnp.stack(split_high_low(bias_share), axis=0)
    tags = jnp.pad(tags, ((0, 2 * own - 2), (0, spare - share)))
    pair = jnp.concatenate([pair, jnp.broadcast_to(tags[None], (GROUPS,) + tags.shape)], axis=2)
    back = jnp.broadcast_to(pair[:, None], (GROUPS, span) + pair.shape[1:]).reshape(n_lat, 2 * own, width + spare)
    mine = swap(back, "lat")
    bias_sum = jnp.sum(mine[:, :2, width : width + share].astype(F32), axis=1).reshape(width)
    decoder_bias_grad = bias_sum + tokens * decoder_bias - jnp.sum(activations.astype(F32), axis=0)

    suffix_pair = jnp.transpose(mine[:, :, :width].reshape(n_lat, 2, own, width), (1, 0, 2, 3)).reshape(2, tokens, width)
    back_grads = jnp.einsum("sbd,jd->sbj", suffix_pair, decoder, preferred_element_type=F32)
    partial_grads = jnp.where(below_cut, back_grads[0], back_grads[1]).astype(BF)
    pieces = swap(partial_grads.reshape(n_wid, rows, latents), "wid")
    my_grads = (kept_rows * jnp.sum(pieces.astype(F32), axis=0)).astype(BF)
    pre_low = spread(my_grads, "wid").reshape(tokens, latents)
    encoder_bias_grad = jnp.sum(pre_low.astype(F32), axis=0)
    encoder_grad = lax.dot_general(
        activations, pre_low, (((0,), (0,)), ((), ())), preferred_element_type=F32
    ).astype(BF)
    decoder_grad = jnp.einsum(
        "sbj,sbd->jd", both_codes, suffix_pair, preferred_element_type=F32
    ).astype(BF)
    return (encoder_grad, encoder_bias_grad, decoder_grad, decoder_bias_grad)


def solution(mesh):
    placed = (
        P(None, "wid"),
        P("wid", "lat"),
        P("lat"),
        P("lat", "wid"),
        P("wid"),
        P(None, "lat"),
        P(),
    )
    return jax.shard_map(
        body,
        mesh=mesh,
        in_specs=placed,
        out_specs=(P("wid", "lat"), P("lat"), P("lat", "wid"), P("wid")),
        check_vma=False,
    )
```

time: 784 us -> 121 us (0.15)
  the two profiles are of different devices: /device:TPU:6 before, /device:TPU:1 now
where the time goes in v1:
time: 121 us; the launch traced here: 120 us
  waiting for transfers between devices  55 us (45%)
  starting transfers between devices  47.7 us (39%)
  local copies, waits for them, and re-layouts  6.6 us (5%)
  matrix products  4.88 us (4%)
  other arithmetic  4.44 us (4%)
  between operations  1.57 us (1%)
    all_to_all x6, waiting for transfers between devices, swap(): return lax.all_to_all(x, axis, 0, 0, tiled=False)  55 us
    all_to_all x6, starting transfers between devices, swap(): return lax.all_to_all(x, axis, 0, 0, tiled=False)  47.7 us
  transfers between devices with their start and end apart: 6, of which 6 were waited for; matrix products, arithmetic and copies ran while one was open for 2% of the time, Pallas kernels for 0%

profile of v1, /device:TPU:1, one launch (start us, length us, event | category | flops | bytes accessed | tf_op | source)
XLA Modules:
  0.0 120.2 jit_solution(12134349478773107170)
XLA Ops:
  0.6 0.0 copy-start
  0.6 2.0 %convolution_convert_fusion.1 = bf16[128,512]{1,0:T(8,128)(2,1)} fusion(bf16[128,448]{0,1:T(8,128)(2,1)} %param.7, bf16[448,512]{1,0:T(8,128)(2,1)} %param.8), kind=kOutput, calls=%fused_computation.4 | convolution fusion | flops 58785792 | bytes 704512 | tf_op jit(solution)/shard_map/dot_general | solution.py:46
  2.7 10.2 %all-to-all-start = ((bf16[8,16,512]{2,1,0:T(8,128)(2,1)}), bf16[8,16,512]{2,1,0:T(8,128)(2,1)S(1)}, u32[]{:S(2)}, u32[]{:S(2)}) async-start(bf16[8,16,512]{2,1,0:T(8,128)(2,1)} %bitcast.1), calls=%async_computation | async-start | bytes 262144 | tf_op jit(solution)/shard_map/all_to_all | solution.py:13
  12.8 0.0 copy-start.3
  12.8 5.3 %all-to-all-done = bf16[8,16,512]{2,1,0:T(8,128)(2,1)S(1)} async-done(((bf16[8,16,512]{2,1,0:T(8,128)(2,1)}), bf16[8,16,512]{2,1,0:T(8,128)(2,1)S(1)}, u32[]{:S(2)}, u32[]{:S(2)}) %all-to-all-start) | async-done | bytes 131104 | tf_op jit(solution)/shard_map/all_to_all | solution.py:13
  18.2 0.0 copy-done.3
  18.2 0.8 multiply_convert_fusion.1
  18.9 0.7 broadcast_in_dim.38
  19.6 4.1 %all-to-all-start.1 = ((bf16[8,16,512]{2,1,0:T(8,128)(2,1)}), bf16[8,16,512]{2,1,0:T(8,128)(2,1)S(1)}, u32[]{:S(2)}, u32[]{:S(2)}) async-start(bf16[8,16,512]{2,1,0:T(8,128)(2,1)} %broadcast_in_dim.38), calls=%async_computation.1 | async-start | bytes 262144 | tf_op jit(solution)/shard_map/all_to_all | solution.py:13
  23.7 0.0 copy-start.4
  23.7 0.7 copy-done.4
  24.4 0.6 dynamic_slice.10
  25.7 3.4 %all-to-all-done.1 = bf16[8,16,512]{2,1,0:T(8,128)(2,1)S(1)} async-done(((bf16[8,16,512]{2,1,0:T(8,128)(2,1)}), bf16[8,16,512]{2,1,0:T(8,128)(2,1)S(1)}, u32[]{:S(2)}, u32[]{:S(2)}) %all-to-all-start.1) | async-done | bytes 131104 | tf_op jit(solution)/shard_map/all_to_all | solution.py:13
  29.1 0.0 copy-done
  29.1 0.4 fusion.42
  29.6 0.1 add.118
  29.7 0.1 copy.77
  29.8 0.1 copy.106
  29.9 0.2 copy.75
  30.2 0.1 fusion.7
  30.3 0.9 copy.80
  31.2 0.0 copy-start.1
  31.2 14.2 %all-to-all-start.2 = ((bf16[64,4,512]{2,1,0:T(4,128)(2,1)}), bf16[64,4,512]{2,1,0:T(4,128)(2,1)S(1)}, u32[]{:S(2)}, u32[]{:S(2)}) async-start(bf16[64,4,512]{2,1,0:T(4,128)(2,1)} %copy.80), calls=%async_computation.2 | async-start | bytes 524288 | tf_op jit(solution)/shard_map/all_to_all | solution.py:13
  45.4 0.0 copy-done.1
  45.4 0.1 constant_dynamic-slice_fusion
  45.5 0.1 copy.96
  45.6 18.5 %all-to-all-done.2 = bf16[64,4,512]{2,1,0:T(4,128)(2,1)S(1)} async-done(((bf16[64,4,512]{2,1,0:T(4,128)(2,1)}), bf16[64,4,512]{2,1,0:T(4,128)(2,1)S(1)}, u32[]{:S(2)}, u32[]{:S(2)}) %all-to-all-start.2) | async-done | bytes 262176 | tf_op jit(solution)/shard_map/all_to_all | solution.py:13
  64.1 0.1 convert_reduce_fusion.5
  64.4 0.1 convert.41
  64.5 0.1 slice_reduce_fusion
  64.6 0.0 copy-start.2
  64.6 0.7 copy-done.2
  65.5 0.1 pad_maximum_fusion.3
  65.6 0.8 broadcast_in_dim.41
  66.4 8.1 %all-to-all-start.3 = ((bf16[64,4,512]{2,1,0:T(4,128)(2,1)}), bf16[64,4,512]{2,1,0:T(4,128)(2,1)S(1)}, u32[]{:S(2)}, u32[]{:S(2)}) async-start(bf16[64,4,512]{2,1,0:T(4,128)(2,1)} %bitcast.26), calls=%async_computation.3 | async-start | bytes 524288 | tf_op jit(solution)/shard_map/all_to_all | solution.py:13
  74.5 0.1 convert_reduce_fusion.3
  74.6 18.1 %all-to-all-done.3 = bf16[64,4,512]{2,1,0:T(4,128)(2,1)S(1)} async-done(((bf16[64,4,512]{2,1,0:T(4,128)(2,1)}), bf16[64,4,512]{2,1,0:T(4,128)(2,1)S(1)}, u32[]{:S(2)}, u32[]{:S(2)}) %all-to-all-start.3) | async-done | bytes 262176 | tf_op jit(solution)/shard_map/all_to_all | solution.py:13
  92.8 0.3 copy.92
  93.0 0.2 copy.93
  93.3 1.0 fusion
  94.3 0.3 fusion.3
  94.7 0.7 select_convert_fusion
  95.3 7.0 %all-to-all-start.4 = ((bf16[8,16,512]{2,1,0:T(8,128)(2,1)}), bf16[8,16,512]{2,1,0:T(8,128)(2,1)S(1)}, u32[]{:S(2)}, u32[]{:S(2)}) async-start(bf16[8,16,512]{2,1,0:T(8,128)(2,1)} %select_convert_fusion), calls=%async_computation.4 | async-start | bytes 262144 | tf_op jit(solution)/shard_map/all_to_all | solution.py:13
  102.3 0.2 convert_reduce_fusion.4
  102.5 0.1 reshape.204
  102.6 5.0 %all-to-all-done.4 = bf16[8,16,512]{2,1,0:T(8,128)(2,1)S(1)} async-done(((bf16[8,16,512]{2,1,0:T(8,128)(2,1)}), bf16[8,16,512]{2,1,0:T(8,128)(2,1)S(1)}, u32[]{:S(2)}, u32[]{:S(2)}) %all-to-all-start.4) | async-done | bytes 131104 | tf_op jit(solution)/shard_map/all_to_all | solution.py:13
  107.6 0.8 multiply_convert_fusion
  108.4 0.7 broadcast_in_dim.62
  109.1 4.1 %all-to-all-start.5 = ((bf16[8,16,512]{2,1,0:T(8,128)(2,1)}), bf16[8,16,512]{2,1,0:T(8,128)(2,1)S(1)}, u32[]{:S(2)}, u32[]{:S(2)}) async-start(bf16[8,16,512]{2,1,0:T(8,128)(2,1)} %broadcast_in_dim.62), calls=%async_computation.5 | async-start | bytes 262144 | tf_op jit(solution)/shard_map/all_to_all | solution.py:13
  113.2 0.6 add_subtract_fusion
  113.8 4.7 %all-to-all-done.5 = bf16[8,16,512]{2,1,0:T(8,128)(2,1)S(1)} async-done(((bf16[8,16,512]{2,1,0:T(8,128)(2,1)}), bf16[8,16,512]{2,1,0:T(8,128)(2,1)S(1)}, u32[]{:S(2)}, u32[]{:S(2)}) %all-to-all-start.5) | async-done | bytes 131104 | tf_op jit(solution)/shard_map/all_to_all | solution.py:13
  118.5 1.0 fusion.1
  119.5 0.6 convert_reduce_fusion
  (33 shorter events, 0.6 us)
Async XLA Ops:
  0.6 28.4 %copy-start = (bf16[512,448]{0,1:T(8,128)(2,1)S(1)}, bf16[512,448]{0,1:T(8,128)(2,1)}, u32[]{:S(2)}) copy-start(bf16[512,448]{0,1:T(8,128)(2,1)} %param.10) | copy-start | bytes 1376260
  2.7 15.4 %all-to-all-start = ((bf16[8,16,512]{2,1,0:T(8,128)(2,1)}), bf16[8,16,512]{2,1,0:T(8,128)(2,1)S(1)}, u32[]{:S(2)}, u32[]{:S(2)}) async-start(bf16[8,16,512]{2,1,0:T(8,128)(2,1)} %bitcast.1), calls=%async_computation | async-start | bytes 262144 | tf_op jit(solution)/shard_map/all_to_all | solution.py:13
  12.8 5.3 %copy-start.3 = (f32[512]{0:T(512)S(1)}, f32[512]{0:T(512)}, u32[]{:S(2)}) copy-start(f32[512]{0:T(512)} %param.9) | copy-start | bytes 6148
  19.6 9.4 %all-to-all-start.1 = ((bf16[8,16,512]{2,1,0:T(8,128)(2,1)}), bf16[8,16,512]{2,1,0:T(8,128)(2,1)S(1)}, u32[]{:S(2)}, u32[]{:S(2)}) async-start(bf16[8,16,512]{2,1,0:T(8,128)(2,1)} %broadcast_in_dim.38), calls=%async_computation.1 | async-start | bytes 262144 | tf_op jit(solution)/shard_map/all_to_all | solution.py:13
  23.7 0.7 copy-start.4
  31.2 14.2 %copy-start.1 = (bf16[128,448]{0,1:T(8,128)(2,1)S(1)}, bf16[128,448]{0,1:T(8,128)(2,1)}, u32[]{:S(2)}) copy-start(bf16[128,448]{0,1:T(8,128)(2,1)} %param.7) | copy-start | bytes 344068
  31.2 32.9 %all-to-all-start.2 = ((bf16[64,4,512]{2,1,0:T(4,128)(2,1)}), bf16[64,4,512]{2,1,0:T(4,128)(2,1)S(1)}, u32[]{:S(2)}, u32[]{:S(2)}) async-start(bf16[64,4,512]{2,1,0:T(4,128)(2,1)} %copy.80), calls=%async_computation.2 | async-start | bytes 524288 | tf_op jit(solution)/shard_map/all_to_all | solution.py:13
  64.6 0.7 copy-start.2
  66.4 26.3 %all-to-all-start.3 = ((bf16[64,4,512]{2,1,0:T(4,128)(2,1)}), bf16[64,4,512]{2,1,0:T(4,128)(2,1)S(1)}, u32[]{:S(2)}, u32[]{:S(2)}) async-start(bf16[64,4,512]{2,1,0:T(4,128)(2,1)} %bitcast.26), calls=%async_computation.3 | async-start | bytes 524288 | tf_op jit(solution)/shard_map/all_to_all | solution.py:13
  95.3 12.3 %all-to-all-start.4 = ((bf16[8,16,512]{2,1,0:T(8,128)(2,1)}), bf16[8,16,512]{2,1,0:T(8,128)(2,1)S(1)}, u32[]{:S(2)}, u32[]{:S(2)}) async-start(bf16[8,16,512]{2,1,0:T(8,128)(2,1)} %select_convert_fusion), calls=%async_computation.4 | async-start | bytes 262144 | tf_op jit(solution)/shard_map/all_to_all | solution.py:13
  109.1 9.4 %all-to-all-start.5 = ((bf16[8,16,512]{2,1,0:T(8,128)(2,1)}), bf16[8,16,512]{2,1,0:T(8,128)(2,1)S(1)}, u32[]{:S(2)}, u32[]{:S(2)}) async-start(bf16[8,16,512]{2,1,0:T(8,128)(2,1)} %broadcast_in_dim.62), calls=%async_computation.5 | async-start | bytes 262144 | tf_op jit(solution)/shard_map/all_to_all | solution.py:13

commit v2 on v1

v2 whole, which is shorter than its diff:
```python
import jax
import jax.numpy as jnp
from jax import lax
from jax.sharding import PartitionSpec as P

GROUPS = 8
BF = jnp.bfloat16
F32 = jnp.float32

N_Y, N_FAR, NEAR = 4, 4, 4
N_Z = N_FAR * NEAR
SLICES = N_Y * NEAR
NEAR_GROUPS = [[N_Z * y + NEAR * q + r for y in range(N_Y) for r in range(NEAR)] for q in range(N_FAR)]
FAR_GROUPS = [[N_Z * y + NEAR * q + r for q in range(N_FAR)] for y in range(N_Y) for r in range(NEAR)]
PIECE = 32


def swap(x, axis, groups=None):
    return lax.all_to_all(x, axis, 0, 0, axis_index_groups=groups, tiled=False)


def copies(x, count):
    return jnp.broadcast_to(x[None], (count,) + x.shape)


def dot(a, b, over):
    return lax.dot_general(a, b, (((over[0],), (over[1],)), ((), ())), preferred_element_type=F32)


def pad_rows(x, rows):
    return jnp.pad(x.reshape(SLICES, rows, x.shape[1]), ((0, 0), (0, PIECE - rows), (0, 0)))


def sum_codes(pieces, kept, bias):
    return (kept * (jnp.sum(pieces.astype(F32), axis=0) + bias)).astype(BF)


def sum_grads(pieces, kept):
    return (kept * jnp.sum(pieces.astype(F32), axis=0)).astype(BF)


def split_codes(codes, below):
    zero = jnp.zeros_like(codes)
    return jnp.where(below, codes, zero), jnp.where(below, zero, codes)


def decode(codes, below, dec_pad):
    low, high = split_codes(codes, below)
    shape = (SLICES, PIECE, codes.shape[0])
    decoded = [dot(dec_pad, part, (1, 1)).reshape(shape) for part in (low, high)]
    return jnp.concatenate(decoded, axis=1).astype(BF)


def near_sums(got):
    tokens = got.shape[-1]
    got = got.astype(F32).reshape(N_Y, NEAR, 2 * PIECE, tokens)
    high = jnp.sum(got[:, :, PIECE:], axis=1)
    return jnp.concatenate([got[:, 0, :PIECE], high], axis=1).astype(BF)


def suffixes_of(got, base, late, rows):
    got = got.astype(F32)
    low, high = got[:, :, :PIECE], got[:, :, PIECE:]
    run = base
    errors = []
    for y in range(N_Y):
        run = run + ((high[0, y] + high[1, y]) + low[2, y])
        errors.append(run)
        part = high[2, y] + high[3, y]
        run = run + (part + low[0, y + 1] if y + 1 < N_Y else part)
        errors.append(run)
    tail = jnp.zeros_like(base)
    suffix = []
    for error in reversed(errors):
        tail = tail + error
        suffix.append(tail / GROUPS)
    suffix = suffix[::-1]
    row = lax.broadcasted_iota(jnp.int32, base.shape, 0)
    lane = lax.broadcasted_iota(jnp.int32, base.shape, 1)
    token_sum = jnp.sum(suffix[0], axis=1, keepdims=True)
    token_row = jnp.sum(jnp.where(row == lane, token_sum, 0.0), axis=0, keepdims=True)
    token_high = token_row.astype(BF).astype(F32)
    out = []
    for y in range(N_Y):
        own = jnp.where(late, suffix[2 * y + 1], suffix[2 * y])
        previous = jnp.where(late, suffix[2 * y], suffix[max(2 * y - 1, 0)])
        previous = jnp.where(row == rows, token_high, jnp.where(row == rows + 1, token_row - token_high, previous))
        out += [jnp.concatenate([previous, own], axis=0).astype(BF)] * NEAR
    return jnp.stack(out)


def back(got, below, dec_pad):
    shape = (SLICES * PIECE, got.shape[-1])
    low, high = got[:, :PIECE].reshape(shape), got[:, PIECE:].reshape(shape)
    return jnp.where(below, dot(low, dec_pad, (0, 0)), dot(high, dec_pad, (0, 0))).astype(BF)


def body(activations, encoder, encoder_bias, decoder, decoder_bias, kept_mask, boundaries):
    tokens, width = activations.shape
    latents = encoder.shape[1]
    n_wid = lax.axis_size("wid")
    place = lax.axis_index("lat")
    part = lax.axis_index("wid")
    rows = tokens // n_wid
    piece = width // SLICES
    span = lax.axis_size("lat") // GROUPS
    group = place // span
    y, z = place // N_Z, place % N_Z
    my_slice = NEAR * y + z % NEAR
    late = z // NEAR >= N_FAR // 2

    has_cut = (place % span == 0) & (group > 0)
    cut_point = jnp.where(has_cut, boundaries[jnp.maximum(group - 1, 0)], 0)
    latent_ids = place * latents + jnp.arange(latents, dtype=jnp.int32)
    below = (latent_ids < cut_point)[None, :]
    kept_rows = lax.dynamic_slice_in_dim(kept_mask, part * rows, rows, 0).astype(F32)

    enc_part = dot(activations, encoder, (1, 0)).astype(BF)
    pieces = swap(enc_part.reshape(n_wid, rows, latents), "wid")
    dec_pad = pad_rows(decoder.T, piece).reshape(SLICES * PIECE, latents)
    target = lax.dynamic_index_in_dim(pad_rows(activations.T, piece), my_slice, 0, False).astype(F32)
    base = lax.dynamic_index_in_dim(pad_rows(decoder_bias[:, None], piece), my_slice, 0, False) - target
    my_codes = sum_codes(pieces, kept_rows, encoder_bias[None])
    codes = swap(copies(my_codes, n_wid), "wid").reshape(tokens, latents)

    got = swap(decode(codes, below, dec_pad), "lat", NEAR_GROUPS)
    got = swap(copies(near_sums(got), N_FAR), "lat", FAR_GROUPS)
    got = swap(suffixes_of(got, base, late, piece), "lat", NEAR_GROUPS)

    partial_grads = back(got, below, dec_pad)
    pieces = swap(partial_grads.reshape(n_wid, rows, latents), "wid")
    suffix_low = got[:, :piece].reshape(width, tokens)
    suffix_high = got[:, PIECE : PIECE + piece].reshape(width, tokens)
    low, high = split_codes(codes, below)
    decoder_grad = (dot(suffix_low, low, (1, 0)) + dot(suffix_high, high, (1, 0))).astype(BF).T
    tags = got[:, piece : piece + 2, :piece].astype(F32)
    decoder_bias_grad = (tags[:, 0] + tags[:, 1]).reshape(width)
    my_grads = sum_grads(pieces, kept_rows)
    pre_low = swap(copies(my_grads, n_wid), "wid").reshape(tokens, latents)
    encoder_bias_grad = jnp.sum(pre_low.astype(F32), axis=0)
    encoder_grad = dot(activations, pre_low, (0, 0)).astype(BF)
    return (encoder_grad, encoder_bias_grad, decoder_grad, decoder_bias_grad)


def solution(mesh):
    placed = (
        P(None, "wid"),
        P("wid", "lat"),
        P("lat"),
        P("lat", "wid"),
        P("wid"),
        P(None, "lat"),
        P(),
    )
    return jax.shard_map(
        body,
        mesh=mesh,
        in_specs=placed,
        out_specs=(P("wid", "lat"), P("lat"), P("lat", "wid"), P("wid")),
        check_vma=False,
    )
```

time: 121 us -> 115 us (0.950)
  blocking collectives: 0 us -> 27 us
  waiting for transfers between devices: 55 us -> 31.6 us
  starting transfers between devices: 47.7 us -> 39 us
  other arithmetic: 4.44 us -> 3.16 us
    all_to_all x0 -> x2, blocking collectives: none -> 27 us  [swap(): return lax.all_to_all(x, axis, 0, 0, axis_index_groups=groups, tiled=False)]
    all_to_all x6 -> x5, waiting for transfers between devices: 55 us -> 31.6 us  [swap(): return lax.all_to_all(x, axis, 0, 0, axis_index_groups=groups, tiled=False)]
    all_to_all x6 -> x5, starting transfers between devices: 47.7 us -> 39 us  [swap(): return lax.all_to_all(x, axis, 0, 0, axis_index_groups=groups, tiled=False)]
    dot_general x5 -> x8, matrix products: 4.88 us -> 5.9 us  [dot(): lax.dot_general(a, b, (((over[0],), (over[1],)), ((), ())), preferred_ele...]
  transfers between devices with their start and end apart: 6 -> 5, of which waited for: 6 -> 5; matrix products, arithmetic and copies ran while one was open for 2% -> 2% of each run, Pallas kernels for 0% -> 0%
where the time goes in v2:
time: 115 us; the launch traced here: 114 us
  starting transfers between devices  39 us (34%)
  waiting for transfers between devices  31.6 us (27%)
  blocking collectives  27 us (23%)
  local copies, waits for them, and re-layouts  5.98 us (5%)
  matrix products  5.9 us (5%)
  other arithmetic  3.16 us (3%)
  between operations  1.55 us (1%)
    all_to_all x5, starting transfers between devices, swap(): return lax.all_to_all(x, axis, 0, 0, axis_index_groups=groups, tiled=False)  39 us
    all_to_all x5, waiting for transfers between devices, swap(): return lax.all_to_all(x, axis, 0, 0, axis_index_groups=groups, tiled=False)  31.6 us
    all_to_all x2, blocking collectives, swap(): return lax.all_to_all(x, axis, 0, 0, axis_index_groups=groups, tiled=False)  27 us
    dot_general x8, matrix products, dot(): lax.dot_general(a, b, (((over[0],), (over[1],)), ((), ())), preferred_ele...  5.9 us
    unnamed x12, local copies, waits for them, and re-layouts  2.35 us
  transfers between devices with their start and end apart: 5, of which 5 were waited for; matrix products, arithmetic and copies ran while one was open for 2% of the time, Pallas kernels for 0%

profile of v2, /device:TPU:1, one launch (start us, length us, event | category | flops | bytes accessed | tf_op | source)
XLA Modules:
  0.0 114.2 jit_solution(14546102039374409216)
XLA Ops:
  0.6 0.0 copy-start
  0.6 1.0 copy-done
  1.7 0.0 copy-start.4
  1.7 1.8 %convolution_convert_fusion.3 = bf16[128,512]{1,0:T(8,128)(2,1)} fusion(bf16[128,448]{0,1:T(8,128)(2,1)} %param.7, bf16[448,512]{1,0:T(8,128)(2,1)S(1)} %copy-done), kind=kOutput, calls=%fused_computation.10 | convolution fusion | flops 58785792 | bytes 704512 | tf_op jit(solution)/shard_map/dot_general | solution.py:27
  3.5 0.0 copy-start.2
  3.5 10.3 %all-to-all-start = ((bf16[8,16,512]{2,1,0:T(8,128)(2,1)}), bf16[8,16,512]{2,1,0:T(8,128)(2,1)S(1)}, u32[]{:S(2)}, u32[]{:S(2)}) async-start(bf16[8,16,512]{2,1,0:T(8,128)(2,1)} %bitcast.5), calls=%async_computation | async-start | bytes 262144 | tf_op jit(solution)/shard_map/all_to_all | solution.py:19
  13.8 5.3 %all-to-all-done = bf16[8,16,512]{2,1,0:T(8,128)(2,1)S(1)} async-done(((bf16[8,16,512]{2,1,0:T(8,128)(2,1)}), bf16[8,16,512]{2,1,0:T(8,128)(2,1)S(1)}, u32[]{:S(2)}, u32[]{:S(2)}) %all-to-all-start) | async-done | bytes 131104 | tf_op jit(solution)/shard_map/all_to_all | solution.py:19
  19.1 0.0 copy-done.4
  19.1 0.8 multiply_convert_fusion.1
  19.9 0.7 broadcast_in_dim.92
  20.5 4.1 %all-to-all-start.1 = ((bf16[8,16,512]{2,1,0:T(8,128)(2,1)}), bf16[8,16,512]{2,1,0:T(8,128)(2,1)S(1)}, u32[]{:S(2)}, u32[]{:S(2)}) async-start(bf16[8,16,512]{2,1,0:T(8,128)(2,1)} %broadcast_in_dim.92), calls=%async_computation.1 | async-start | bytes 262144 | tf_op jit(solution)/shard_map/all_to_all | solution.py:19
  24.7 0.0 copy-done.2
  24.7 0.1 reshape.667
  24.8 0.0 copy-start.5
  24.8 0.6 copy-done.5
  25.4 0.6 dynamic_slice.15
  26.7 3.3 %all-to-all-done.1 = bf16[8,16,512]{2,1,0:T(8,128)(2,1)S(1)} async-done(((bf16[8,16,512]{2,1,0:T(8,128)(2,1)}), bf16[8,16,512]{2,1,0:T(8,128)(2,1)S(1)}, u32[]{:S(2)}, u32[]{:S(2)}) %all-to-all-start.1) | async-done | bytes 131104 | tf_op jit(solution)/shard_map/all_to_all | solution.py:19
  30.0 0.3 convolution_convert_fusion.1
  30.3 0.3 convolution_convert_fusion.2
  30.6 13.5 %all_to_all.35 = bf16[16,64,128]{2,1,0:T(8,128)(2,1)S(1)} all-to-all(bf16[16,64,128]{2,1,0:T(8,128)(2,1)S(1)} %pad_maximum_fusion), channel_id=1, replica_groups={{0,8,16,24,128,136,144,152,256,264,272,280,384,392,400,408},{32,40,48,5..., dimensions={0} | all-to-all | bytes 524288 | tf_op jit(solution)/shard_map/all_to_all | solution.py:19
  44.1 0.8 broadcast_in_dim.93
  44.9 0.0 copy-start.1
  44.9 12.2 %all-to-all-start.3 = ((bf16[4,4,64,128]{3,2,1,0:T(8,128)(2,1)}), bf16[4,4,64,128]{3,2,1,0:T(8,128)(2,1)S(1)}, u32[]{:S(2)}, u32[]{:S(2)}) async-start(bf16[4,4,64,128]{3,2,1,0:T(8,128)(2,1)} %broadcast_in_dim.93), calls=%async_computation.3 | async-start | bytes 524288 | tf_op jit(solution)/shard_map/all_to_all | solution.py:19
  57.1 0.0 copy-start.3
  57.1 0.7 copy-done.3
  57.8 0.1 reshape_broadcast_in_dim.3
  57.9 0.0 copy-done.1
  58.0 14.5 %all-to-all-done.3 = bf16[4,4,64,128]{3,2,1,0:T(8,128)(2,1)S(1)} async-done(((bf16[4,4,64,128]{3,2,1,0:T(8,128)(2,1)}), bf16[4,4,64,128]{3,2,1,0:T(8,128)(2,1)S(1)}, u32[]{:S(2)}, u32[]{:S(2)}) %all-to-all-start.3) | async-done | bytes 262176 | tf_op jit(solution)/shard_map/all_to_all | solution.py:19
  72.5 0.2 fusion.20
  72.7 0.1 select_reduce_fusion
  72.8 0.1 select_convert_fusion.1
  72.9 0.1 select_convert_fusion.5
  73.0 0.1 select_convert_fusion
  73.1 0.1 select_convert_fusion.7
  73.4 13.6 %all_to_all.36 = bf16[16,64,128]{2,1,0:T(8,128)(2,1)S(1)} all-to-all(bf16[16,64,128]{2,1,0:T(8,128)(2,1)S(1)} %constant_dynamic-update-slice_fusion), channel_id=1, replica_groups={{0,8,16,24,128,136,144,152,256,264,272,280,384,392,400,408},{32,40,48,5..., dimensions={0} | all-to-all | bytes 524288 | tf_op jit(solution)/shard_map/all_to_all | solution.py:19
  87.0 0.2 convolution_bitcast_fusion
  87.2 0.9 fusion.3
  88.2 8.2 %all-to-all-start.5 = ((bf16[8,16,512]{2,1,0:T(8,128)(2,1)}), bf16[8,16,512]{2,1,0:T(8,128)(2,1)S(1)}, u32[]{:S(2)}, u32[]{:S(2)}) async-start(bf16[8,16,512]{2,1,0:T(8,128)(2,1)} %bitcast.30), calls=%async_computation.5 | async-start | bytes 262144 | tf_op jit(solution)/shard_map/all_to_all | solution.py:19
  96.4 0.3 fusion.34
  96.7 1.0 fusion
  97.7 4.0 %all-to-all-done.5 = bf16[8,16,512]{2,1,0:T(8,128)(2,1)S(1)} async-done(((bf16[8,16,512]{2,1,0:T(8,128)(2,1)}), bf16[8,16,512]{2,1,0:T(8,128)(2,1)S(1)}, u32[]{:S(2)}, u32[]{:S(2)}) %all-to-all-start.5) | async-done | bytes 131104 | tf_op jit(solution)/shard_map/all_to_all | solution.py:19
  101.7 0.8 multiply_convert_fusion
  102.5 0.7 broadcast_in_dim.98
  103.1 4.1 %all-to-all-start.6 = ((bf16[8,16,512]{2,1,0:T(8,128)(2,1)}), bf16[8,16,512]{2,1,0:T(8,128)(2,1)S(1)}, u32[]{:S(2)}, u32[]{:S(2)}) async-start(bf16[8,16,512]{2,1,0:T(8,128)(2,1)} %broadcast_in_dim.98), calls=%async_computation.6 | async-start | bytes 262144 | tf_op jit(solution)/shard_map/all_to_all | solution.py:19
  107.3 0.7 add.596
  108.0 4.6 %all-to-all-done.6 = bf16[8,16,512]{2,1,0:T(8,128)(2,1)S(1)} async-done(((bf16[8,16,512]{2,1,0:T(8,128)(2,1)}), bf16[8,16,512]{2,1,0:T(8,128)(2,1)S(1)}, u32[]{:S(2)}, u32[]{:S(2)}) %all-to-all-start.6) | async-done | bytes 131104 | tf_op jit(solution)/shard_map/all_to_all | solution.py:19
  112.6 1.0 fusion.1
  113.6 0.6 convert_reduce_fusion
  (35 shorter events, 0.5 us)
Async XLA Ops:
  0.6 1.0 copy-start
  1.7 17.4 %copy-start.4 = (f32[512]{0:T(512)S(1)}, f32[512]{0:T(512)}, u32[]{:S(2)}) copy-start(f32[512]{0:T(512)} %param.9) | copy-start | bytes 6148
  3.5 21.2 %copy-start.2 = (bf16[512,448]{0,1:T(8,128)(2,1)S(1)}, bf16[512,448]{0,1:T(8,128)(2,1)}, u32[]{:S(2)}) copy-start(bf16[512,448]{0,1:T(8,128)(2,1)} %param.10) | copy-start | bytes 1376260
  3.5 15.6 %all-to-all-start = ((bf16[8,16,512]{2,1,0:T(8,128)(2,1)}), bf16[8,16,512]{2,1,0:T(8,128)(2,1)S(1)}, u32[]{:S(2)}, u32[]{:S(2)}) async-start(bf16[8,16,512]{2,1,0:T(8,128)(2,1)} %bitcast.5), calls=%async_computation | async-start | bytes 262144 | tf_op jit(solution)/shard_map/all_to_all | solution.py:19
  20.5 9.4 %all-to-all-start.1 = ((bf16[8,16,512]{2,1,0:T(8,128)(2,1)}), bf16[8,16,512]{2,1,0:T(8,128)(2,1)S(1)}, u32[]{:S(2)}, u32[]{:S(2)}) async-start(bf16[8,16,512]{2,1,0:T(8,128)(2,1)} %broadcast_in_dim.92), calls=%async_computation.1 | async-start | bytes 262144 | tf_op jit(solution)/shard_map/all_to_all | solution.py:19
  24.8 0.7 copy-start.5
  44.9 13.0 %copy-start.1 = (bf16[128,448]{0,1:T(8,128)(2,1)S(1)}, bf16[128,448]{0,1:T(8,128)(2,1)}, u32[]{:S(2)}) copy-start(bf16[128,448]{0,1:T(8,128)(2,1)} %param.7) | copy-start | bytes 344068
  44.9 27.6 %all-to-all-start.3 = ((bf16[4,4,64,128]{3,2,1,0:T(8,128)(2,1)}), bf16[4,4,64,128]{3,2,1,0:T(8,128)(2,1)S(1)}, u32[]{:S(2)}, u32[]{:S(2)}) async-start(bf16[4,4,64,128]{3,2,1,0:T(8,128)(2,1)} %broadcast_in_dim.93), calls=%async_computation.3 | async-start | bytes 524288 | tf_op jit(solution)/shard_map/all_to_all | solution.py:19
  57.1 0.7 copy-start.3
  88.2 13.5 %all-to-all-start.5 = ((bf16[8,16,512]{2,1,0:T(8,128)(2,1)}), bf16[8,16,512]{2,1,0:T(8,128)(2,1)S(1)}, u32[]{:S(2)}, u32[]{:S(2)}) async-start(bf16[8,16,512]{2,1,0:T(8,128)(2,1)} %bitcast.30), calls=%async_computation.5 | async-start | bytes 262144 | tf_op jit(solution)/shard_map/all_to_all | solution.py:19
  103.1 9.4 %all-to-all-start.6 = ((bf16[8,16,512]{2,1,0:T(8,128)(2,1)}), bf16[8,16,512]{2,1,0:T(8,128)(2,1)S(1)}, u32[]{:S(2)}, u32[]{:S(2)}) async-start(bf16[8,16,512]{2,1,0:T(8,128)(2,1)} %broadcast_in_dim.98), calls=%async_computation.6 | async-start | bytes 262144 | tf_op jit(solution)/shard_map/all_to_all | solution.py:19

commit v3 on v2

v3 whole, which is shorter than its diff:
```python
import jax
import jax.numpy as jnp
from jax import lax
from jax.experimental import pallas as pl
from jax.experimental.pallas import tpu as pltpu
from jax.sharding import PartitionSpec as P

GROUPS = 8
BF = jnp.bfloat16
F32 = jnp.float32

N_Y, N_FAR, NEAR = 4, 4, 4
N_Z = N_FAR * NEAR
SLICES = N_Y * NEAR
NEAR_GROUPS = [[N_Z * y + NEAR * q + r for y in range(N_Y) for r in range(NEAR)] for q in range(N_FAR)]
FAR_GROUPS = [[N_Z * y + NEAR * q + r for q in range(N_FAR)] for y in range(N_Y) for r in range(NEAR)]
PIECE = 32
N_CORE, N_X = 2, 4
CORE_PAIRS = [(i, i ^ 1) for i in range(N_CORE * N_X)]
CHIP_GROUPS = [[N_CORE * x + c for x in range(N_X)] for c in range(N_CORE)]


def swap(x, axis, groups=None):
    return lax.all_to_all(x, axis, 0, 0, axis_index_groups=groups, tiled=False)


def copies(x, count):
    return jnp.broadcast_to(x[None], (count,) + x.shape)


def dot(a, b, over):
    return lax.dot_general(a, b, (((over[0],), (over[1],)), ((), ())), preferred_element_type=F32)


def pad_rows(x, rows):
    return jnp.pad(x.reshape(SLICES, rows, x.shape[1]), ((0, 0), (0, PIECE - rows), (0, 0)))


def call(stage, shapes, scalars, *arrays):
    n_in = len(arrays)

    def kernel(scalar_ref, *refs):
        values = [scalar_ref[i] for i in range(len(scalars))]
        outs = stage(*values, *[ref[...] for ref in refs[:n_in]])
        for ref, out in zip(refs[n_in:], outs, strict=True):
            if isinstance(out, list):
                for i, one in enumerate(out):
                    ref[i] = one
            else:
                ref[...] = out

    vmem = pl.BlockSpec(memory_space=pltpu.VMEM)
    return pl.pallas_call(
        kernel,
        out_shape=[jax.ShapeDtypeStruct(shape, dtype) for shape, dtype in shapes],
        in_specs=[pl.BlockSpec(memory_space=pltpu.SMEM)] + [vmem] * n_in,
        out_specs=[vmem] * len(shapes),
        compiler_params=pltpu.CompilerParams(vmem_limit_bytes=32 * 1024 * 1024),
        name=stage.__name__,
    )(jnp.stack([jnp.asarray(v, jnp.int32) for v in scalars]), *arrays)


def half_of(core, x, other=False):
    half = x.shape[0] // N_CORE
    first = core == (1 if other else 0)
    return jnp.where(first, x[:half], x[half:])


def joined(core, own, other):
    own, other = own.astype(F32), other.astype(F32)
    return jnp.concatenate([jnp.where(core == 0, own, other), jnp.where(core == 0, other, own)], axis=0)


def split_codes(codes, cut):
    below = lax.broadcasted_iota(jnp.int32, codes.shape, 1) < cut
    return jnp.where(below, codes, 0.0).astype(BF), jnp.where(below, 0.0, codes).astype(BF)


def encode(core, activations, encoder):
    part = dot(activations, encoder, (0, 0))
    return half_of(core, part), half_of(core, part, True)


def pair_sum(core, kept, got):
    return ([(kept + got).astype(BF)] * N_X,)


def kept_codes(core, pieces, mask, bias):
    total = jnp.sum(pieces.astype(F32), axis=0) + bias
    return ((half_of(core, mask).astype(F32) * total).astype(BF),)


def kept_grads(core, pieces, mask):
    return ((half_of(core, mask).astype(F32) * jnp.sum(pieces.astype(F32), axis=0)).astype(BF),)


def decode(core, cut, own, other, dec_pad):
    codes = joined(core, own, other)
    shape = (SLICES, PIECE, codes.shape[0])
    decoded = [dot(dec_pad, part, (1, 1)).reshape(shape) for part in split_codes(codes, cut)]
    return (jnp.concatenate(decoded, axis=1).astype(BF),)


def near_sums(core, got):
    tokens = got.shape[-1]
    got = got.astype(F32).reshape(N_Y, NEAR, 2 * PIECE, tokens)
    high = jnp.sum(got[:, :, PIECE:], axis=1)
    return ([jnp.concatenate([got[:, 0, :PIECE], high], axis=1).astype(BF)] * N_FAR,)


def suffixes(late, rows, got, base):
    got = got.astype(F32)
    low, high = got[:, :, :PIECE], got[:, :, PIECE:]
    run = base
    errors = []
    for y in range(N_Y):
        run = run + ((high[0, y] + high[1, y]) + low[2, y])
        errors.append(run)
        part = high[2, y] + high[3, y]
        run = run + (part + low[0, y + 1] if y + 1 < N_Y else part)
        errors.append(run)
    tail = jnp.zeros_like(base)
    suffix = []
    for error in reversed(errors):
        tail = tail + error
        suffix.append(tail / GROUPS)
    suffix = suffix[::-1]
    row = lax.broadcasted_iota(jnp.int32, base.shape, 0)
    lane = lax.broadcasted_iota(jnp.int32, base.shape, 1)
    token_sum = jnp.sum(suffix[0], axis=1, keepdims=True)
    token_row = jnp.sum(jnp.where(row == lane, token_sum, 0.0), axis=0, keepdims=True)
    token_high = token_row.astype(BF).astype(F32)
    out = []
    for y in range(N_Y):
        own = jnp.where(late == 1, suffix[2 * y + 1], suffix[2 * y])
        previous = jnp.where(late == 1, suffix[2 * y], suffix[max(2 * y - 1, 0)])
        previous = jnp.where(row == rows, token_high, jnp.where(row == rows + 1, token_row - token_high, previous))
        out += [jnp.concatenate([previous, own], axis=0).astype(BF)] * NEAR
    return (out,)


def back(core, cut, got, dec_pad):
    tokens = got.shape[-1]
    got = got.astype(F32)
    low = got[:, :PIECE].reshape(SLICES * PIECE, tokens).astype(BF)
    high = got[:, PIECE:].reshape(SLICES * PIECE, tokens).astype(BF)
    low, high = dot(low, dec_pad, (0, 0)), dot(high, dec_pad, (0, 0))
    below = lax.broadcasted_iota(jnp.int32, low.shape, 1) < cut
    part = jnp.where(below, low, high)
    return half_of(core, part), half_of(core, part, True)


def encoder_grads(core, own, other, activations):
    grads = joined(core, own, other)
    return dot(activations, grads.astype(BF), (1, 0)).astype(BF), jnp.sum(grads, axis=0, keepdims=True)


def chip_swap(x):
    return lax.ppermute(x, "wid", CORE_PAIRS)


def body(activations, encoder, encoder_bias, decoder, decoder_bias, kept_mask, boundaries):
    tokens, width = activations.shape
    latents = encoder.shape[1]
    place = lax.axis_index("lat")
    core = lax.axis_index("wid") % N_CORE
    piece = width // SLICES
    span = lax.axis_size("lat") // GROUPS
    group = place // span
    y, z = place // N_Z, place % N_Z
    my_slice = NEAR * y + z % NEAR
    late = z // NEAR >= N_FAR // 2
    half = (tokens // N_CORE, latents)
    half_f32 = [(half, F32)] * 2
    half_low = [(half, BF)]
    many = [((N_X,) + half, BF)]
    sliced = [((SLICES, 2 * PIECE, tokens), BF)]

    has_cut = (place % span == 0) & (group > 0)
    cut = jnp.where(has_cut, boundaries[jnp.maximum(group - 1, 0)] - place * latents, 0)
    rows_act = activations.T
    dec_pad = pad_rows(decoder.T, piece).reshape(SLICES * PIECE, latents)
    target = lax.dynamic_index_in_dim(pad_rows(rows_act, piece), my_slice, 0, False).astype(F32)
    base = lax.dynamic_index_in_dim(pad_rows(decoder_bias[:, None], piece), my_slice, 0, False) - target

    kept, sent = call(encode, half_f32, [core], rows_act, encoder)
    (total,) = call(pair_sum, many, [core], kept, chip_swap(sent))
    pieces = swap(total, "wid", CHIP_GROUPS)
    (own_codes,) = call(kept_codes, half_low, [core], pieces, kept_mask, encoder_bias[None])
    other_codes = chip_swap(own_codes)

    (got,) = call(decode, sliced, [core, cut], own_codes, other_codes, dec_pad)
    got = swap(got, "lat", NEAR_GROUPS)
    (got,) = call(near_sums, [((N_FAR, N_Y, 2 * PIECE, tokens), BF)], [core], got)
    got = swap(got, "lat", FAR_GROUPS)
    (got,) = call(suffixes, sliced, [late, piece], got, base)
    got = swap(got, "lat", NEAR_GROUPS)

    kept, sent = call(back, half_f32, [core, cut], got, dec_pad)
    (total,) = call(pair_sum, many, [core], kept, chip_swap(sent))
    pieces = swap(total, "wid", CHIP_GROUPS)
    suffix_low = got[:, :piece].reshape(width, tokens)
    suffix_high = got[:, PIECE : PIECE + piece].reshape(width, tokens)
    low, high = split_codes(joined(core, own_codes, other_codes), cut)
    decoder_grad = (dot(suffix_low, low, (1, 0)) + dot(suffix_high, high, (1, 0))).astype(BF).T
    tags = got[:, piece : piece + 2, :piece].astype(F32)
    decoder_bias_grad = (tags[:, 0] + tags[:, 1]).reshape(width)
    (own_grads,) = call(kept_grads, half_low, [core], pieces, kept_mask)
    other_grads = chip_swap(own_grads)
    encoder_grad, encoder_bias_grad = call(
        encoder_grads, [((width, latents), BF), ((1, latents), F32)], [core], own_grads, other_grads, rows_act
    )
    return (encoder_grad, encoder_bias_grad.reshape(latents), decoder_grad, decoder_bias_grad)


def solution(mesh):
    placed = (
        P(None, "wid"),
        P("wid", "lat"),
        P("lat"),
        P("lat", "wid"),
        P("wid"),
        P(None, "lat"),
        P(),
    )
    return jax.shard_map(
        body,
        mesh=mesh,
        in_specs=placed,
        out_specs=(P("wid", "lat"), P("lat"), P("lat", "wid"), P("wid")),
        check_vma=False,
    )
```

time: 115 us -> 111 us (0.965)
  blocking collectives: 27 us -> 13.3 us
  starting transfers between devices: 39 us -> 46.5 us
  Pallas kernels: 0 us -> 6.83 us
  matrix products: 5.9 us -> 1.3 us
  waiting for transfers between devices: 31.6 us -> 35.5 us
  other arithmetic: 3.16 us -> 0.31 us
  local copies, waits for them, and re-layouts: 5.98 us -> 4.83 us
    ppermute x0 -> x4, starting transfers between devices: none -> 21.4 us  [chip_swap(): return lax.ppermute(x, 'wid', CORE_PAIRS)]
    all_to_all x5 -> x4, starting transfers between devices: 39 us -> 25.1 us  [swap(): return lax.all_to_all(x, axis, 0, 0, axis_index_groups=groups, tiled=False)]
    all_to_all x2 -> x1, blocking collectives: 27 us -> 13.3 us  [swap(): return lax.all_to_all(x, axis, 0, 0, axis_index_groups=groups, tiled=False)]
    pallas_call x0 -> x10, Pallas kernels: none -> 6.83 us  [call(): pl.pallas_call(kernel, out_shape=[jax.ShapeDtypeStruct(shape, dtype) for...]
    dot_general x8 -> x2, matrix products: 5.9 us -> 1.3 us  [dot(): lax.dot_general(a, b, (((over[0],), (over[1],)), ((), ())), preferred_ele...]
    broadcast_in_dim x3 -> x0, local copies, waits for them, and re-layouts: 2.09 us -> none  [copies(): return jnp.broadcast_to(x[None], (count,) + x.shape)]
    ppermute x0 -> x4, waiting for transfers between devices: none -> 1.94 us  [chip_swap(): return lax.ppermute(x, 'wid', CORE_PAIRS)]
    all_to_all x5 -> x4, waiting for transfers between devices: 31.6 us -> 33.5 us  [swap(): return lax.all_to_all(x, axis, 0, 0, axis_index_groups=groups, tiled=False)]
  transfers between devices with their start and end apart: 5 -> 8, of which waited for: 5 -> 7; matrix products, arithmetic and copies ran while one was open for 2% -> 3% of each run, Pallas kernels for 0% -> 0%
where the time goes in v3:
time: 111 us; the launch traced here: 110 us
  starting transfers between devices  46.5 us (42%)
  waiting for transfers between devices  35.5 us (32%)
  blocking collectives  13.3 us (12%)
  Pallas kernels  6.83 us (6%)
  local copies, waits for them, and re-layouts  4.83 us (4%)
  between operations  1.59 us (1%)
  matrix products  1.3 us (1%)
    all_to_all x4, waiting for transfers between devices, swap(): return lax.all_to_all(x, axis, 0, 0, axis_index_groups=groups, tiled=False)  33.5 us
    all_to_all x4, starting transfers between devices, swap(): return lax.all_to_all(x, axis, 0, 0, axis_index_groups=groups, tiled=False)  25.1 us
    ppermute x4, starting transfers between devices, chip_swap(): return lax.ppermute(x, 'wid', CORE_PAIRS)  21.4 us
    all_to_all x1, blocking collectives, swap(): return lax.all_to_all(x, axis, 0, 0, axis_index_groups=groups, tiled=False)  13.3 us
    pallas_call x10, Pallas kernels, call(): pl.pallas_call(kernel, out_shape=[jax.ShapeDtypeStruct(shape, dtype) for...  6.83 us
    unnamed x16, local copies, waits for them, and re-layouts  3.25 us
  transfers between devices with their start and end apart: 8, of which 7 were waited for; matrix products, arithmetic and copies ran while one was open for 3% of the time, Pallas kernels for 0%

profile of v3, /device:TPU:1, one launch (start us, length us, event | category | flops | bytes accessed | tf_op | source)
XLA Modules:
  0.0 110.1 jit_solution(13591301738880413356)
XLA Ops:
  0.6 0.0 copy-start.1
  0.7 0.9 copy-done.1
  1.5 0.0 copy-start.3
  1.5 1.0 copy-done.3
  2.6 0.3 encode.1
  2.8 8.8 %collective-permute-start = (f32[64,512]{1,0:T(8,128)S(1)}, f32[64,512]{1,0:T(8,128)S(1)}, u32[]{:S(2)}, u32[]{:S(2)}) collective-permute-start(f32[64,512]{1,0:T(8,128)S(1)} %get-tuple-element.11), channel_id=1, source_target_pairs={{0,1},{1,0},{2,3},{3,2},{4,5},{5,4},{6,7},{7,6},{8,9},{9,8},{10,11... | collective-permute-start | bytes 393224 | tf_op jit(solution)/shard_map/ppermute | solution.py:159
  11.6 1.0 collective-permute-done.refs_1_
  12.6 0.0 copy-start.5
  12.6 0.7 pair_sum.2
  13.3 3.4 %all-to-all-start = ((bf16[4,64,512]{2,1,0:T(8,128)(2,1)}), bf16[4,64,512]{2,1,0:T(8,128)(2,1)S(1)}, u32[]{:S(2)}, u32[]{:S(2)}) async-start(bf16[4,64,512]{2,1,0:T(8,128)(2,1)} %pair_sum.2), calls=%async_computation | async-start | bytes 524288 | tf_op jit(solution)/shard_map/all_to_all | solution.py:24
  16.8 0.0 copy-done.5
  16.8 0.1 reshape.33
  16.9 0.0 copy-start.7
  16.9 0.6 copy-done.7
  17.5 0.6 dynamic_slice.11
  18.8 0.0 copy-start
  18.8 0.0 copy-start.4
  18.8 4.0 %all-to-all-done.refs_0_ = bf16[4,64,512]{2,1,0:T(8,128)(2,1)S(1)} async-done(((bf16[4,64,512]{2,1,0:T(8,128)(2,1)}), bf16[4,64,512]{2,1,0:T(8,128)(2,1)S(1)}, u32[]{:S(2)}, u32[]{:S(2)}) %all-to-all-start) | async-done | bytes 262176 | tf_op jit(solution)/shard_map/all_to_all | solution.py:24
  22.8 0.0 copy-done
  22.8 0.0 copy-done.4
  22.8 0.1 kept_codes.1.refs_0_
  22.9 3.4 %collective-permute-start.1 = (bf16[64,512]{1,0:T(8,128)(2,1)S(1)}, bf16[64,512]{1,0:T(8,128)(2,1)S(1)}, u32[]{:S(2)}, u32[]{:S(2)}) collective-permute-start(bf16[64,512]{1,0:T(8,128)(2,1)S(1)} %kept_codes.1.refs_0_), channel_id=1, source_target_pairs={{0,1},{1,0},{2,3},{3,2},{4,5},{5,4},{6,7},{7,6},{8,9},{9,8},{10,11... | collective-permute-start | bytes 196616 | tf_op jit(solution)/shard_map/ppermute | solution.py:159
  26.3 0.1 pad_add_fusion.scalar_ref
  26.4 0.8 collective-permute-done.1.refs_1_
  27.2 1.0 decode.1
  28.2 13.3 %all_to_all.25.refs_0_ = bf16[16,64,128]{2,1,0:T(8,128)(2,1)S(1)} all-to-all(bf16[16,64,128]{2,1,0:T(8,128)(2,1)S(1)} %decode.1), channel_id=1, replica_groups={{0,8,16,24,128,136,144,152,256,264,272,280,384,392,400,408},{32,40,48,5..., dimensions={0} | all-to-all | bytes 524288 | tf_op jit(solution)/shard_map/all_to_all | solution.py:24
  41.5 0.7 near_sums.1
  42.2 0.0 copy-start.2
  42.2 12.2 %all-to-all-start.2 = ((bf16[4,4,64,128]{3,2,1,0:T(8,128)(2,1)}), bf16[4,4,64,128]{3,2,1,0:T(8,128)(2,1)S(1)}, u32[]{:S(2)}, u32[]{:S(2)}) async-start(bf16[4,4,64,128]{3,2,1,0:T(8,128)(2,1)} %near_sums.1), calls=%async_computation.2 | async-start | bytes 524288 | tf_op jit(solution)/shard_map/all_to_all | solution.py:24
  54.4 0.0 copy-done.2
  54.5 0.0 copy-start.6
  54.5 0.7 copy-done.6
  55.2 0.1 reshape_broadcast_in_dim.3
  55.3 0.1 pad_add_fusion.1.scalar_ref
  55.4 0.1 convert_subtract_fusion.refs_1_
  55.4 14.8 %all-to-all-done.2.refs_0_ = bf16[4,4,64,128]{3,2,1,0:T(8,128)(2,1)S(1)} async-done(((bf16[4,4,64,128]{3,2,1,0:T(8,128)(2,1)}), bf16[4,4,64,128]{3,2,1,0:T(8,128)(2,1)S(1)}, u32[]{:S(2)}, u32[]{:S(2)}) %all-to-all-start.2) | async-done | bytes 262176 | tf_op jit(solution)/shard_map/all_to_all | solution.py:24
  70.3 1.4 %suffixes.1 = bf16[16,64,128]{2,1,0:T(8,128)(2,1)} custom-call(s32[2]{0:T(128)S(1)} %pad_add_fusion.1.scalar_ref, bf16[4,4,64,128]{3,2,1,0:T(8,128)(2,1)S(1)} %all-to-all-done.2.refs_0_, f32[32,128]{1,0:T(8,128)S(1)} %convert_subtract_fusion.refs_1_), custom_call_target="tpu_custom_call" | custom-call | tf_op jit(solution)/shard_map/suffixes/pallas_call | solution.py:53
  71.7 6.1 %all-to-all-start.3 = ((bf16[16,64,128]{2,1,0:T(8,128)(2,1)}), bf16[16,64,128]{2,1,0:T(8,128)(2,1)S(1)}, u32[]{:S(2)}, u32[]{:S(2)}) async-start(bf16[16,64,128]{2,1,0:T(8,128)(2,1)} %suffixes.1), calls=%async_computation.3 | async-start | bytes 524288 | tf_op jit(solution)/shard_map/all_to_all | solution.py:24
  77.8 8.0 %all-to-all-done.3.refs_0_ = bf16[16,64,128]{2,1,0:T(8,128)(2,1)S(1)} async-done(((bf16[16,64,128]{2,1,0:T(8,128)(2,1)}), bf16[16,64,128]{2,1,0:T(8,128)(2,1)S(1)}, u32[]{:S(2)}, u32[]{:S(2)}) %all-to-all-start.3) | async-done | bytes 262176 | tf_op jit(solution)/shard_map/all_to_all | solution.py:24
  85.8 0.9 back.1
  86.7 6.5 %collective-permute-start.2 = (f32[64,512]{1,0:T(8,128)S(1)}, f32[64,512]{1,0:T(8,128)S(1)}, u32[]{:S(2)}, u32[]{:S(2)}) collective-permute-start(f32[64,512]{1,0:T(8,128)S(1)} %get-tuple-element.13), channel_id=1, source_target_pairs={{0,1},{1,0},{2,3},{3,2},{4,5},{5,4},{6,7},{7,6},{8,9},{9,8},{10,11... | collective-permute-start | bytes 393224 | tf_op jit(solution)/shard_map/ppermute | solution.py:159
  93.2 0.3 fusion.1
  93.4 1.0 fusion
  94.5 0.0 collective-permute-done.2.refs_1_
  94.5 0.7 pair_sum.3
  95.2 3.4 %all-to-all-start.4 = ((bf16[4,64,512]{2,1,0:T(8,128)(2,1)}), bf16[4,64,512]{2,1,0:T(8,128)(2,1)S(1)}, u32[]{:S(2)}, u32[]{:S(2)}) async-start(bf16[4,64,512]{2,1,0:T(8,128)(2,1)} %pair_sum.3), calls=%async_computation.4 | async-start | bytes 524288 | tf_op jit(solution)/shard_map/all_to_all | solution.py:24
  98.6 6.8 %all-to-all-done.4.refs_0_ = bf16[4,64,512]{2,1,0:T(8,128)(2,1)S(1)} async-done(((bf16[4,64,512]{2,1,0:T(8,128)(2,1)}), bf16[4,64,512]{2,1,0:T(8,128)(2,1)S(1)}, u32[]{:S(2)}, u32[]{:S(2)}) %all-to-all-start.4) | async-done | bytes 262176 | tf_op jit(solution)/shard_map/all_to_all | solution.py:24
  105.4 0.1 kept_grads.1.refs_0_
  105.5 2.7 %collective-permute-start.3 = (bf16[64,512]{1,0:T(8,128)(2,1)S(1)}, bf16[64,512]{1,0:T(8,128)(2,1)S(1)}, u32[]{:S(2)}, u32[]{:S(2)}) collective-permute-start(bf16[64,512]{1,0:T(8,128)(2,1)S(1)} %kept_grads.1.refs_0_), channel_id=1, source_target_pairs={{0,1},{1,0},{2,3},{3,2},{4,5},{5,4},{6,7},{7,6},{8,9},{9,8},{10,11... | collective-permute-start | bytes 196616 | tf_op jit(solution)/shard_map/ppermute | solution.py:159
  108.2 0.7 add.52
  108.9 0.2 collective-permute-done.3.refs_1_
  109.1 1.1 encoder_grads.1
  (10 shorter events, 0.2 us)
Async XLA Ops:
  0.6 0.9 copy-start.1
  1.5 1.0 copy-start.3
  2.8 9.8 %collective-permute-start = (f32[64,512]{1,0:T(8,128)S(1)}, f32[64,512]{1,0:T(8,128)S(1)}, u32[]{:S(2)}, u32[]{:S(2)}) collective-permute-start(f32[64,512]{1,0:T(8,128)S(1)} %get-tuple-element.11), channel_id=1, source_target_pairs={{0,1},{1,0},{2,3},{3,2},{4,5},{5,4},{6,7},{7,6},{8,9},{9,8},{10,11... | collective-permute-start | bytes 393224 | tf_op jit(solution)/shard_map/ppermute | solution.py:159
  12.6 4.2 %copy-start.5 = (bf16[512,448]{0,1:T(8,128)(2,1)S(1)}, bf16[512,448]{0,1:T(8,128)(2,1)}, u32[]{:S(2)}) copy-start(bf16[512,448]{0,1:T(8,128)(2,1)} %param.10) | copy-start | bytes 1376260
  13.3 9.5 %all-to-all-start = ((bf16[4,64,512]{2,1,0:T(8,128)(2,1)}), bf16[4,64,512]{2,1,0:T(8,128)(2,1)S(1)}, u32[]{:S(2)}, u32[]{:S(2)}) async-start(bf16[4,64,512]{2,1,0:T(8,128)(2,1)} %pair_sum.2), calls=%async_computation | async-start | bytes 524288 | tf_op jit(solution)/shard_map/all_to_all | solution.py:24
  16.9 0.7 copy-start.7
  18.8 4.1 %copy-start = (s32[128,512]{1,0:T(8,128)S(1)}, s32[128,512]{1,0:T(8,128)}, u32[]{:S(2)}) copy-start(s32[128,512]{1,0:T(8,128)} %refs_1_.5) | copy-start | bytes 786436
  18.8 4.1 %copy-start.4 = (f32[512]{0:T(512)S(1)}, f32[512]{0:T(512)}, u32[]{:S(2)}) copy-start(f32[512]{0:T(512)} %param.9) | copy-start | bytes 6148
  22.9 4.3 %collective-permute-start.1 = (bf16[64,512]{1,0:T(8,128)(2,1)S(1)}, bf16[64,512]{1,0:T(8,128)(2,1)S(1)}, u32[]{:S(2)}, u32[]{:S(2)}) collective-permute-start(bf16[64,512]{1,0:T(8,128)(2,1)S(1)} %kept_codes.1.refs_0_), channel_id=1, source_target_pairs={{0,1},{1,0},{2,3},{3,2},{4,5},{5,4},{6,7},{7,6},{8,9},{9,8},{10,11... | collective-permute-start | bytes 196616 | tf_op jit(solution)/shard_map/ppermute | solution.py:159
  42.2 12.2 %copy-start.2 = (bf16[128,448]{0,1:T(8,128)(2,1)S(1)}, bf16[128,448]{0,1:T(8,128)(2,1)}, u32[]{:S(2)}) copy-start(bf16[128,448]{0,1:T(8,128)(2,1)} %param.7) | copy-start | bytes 344068
  42.2 28.0 %all-to-all-start.2 = ((bf16[4,4,64,128]{3,2,1,0:T(8,128)(2,1)}), bf16[4,4,64,128]{3,2,1,0:T(8,128)(2,1)S(1)}, u32[]{:S(2)}, u32[]{:S(2)}) async-start(bf16[4,4,64,128]{3,2,1,0:T(8,128)(2,1)} %near_sums.1), calls=%async_computation.2 | async-start | bytes 524288 | tf_op jit(solution)/shard_map/all_to_all | solution.py:24
  54.5 0.7 copy-start.6
  71.7 14.1 %all-to-all-start.3 = ((bf16[16,64,128]{2,1,0:T(8,128)(2,1)}), bf16[16,64,128]{2,1,0:T(8,128)(2,1)S(1)}, u32[]{:S(2)}, u32[]{:S(2)}) async-start(bf16[16,64,128]{2,1,0:T(8,128)(2,1)} %suffixes.1), calls=%async_computation.3 | async-start | bytes 524288 | tf_op jit(solution)/shard_map/all_to_all | solution.py:24
  86.7 7.8 %collective-permute-start.2 = (f32[64,512]{1,0:T(8,128)S(1)}, f32[64,512]{1,0:T(8,128)S(1)}, u32[]{:S(2)}, u32[]{:S(2)}) collective-permute-start(f32[64,512]{1,0:T(8,128)S(1)} %get-tuple-element.13), channel_id=1, source_target_pairs={{0,1},{1,0},{2,3},{3,2},{4,5},{5,4},{6,7},{7,6},{8,9},{9,8},{10,11... | collective-permute-start | bytes 393224 | tf_op jit(solution)/shard_map/ppermute | solution.py:159
  95.2 10.2 %all-to-all-start.4 = ((bf16[4,64,512]{2,1,0:T(8,128)(2,1)}), bf16[4,64,512]{2,1,0:T(8,128)(2,1)S(1)}, u32[]{:S(2)}, u32[]{:S(2)}) async-start(bf16[4,64,512]{2,1,0:T(8,128)(2,1)} %pair_sum.3), calls=%async_computation.4 | async-start | bytes 524288 | tf_op jit(solution)/shard_map/all_to_all | solution.py:24
  105.5 3.6 %collective-permute-start.3 = (bf16[64,512]{1,0:T(8,128)(2,1)S(1)}, bf16[64,512]{1,0:T(8,128)(2,1)S(1)}, u32[]{:S(2)}, u32[]{:S(2)}) collective-permute-start(bf16[64,512]{1,0:T(8,128)(2,1)S(1)} %kept_grads.1.refs_0_), channel_id=1, source_target_pairs={{0,1},{1,0},{2,3},{3,2},{4,5},{5,4},{6,7},{7,6},{8,9},{9,8},{10,11... | collective-permute-start | bytes 196616 | tf_op jit(solution)/shard_map/ppermute | solution.py:159

commit v4 on v3

v4 whole, which is shorter than its diff:
```python
import jax
import jax.numpy as jnp
from jax import lax
from jax.experimental import pallas as pl
from jax.experimental.pallas import tpu as pltpu
from jax.sharding import PartitionSpec as P

GROUPS = 8
BF = jnp.bfloat16
F32 = jnp.float32

N_Y, N_FAR, NEAR = 4, 4, 4
N_Z = N_FAR * NEAR
SLICES = N_Y * NEAR
TURN = [0, 0, NEAR // 2, NEAR // 2]


def at(y, q, s):
    return N_Z * y + NEAR * q + (s + TURN[q]) % NEAR


NEAR_GROUPS = [[at(y, q, s) for y in range(N_Y) for s in range(NEAR)] for q in range(N_FAR)]
FAR_GROUPS = [[at(y, q, s) for q in range(N_FAR)] for y in range(N_Y) for s in range(NEAR)]
PIECE = 32
FILLED = 28
N_CORE, N_X = 2, 4
CORE_GROUPS = [[N_CORE * x + c for c in range(N_CORE)] for x in range(N_X)]
CHIP_GROUPS = [[N_CORE * x + c for x in range(N_X)] for c in range(N_CORE)]


def swap(x, axis, groups=None):
    return lax.all_to_all(x, axis, 0, 0, axis_index_groups=groups, tiled=False)


def copies(x, count):
    return jnp.broadcast_to(x[None], (count,) + x.shape)


def dot(a, b, over):
    return lax.dot_general(a, b, (((over[0],), (over[1],)), ((), ())), preferred_element_type=F32)


def to_slices(x):
    zeros = jnp.zeros((PIECE - FILLED, x.shape[1]), x.dtype)
    return jnp.stack([jnp.concatenate([x[FILLED * i : FILLED * (i + 1)], zeros], axis=0) for i in range(SLICES)])


def from_slices(x):
    return jnp.concatenate([x[i, :FILLED] for i in range(SLICES)], axis=0)


def call(stage, shapes, scalars, *arrays):
    n_in = len(arrays)
    scalars = scalars or [0]

    def kernel(scalar_ref, *refs):
        values = [scalar_ref[i] for i in range(len(scalars))]
        outs = stage(*values, *[ref[...] for ref in refs[:n_in]])
        for ref, out in zip(refs[n_in:], outs, strict=True):
            if isinstance(out, list):
                for i, one in enumerate(out):
                    ref[i] = one
            else:
                ref[...] = out

    vmem = pl.BlockSpec(memory_space=pltpu.VMEM)
    return pl.pallas_call(
        kernel,
        out_shape=[jax.ShapeDtypeStruct(shape, dtype) for shape, dtype in shapes],
        in_specs=[pl.BlockSpec(memory_space=pltpu.SMEM)] + [vmem] * n_in,
        out_specs=[vmem] * len(shapes),
        compiler_params=pltpu.CompilerParams(vmem_limit_bytes=32 * 1024 * 1024),
        name=stage.__name__,
    )(jnp.stack([jnp.asarray(v, jnp.int32) for v in scalars]), *arrays)


def half_of(core, x):
    half = x.shape[0] // N_CORE
    return jnp.where(core == 0, x[:half], x[half:])


def split_codes(codes, cut):
    below = lax.broadcasted_iota(jnp.int32, codes.shape, 1) < cut
    return jnp.where(below, codes, 0.0).astype(BF), jnp.where(below, 0.0, codes).astype(BF)


def encode_kernel(act_hbm, enc_hbm, out_ref, act, enc, sems):
    copies = [pltpu.make_async_copy(act_hbm, act, sems.at[0]), pltpu.make_async_copy(enc_hbm, enc, sems.at[1])]
    for copy in copies:
        copy.start()
    for copy in copies:
        copy.wait()
    out_ref[...] = dot(act[...], enc[...], (0, 0))


def encode(activations, encoder):
    hbm = pl.BlockSpec(memory_space=pltpu.HBM)
    return pl.pallas_call(
        encode_kernel,
        out_shape=jax.ShapeDtypeStruct((activations.shape[1], encoder.shape[1]), F32),
        in_specs=[hbm, hbm],
        out_specs=pl.BlockSpec(memory_space=pltpu.VMEM),
        scratch_shapes=[
            pltpu.VMEM(activations.shape, BF),
            pltpu.VMEM(encoder.shape, BF),
            pltpu.SemaphoreType.DMA((2,)),
        ],
        compiler_params=pltpu.CompilerParams(vmem_limit_bytes=32 * 1024 * 1024),
        name="encode",
    )(activations, encoder)


def pair_sum(core, parts):
    return ([(half_of(core, parts[0]) + half_of(core, parts[1])).astype(BF)] * N_X,)


def kept_codes(core, pieces, mask, bias):
    total = jnp.sum(pieces.astype(F32), axis=0) + bias
    return ((half_of(core, mask).astype(F32) * total).astype(BF),)


def kept_grads(core, pieces, mask):
    return ((half_of(core, mask).astype(F32) * jnp.sum(pieces.astype(F32), axis=0)).astype(BF),)


def lanes_of(core, x):
    zeros = jnp.zeros_like(x)
    first, second = jnp.concatenate([x, zeros], axis=0), jnp.concatenate([zeros, x], axis=0)
    return first if core == 0 else second


def decode(cut, codes, decoders):
    decoded = []
    for part in split_codes(codes.astype(F32), cut):
        both = dot(decoders[0], lanes_of(0, part), (1, 1)) + dot(decoders[1], lanes_of(1, part), (1, 1))
        decoded.append(to_slices(both))
    return (jnp.concatenate(decoded, axis=1).astype(BF),)


def near_sums(core, got):
    tokens = got.shape[-1]
    got = got.astype(F32).reshape(N_Y, NEAR, 2 * PIECE, tokens)
    return ([jnp.sum(got, axis=1).astype(BF)] * N_FAR,)


def suffixes(late, rows, got, base):
    got = got.astype(F32)
    low, high = got[:, :, :PIECE], got[:, :, PIECE:]
    run = base
    errors = []
    for y in range(N_Y):
        run = run + ((high[0, y] + high[1, y]) + low[2, y])
        errors.append(run)
        part = high[2, y] + high[3, y]
        run = run + (part + low[0, y + 1] if y + 1 < N_Y else part)
        errors.append(run)
    tail = jnp.zeros_like(base)
    suffix = []
    for error in reversed(errors):
        tail = tail + error
        suffix.append(tail / GROUPS)
    suffix = suffix[::-1]
    row = lax.broadcasted_iota(jnp.int32, base.shape, 0)
    lane = lax.broadcasted_iota(jnp.int32, base.shape, 1)
    tags = []
    own = lane < base.shape[1] // N_CORE
    for side in (own, jnp.logical_not(own)):
        token_sum = jnp.sum(jnp.where(side, suffix[0], 0.0), axis=1, keepdims=True)
        token_row = jnp.sum(jnp.where(row == lane, token_sum, 0.0), axis=0, keepdims=True)
        token_high = token_row.astype(BF).astype(F32)
        tags += [token_high, token_row - token_high]
    out = []
    for y in range(N_Y):
        own = jnp.where(late == 1, suffix[2 * y + 1], suffix[2 * y])
        previous = jnp.where(late == 1, suffix[2 * y], suffix[max(2 * y - 1, 0)])
        for i, tag in enumerate(tags):
            previous = jnp.where(row == rows + i, tag, previous)
        out += [jnp.concatenate([previous, own], axis=0).astype(BF)] * NEAR
    return (out,)


def slots(got):
    got = got.astype(F32)
    return from_slices(got[:, :PIECE]).astype(BF), from_slices(got[:, PIECE:]).astype(BF)


def back(cut, got, decoders):
    half = got.shape[-1] // N_CORE
    low, high = [dot(x, decoders[0], (0, 0))[:half] + dot(x, decoders[1], (0, 0))[half:] for x in slots(got)]
    below = lax.broadcasted_iota(jnp.int32, low.shape, 1) < cut
    return ([jnp.where(below, low, high).astype(BF)] * N_X,)


def decoder_grads(core, cut, got, codes):
    total = 0.0
    for half in range(N_CORE):
        parts = split_codes(codes[half].astype(F32), cut)
        for suffix, part in zip(slots(got[half]), parts):
            part = part.astype(F32)
            part = jnp.where(core == 0, lanes_of(0, part), lanes_of(1, part)).astype(BF)
            total = total + dot(suffix, part, (1, 0))
    return (total.astype(BF),)


def encoder_grads(_, grads, activations):
    grads = jnp.concatenate([grads[0], grads[1]], axis=0)
    bias = jnp.sum(grads.astype(F32), axis=0, keepdims=True)
    return dot(activations, grads, (1, 0)).astype(BF), bias


def both_cores(x):
    return lax.all_gather(x, "wid", axis_index_groups=CORE_GROUPS)


def body(activations, encoder, encoder_bias, decoder, decoder_bias, kept_mask, boundaries):
    tokens, width = activations.shape
    latents = encoder.shape[1]
    place = lax.axis_index("lat")
    core = lax.axis_index("wid") % N_CORE
    span = lax.axis_size("lat") // GROUPS
    group = place // span
    y, z = place // N_Z, place % N_Z
    late = z // NEAR >= N_FAR // 2
    my_slice = NEAR * y + (z - jnp.where(late, NEAR // 2, 0)) % NEAR
    half = (tokens // N_CORE, latents)
    half_low = [(half, BF)]
    many = [((N_X,) + half, BF)]
    sliced = [((SLICES, 2 * PIECE, tokens), BF)]

    has_cut = (place % span == 0) & (group > 0)
    cut = jnp.where(has_cut, boundaries[jnp.maximum(group - 1, 0)] - place * latents, 0)
    rows_act = activations.T

    (total,) = call(pair_sum, many, [core], both_cores(encode(rows_act, encoder)))
    decoder_rows, total = lax.optimization_barrier((decoder.T, total))
    pieces = swap(total, "wid", CHIP_GROUPS)
    decoders = both_cores(decoder_rows)
    (my_codes,) = call(kept_codes, half_low, [core], pieces, kept_mask, encoder_bias[None])

    target = lax.dynamic_index_in_dim(rows_act.reshape(SLICES, FILLED, tokens), my_slice, 0, False).astype(F32)
    base = lax.dynamic_index_in_dim(decoder_bias.reshape(SLICES, FILLED, 1), my_slice, 0, False) - target
    base = both_cores(jnp.pad(base, ((0, PIECE - FILLED), (0, 0))))
    base = jnp.where(core == 0, base[:, :, : half[0]], base[:, :, half[0] :])
    base = jnp.concatenate([base[0], base[1]], axis=1)

    (got,) = call(decode, sliced, [cut], my_codes, decoders)
    got = swap(got, "lat", NEAR_GROUPS)
    got, codes = lax.optimization_barrier((got, both_cores(my_codes)))
    (got,) = call(near_sums, [((N_FAR, N_Y, 2 * PIECE, tokens), BF)], [core], got)
    got = swap(got, "lat", FAR_GROUPS)
    (got,) = call(suffixes, sliced, [late, FILLED], got, base)
    got = swap(got, "lat", NEAR_GROUPS)

    (total,) = call(back, many, [cut], got, decoders)
    got, total = lax.optimization_barrier((got, total))
    pieces = swap(total, "wid", CHIP_GROUPS)
    got = both_cores(got)
    (decoder_grad,) = call(decoder_grads, [((width, latents), BF)], [core, cut], got, codes)
    first_tag = jnp.where(core == 0, FILLED, FILLED + 2)
    tags = lax.dynamic_slice_in_dim(got, first_tag, 2, 2)[..., :FILLED]
    decoder_bias_grad = jnp.sum(tags.astype(F32), axis=(0, 2)).reshape(width)
    (my_grads,) = call(kept_grads, half_low, [core], pieces, kept_mask)
    encoder_grad, encoder_bias_grad = call(
        encoder_grads, [((width, latents), BF), ((1, latents), F32)], [], both_cores(my_grads), rows_act
    )
    return (encoder_grad, encoder_bias_grad.reshape(latents), decoder_grad.T, decoder_bias_grad)


def solution(mesh):
    placed = (
        P(None, "wid"),
        P("wid", "lat"),
        P("lat"),
        P("lat", "wid"),
        P("wid"),
        P(None, "lat"),
        P(),
    )
    return jax.shard_map(
        body,
        mesh=mesh,
        in_specs=placed,
        out_specs=(P("wid", "lat"), P("lat"), P("lat", "wid"), P("wid")),
        check_vma=False,
    )
```

time: 111 us -> 98 us (0.88)
  waiting for transfers between devices: 35.5 us -> 21 us
  blocking collectives: 13.3 us -> 27.6 us
  starting transfers between devices: 46.5 us -> 32.9 us
  Pallas kernels: 6.83 us -> 9.11 us
  matrix products: 1.3 us -> 0 us
    all_gather x0 -> x6, blocking collectives: none -> 27.6 us  [both_cores(): return lax.all_gather(x, 'wid', axis_index_groups=CORE_GROUPS)]
    ppermute x4 -> x0, starting transfers between devices: 21.4 us -> none  [chip_swap(): return lax.ppermute(x, 'wid', CORE_PAIRS)]
    all_to_all x1 -> x0, blocking collectives: 13.3 us -> none  [swap(): return lax.all_to_all(x, axis, 0, 0, axis_index_groups=groups, tiled=False)]
    all_to_all x4 -> x5, waiting for transfers between devices: 33.5 us -> 21 us  [swap(): return lax.all_to_all(x, axis, 0, 0, axis_index_groups=groups, tiled=False)]
    all_to_all x4 -> x5, starting transfers between devices: 25.1 us -> 32.9 us  [swap(): return lax.all_to_all(x, axis, 0, 0, axis_index_groups=groups, tiled=False)]
    ppermute x4 -> x0, waiting for transfers between devices: 1.94 us -> none  [chip_swap(): return lax.ppermute(x, 'wid', CORE_PAIRS)]
    pallas_call x10 -> x9, Pallas kernels: 6.83 us -> 8.45 us  [call(): pl.pallas_call(kernel, out_shape=[jax.ShapeDtypeStruct(shape, dtype) for...]
    dot_general x2 -> x0, matrix products: 1.3 us -> none  [dot(): lax.dot_general(a, b, (((over[0],), (over[1],)), ((), ())), preferred_ele...]
  transfers between devices with their start and end apart: 8 -> 5, of which waited for: 7 -> 4; matrix products, arithmetic and copies ran while one was open for 3% -> 2% of each run, Pallas kernels for 0% -> 2%
where the time goes in v4:
time: 98 us; the launch traced here: 97.2 us
  starting transfers between devices  32.9 us (34%)
  blocking collectives  27.6 us (28%)
  waiting for transfers between devices  21 us (21%)
  Pallas kernels  9.11 us (9%)
  local copies, waits for them, and re-layouts  4.64 us (5%)
  between operations  1.56 us (2%)
    all_to_all x5, starting transfers between devices, swap(): return lax.all_to_all(x, axis, 0, 0, axis_index_groups=groups, tiled=False)  32.9 us
    all_gather x6, blocking collectives, both_cores(): return lax.all_gather(x, 'wid', axis_index_groups=CORE_GROUPS)  27.6 us
    all_to_all x5, waiting for transfers between devices, swap(): return lax.all_to_all(x, axis, 0, 0, axis_index_groups=groups, tiled=False)  21 us
    pallas_call x9, Pallas kernels, call(): pl.pallas_call(kernel, out_shape=[jax.ShapeDtypeStruct(shape, dtype) for...  8.45 us
    unnamed x16, local copies, waits for them, and re-layouts  3.25 us
  transfers between devices with their start and end apart: 5, of which 4 were waited for; matrix products, arithmetic and copies ran while one was open for 2% of the time, Pallas kernels for 2%

profile of v4, /device:TPU:1, one launch (start us, length us, event | category | flops | bytes accessed | tf_op | source)
XLA Modules:
  0.0 97.2 jit_solution(5212405211227102718)
XLA Ops:
  0.6 0.0 copy-start.1
  0.7 0.9 copy-done.1
  1.5 0.0 copy-start.3
  1.5 1.0 %copy-done.3 = bf16[448,512]{1,0:T(8,128)(2,1)S(1)} copy-done((bf16[448,512]{1,0:T(8,128)(2,1)S(1)}, bf16[448,512]{1,0:T(8,128)(2,1)}, u32[]{:S(2)}) %copy-start.3) | copy-done | bytes 458776
  2.6 0.7 encode.1
  3.2 8.7 %all-gather = f32[256,512]{1,0:T(8,128)S(1)} all-gather(f32[128,512]{1,0:T(8,128)S(1)} %encode.1), channel_id=2, replica_groups={{0,1},{2,3},{4,5},{6,7},{8,9},{10,11},{12,13},{14,15},{16,17},{18,19},{..., dimensions={0}, use_global_device_ids=true | all-gather | bytes 786432 | tf_op jit(solution)/shard_map/all_gather | solution.py:212
  11.9 0.7 pair_sum.1
  12.6 0.0 copy-start.5
  12.6 3.5 %all-to-all-start = ((bf16[4,64,512]{2,1,0:T(8,128)(2,1)}), bf16[4,64,512]{2,1,0:T(8,128)(2,1)S(1)}, u32[]{:S(2)}, u32[]{:S(2)}) async-start(bf16[4,64,512]{2,1,0:T(8,128)(2,1)} %pair_sum.1), calls=%async_computation | async-start | bytes 524288 | tf_op jit(solution)/shard_map/all_to_all | solution.py:32
  16.2 0.0 copy-start.7
  16.2 0.6 copy-done.7
  16.9 0.6 dynamic_slice.14
  18.1 0.0 copy-done.5
  18.1 0.0 copy-start
  18.1 0.0 copy-start.4
  18.2 2.6 %all-gather.1 = bf16[896,512]{1,0:T(8,128)(2,1)S(1)} all-gather(bf16[448,512]{1,0:T(8,128)(2,1)S(1)} %bitcast.36), channel_id=3, replica_groups={{0,1},{2,3},{4,5},{6,7},{8,9},{10,11},{12,13},{14,15},{16,17},{18,19},{..., dimensions={0}, use_global_device_ids=true | all-gather | bytes 1376256 | tf_op jit(solution)/shard_map/all_gather | solution.py:212
  20.7 1.5 %all-to-all-done.refs_0_ = bf16[4,64,512]{2,1,0:T(8,128)(2,1)S(1)} async-done(((bf16[4,64,512]{2,1,0:T(8,128)(2,1)}), bf16[4,64,512]{2,1,0:T(8,128)(2,1)S(1)}, u32[]{:S(2)}, u32[]{:S(2)}) %all-to-all-start) | async-done | bytes 262176 | tf_op jit(solution)/shard_map/all_to_all | solution.py:32
  22.3 0.0 copy-done
  22.3 0.0 copy-done.4
  22.3 0.1 kept_codes.1.refs_0_
  22.3 1.3 %decode.1 = bf16[16,64,128]{2,1,0:T(8,128)(2,1)} custom-call(s32[1]{0:T(128)} %bitcast.3.scalar_ref, bf16[64,512]{1,0:T(8,128)(2,1)S(1)} %kept_codes.1.refs_0_, bf16[2,448,512]{2,1,0:T(8,128)(2,1)S(1)} %bitcast.24), custom_call_target="tpu_custom_call" | custom-call | tf_op jit(solution)/shard_map/decode/pallas_call | solution.py:67
  23.7 0.0 copy-start.2
  23.7 3.7 %all-to-all-start.1 = ((bf16[16,64,128]{2,1,0:T(8,128)(2,1)}), bf16[16,64,128]{2,1,0:T(8,128)(2,1)S(1)}, u32[]{:S(2)}, u32[]{:S(2)}) async-start(bf16[16,64,128]{2,1,0:T(8,128)(2,1)} %decode.1), calls=%async_computation.1 | async-start | bytes 524288 | tf_op jit(solution)/shard_map/all_to_all | solution.py:32
  27.4 0.0 copy-done.2
  27.5 0.0 copy-start.6
  27.5 0.7 copy-done.6
  28.2 0.1 reshape.23
  28.3 3.4 %all-gather.2 = bf16[128,512]{1,0:T(8,128)(2,1)S(1)} all-gather(bf16[64,512]{1,0:T(8,128)(2,1)S(1)} %kept_codes.1.refs_0_), channel_id=4, replica_groups={{0,1},{2,3},{4,5},{6,7},{8,9},{10,11},{12,13},{14,15},{16,17},{18,19},{..., dimensions={0}, use_global_device_ids=true | all-gather | bytes 196608 | tf_op jit(solution)/shard_map/all_gather | solution.py:212
  31.7 3.9 %all-to-all-done.1.refs_0_ = bf16[16,64,128]{2,1,0:T(8,128)(2,1)S(1)} async-done(((bf16[16,64,128]{2,1,0:T(8,128)(2,1)}), bf16[16,64,128]{2,1,0:T(8,128)(2,1)S(1)}, u32[]{:S(2)}, u32[]{:S(2)}) %all-to-all-start.1) | async-done | bytes 262176 | tf_op jit(solution)/shard_map/all_to_all | solution.py:32
  35.6 0.7 near_sums.1
  36.4 9.9 %all-to-all-start.2 = ((bf16[4,4,64,128]{3,2,1,0:T(8,128)(2,1)}), bf16[4,4,64,128]{3,2,1,0:T(8,128)(2,1)S(1)}, u32[]{:S(2)}, u32[]{:S(2)}) async-start(bf16[4,4,64,128]{3,2,1,0:T(8,128)(2,1)} %near_sums.1), calls=%async_computation.2 | async-start | bytes 524288 | tf_op jit(solution)/shard_map/all_to_all | solution.py:32
  46.2 0.1 convert_subtract_fusion
  46.3 5.0 %all-gather.3 = f32[64,128]{1,0:T(8,128)S(1)} all-gather(f32[32,128]{1,0:T(8,128)S(1)} %pad.4), channel_id=5, replica_groups={{0,1},{2,3},{4,5},{6,7},{8,9},{10,11},{12,13},{14,15},{16,17},{18,19},{..., dimensions={0}, use_global_device_ids=true | all-gather | bytes 49152 | tf_op jit(solution)/shard_map/all_gather | solution.py:212
  51.3 0.1 pad_add_fusion.scalar_ref
  51.4 0.1 slice_select_fusion
  51.5 0.1 pad_maximum_fusion.refs_1_
  51.6 7.5 %all-to-all-done.2.refs_0_ = bf16[4,4,64,128]{3,2,1,0:T(8,128)(2,1)S(1)} async-done(((bf16[4,4,64,128]{3,2,1,0:T(8,128)(2,1)}), bf16[4,4,64,128]{3,2,1,0:T(8,128)(2,1)S(1)}, u32[]{:S(2)}, u32[]{:S(2)}) %all-to-all-start.2) | async-done | bytes 262176 | tf_op jit(solution)/shard_map/all_to_all | solution.py:32
  59.0 1.4 %suffixes.1 = bf16[16,64,128]{2,1,0:T(8,128)(2,1)} custom-call(s32[2]{0:T(128)S(1)} %pad_add_fusion.scalar_ref, bf16[4,4,64,128]{3,2,1,0:T(8,128)(2,1)S(1)} %all-to-all-done.2.refs_0_, f32[32,128]{1,0:T(8,128)S(1)} %pad_maximum_fusion.refs_1_), custom_call_target="tpu_custom_call" | custom-call | tf_op jit(solution)/shard_map/suffixes/pallas_call | solution.py:67
  60.4 8.1 %all-to-all-start.3 = ((bf16[16,64,128]{2,1,0:T(8,128)(2,1)}), bf16[16,64,128]{2,1,0:T(8,128)(2,1)S(1)}, u32[]{:S(2)}, u32[]{:S(2)}) async-start(bf16[16,64,128]{2,1,0:T(8,128)(2,1)} %suffixes.1), calls=%async_computation.3 | async-start | bytes 524288 | tf_op jit(solution)/shard_map/all_to_all | solution.py:32
  68.6 8.0 %all-to-all-done.3.refs_0_ = bf16[16,64,128]{2,1,0:T(8,128)(2,1)S(1)} async-done(((bf16[16,64,128]{2,1,0:T(8,128)(2,1)}), bf16[16,64,128]{2,1,0:T(8,128)(2,1)S(1)}, u32[]{:S(2)}, u32[]{:S(2)}) %all-to-all-start.3) | async-done | bytes 262176 | tf_op jit(solution)/shard_map/all_to_all | solution.py:32
  76.6 1.2 %back.1 = bf16[4,64,512]{2,1,0:T(8,128)(2,1)} custom-call(s32[1]{0:T(128)} %bitcast.3.scalar_ref, bf16[16,64,128]{2,1,0:T(8,128)(2,1)S(1)} %all-to-all-done.3.refs_0_, bf16[2,448,512]{2,1,0:T(8,128)(2,1)S(1)} %bitcast.25), custom_call_target="tpu_custom_call" | custom-call | tf_op jit(solution)/shard_map/back/pallas_call | solution.py:67
  77.8 7.7 %all-to-all-start.4 = ((bf16[4,64,512]{2,1,0:T(8,128)(2,1)}), bf16[4,64,512]{2,1,0:T(8,128)(2,1)S(1)}, u32[]{:S(2)}, u32[]{:S(2)}) async-start(bf16[4,64,512]{2,1,0:T(8,128)(2,1)} %back.1), calls=%async_computation.4 | async-start | bytes 524288 | tf_op jit(solution)/shard_map/all_to_all | solution.py:32
  85.5 0.1 pad_add_fusion.1.scalar_ref
  85.6 4.2 %all-gather.5 = bf16[32,64,128]{2,1,0:T(8,128)(2,1)S(1)} all-gather(bf16[16,64,128]{2,1,0:T(8,128)(2,1)S(1)} %all-to-all-done.3.refs_0_), channel_id=7, replica_groups={{0,1},{2,3},{4,5},{6,7},{8,9},{10,11},{12,13},{14,15},{16,17},{18,19},{..., dimensions={0}, use_global_device_ids=true | all-gather | bytes 786432 | tf_op jit(solution)/shard_map/all_gather | solution.py:212
  89.9 0.7 reshape.26
  90.5 1.9 %decoder_grads.1 = bf16[448,512]{1,0:T(8,128)(2,1)} custom-call(s32[2]{0:T(128)S(1)} %pad_add_fusion.1.scalar_ref, bf16[2,16,64,128]{3,2,1,0:T(8,128)(2,1)S(1)} %bitcast.27, bf16[2,64,512]{2,1,0:T(8,128)(2,1)S(1)} %bitcast.33), custom_call_target="tpu_custom_call" | custom-call | tf_op jit(solution)/shard_map/decoder_grads/pallas_call | solution.py:67
  92.5 0.0 all-to-all-done.4.refs_0_
  92.5 0.1 kept_grads.1
  92.5 3.7 %all-gather.4 = bf16[128,512]{1,0:T(8,128)(2,1)S(1)} all-gather(bf16[64,512]{1,0:T(8,128)(2,1)S(1)} %kept_grads.1), channel_id=6, replica_groups={{0,1},{2,3},{4,5},{6,7},{8,9},{10,11},{12,13},{14,15},{16,17},{18,19},{..., dimensions={0}, use_global_device_ids=true | all-gather | bytes 196608 | tf_op jit(solution)/shard_map/all_gather | solution.py:212
  96.2 1.0 %encoder_grads.1 = (bf16[448,512]{1,0:T(8,128)(2,1)}, f32[1,512]{1,0:T(1,128)}) custom-call(s32[1]{0:T(128)} %constant.87.clone.1.scalar_ref, bf16[2,64,512]{2,1,0:T(8,128)(2,1)S(1)} %bitcast.32, bf16[448,128]{1,0:T(8,128)(2,1)S(1)} %bitcast.31), custom_call_target="tpu_custom_call" | custom-call | tf_op jit(solution)/shard_map/encoder_grads/pallas_call | solution.py:67
  (5 shorter events, 0.1 us)
Async XLA Ops:
  0.6 0.9 copy-start.1
  1.5 1.0 %copy-start.3 = (bf16[448,512]{1,0:T(8,128)(2,1)S(1)}, bf16[448,512]{1,0:T(8,128)(2,1)}, u32[]{:S(2)}) copy-start(bf16[448,512]{1,0:T(8,128)(2,1)} %enc_hbm.1) | copy-start | bytes 1376260
  12.6 5.5 %copy-start.5 = (bf16[512,448]{0,1:T(8,128)(2,1)S(1)}, bf16[512,448]{0,1:T(8,128)(2,1)}, u32[]{:S(2)}) copy-start(bf16[512,448]{0,1:T(8,128)(2,1)} %param.10) | copy-start | bytes 1376260
  12.6 9.6 %all-to-all-start = ((bf16[4,64,512]{2,1,0:T(8,128)(2,1)}), bf16[4,64,512]{2,1,0:T(8,128)(2,1)S(1)}, u32[]{:S(2)}, u32[]{:S(2)}) async-start(bf16[4,64,512]{2,1,0:T(8,128)(2,1)} %pair_sum.1), calls=%async_computation | async-start | bytes 524288 | tf_op jit(solution)/shard_map/all_to_all | solution.py:32
  16.2 0.7 copy-start.7
  18.1 4.2 %copy-start = (s32[128,512]{1,0:T(8,128)S(1)}, s32[128,512]{1,0:T(8,128)}, u32[]{:S(2)}) copy-start(s32[128,512]{1,0:T(8,128)} %refs_1_.3) | copy-start | bytes 786436
  18.1 4.1 %copy-start.4 = (f32[512]{0:T(512)S(1)}, f32[512]{0:T(512)}, u32[]{:S(2)}) copy-start(f32[512]{0:T(512)} %param.9) | copy-start | bytes 6148
  23.7 3.7 %copy-start.2 = (bf16[128,448]{0,1:T(8,128)(2,1)S(1)}, bf16[128,448]{0,1:T(8,128)(2,1)}, u32[]{:S(2)}) copy-start(bf16[128,448]{0,1:T(8,128)(2,1)} %param.7) | copy-start | bytes 344068
  23.7 12.0 %all-to-all-start.1 = ((bf16[16,64,128]{2,1,0:T(8,128)(2,1)}), bf16[16,64,128]{2,1,0:T(8,128)(2,1)S(1)}, u32[]{:S(2)}, u32[]{:S(2)}) async-start(bf16[16,64,128]{2,1,0:T(8,128)(2,1)} %decode.1), calls=%async_computation.1 | async-start | bytes 524288 | tf_op jit(solution)/shard_map/all_to_all | solution.py:32
  27.5 0.7 copy-start.6
  36.4 22.7 %all-to-all-start.2 = ((bf16[4,4,64,128]{3,2,1,0:T(8,128)(2,1)}), bf16[4,4,64,128]{3,2,1,0:T(8,128)(2,1)S(1)}, u32[]{:S(2)}, u32[]{:S(2)}) async-start(bf16[4,4,64,128]{3,2,1,0:T(8,128)(2,1)} %near_sums.1), calls=%async_computation.2 | async-start | bytes 524288 | tf_op jit(solution)/shard_map/all_to_all | solution.py:32
  60.4 16.2 %all-to-all-start.3 = ((bf16[16,64,128]{2,1,0:T(8,128)(2,1)}), bf16[16,64,128]{2,1,0:T(8,128)(2,1)S(1)}, u32[]{:S(2)}, u32[]{:S(2)}) async-start(bf16[16,64,128]{2,1,0:T(8,128)(2,1)} %suffixes.1), calls=%async_computation.3 | async-start | bytes 524288 | tf_op jit(solution)/shard_map/all_to_all | solution.py:32
  77.8 14.7 %all-to-all-start.4 = ((bf16[4,64,512]{2,1,0:T(8,128)(2,1)}), bf16[4,64,512]{2,1,0:T(8,128)(2,1)S(1)}, u32[]{:S(2)}, u32[]{:S(2)}) async-start(bf16[4,64,512]{2,1,0:T(8,128)(2,1)} %back.1), calls=%async_computation.4 | async-start | bytes 524288 | tf_op jit(solution)/shard_map/all_to_all | solution.py:32

commit v5 on v4

v5 whole, which is shorter than its diff:
```python
import jax
import jax.numpy as jnp
from jax import lax
from jax.experimental import pallas as pl
from jax.experimental.pallas import tpu as pltpu
from jax.sharding import PartitionSpec as P

GROUPS = 8
BF = jnp.bfloat16
F32 = jnp.float32

N_Y, N_FAR, NEAR = 4, 4, 4
N_Z = N_FAR * NEAR
SLICES = N_Y * NEAR
TURN = [0, 0, NEAR // 2, NEAR // 2]


def at(y, q, s):
    return N_Z * y + NEAR * q + (s + TURN[q]) % NEAR


NEAR_GROUPS = [[at(y, q, s) for y in range(N_Y) for s in range(NEAR)] for q in range(N_FAR)]
FAR_GROUPS = [[at(y, q, s) for q in range(N_FAR)] for y in range(N_Y) for s in range(NEAR)]
PIECE = 28
ROWS = 2 * PIECE
TAG_ROWS = 8
N_CORE, N_X = 2, 4
CORE_GROUPS = [[N_CORE * x + c for c in range(N_CORE)] for x in range(N_X)]
CHIP_GROUPS = [[N_CORE * x + c for x in range(N_X)] for c in range(N_CORE)]


def swap(x, axis, groups=None):
    return lax.all_to_all(x, axis, 0, 0, axis_index_groups=groups, tiled=False)


def copies(x, count):
    return jnp.broadcast_to(x[None], (count,) + x.shape)


def dot(a, b, over):
    return lax.dot_general(a, b, (((over[0],), (over[1],)), ((), ())), preferred_element_type=F32)


def to_slices(first, second):
    rows = [[x[PIECE * i : PIECE * (i + 1)] for x in (first, second)] for i in range(SLICES)]
    return jnp.stack([jnp.concatenate(pair, axis=0) for pair in rows])


def from_slices(x, core):
    x = x.astype(F32)
    return jnp.concatenate([x[i, PIECE * core : PIECE * (core + 1)] for i in range(SLICES)], axis=0)


def call(stage, shapes, scalars, *arrays):
    n_in = len(arrays)
    scalars = scalars or [0]

    def kernel(scalar_ref, *refs):
        values = [scalar_ref[i] for i in range(len(scalars))]
        outs = stage(*values, *[ref[...] for ref in refs[:n_in]])
        for ref, out in zip(refs[n_in:], outs, strict=True):
            if isinstance(out, list):
                for i, one in enumerate(out):
                    ref[i] = one
            else:
                ref[...] = out

    vmem = pl.BlockSpec(memory_space=pltpu.VMEM)
    return pl.pallas_call(
        kernel,
        out_shape=[jax.ShapeDtypeStruct(shape, dtype) for shape, dtype in shapes],
        in_specs=[pl.BlockSpec(memory_space=pltpu.SMEM)] + [vmem] * n_in,
        out_specs=[vmem] * len(shapes),
        compiler_params=pltpu.CompilerParams(vmem_limit_bytes=32 * 1024 * 1024),
        name=stage.__name__,
    )(jnp.stack([jnp.asarray(v, jnp.int32) for v in scalars]), *arrays)


def half_of(core, x):
    half = x.shape[0] // N_CORE
    return jnp.where(core == 0, x[:half], x[half:])


def split_codes(codes, cut):
    codes = codes.astype(F32)
    below = lax.broadcasted_iota(jnp.int32, codes.shape, 1) < cut
    return jnp.concatenate([jnp.where(below, codes, 0.0), jnp.where(below, 0.0, codes)], axis=0).astype(BF)


def turned(_, activations):
    return (activations.astype(F32).T.astype(BF),)


def encode(_, activations, encoder):
    return (dot(activations, encoder, (1, 0)),)


def pair_sum(core, parts):
    return ([(half_of(core, parts[0]) + half_of(core, parts[1])).astype(BF)] * N_X,)


def kept_codes(core, pieces, mask, bias):
    total = jnp.sum(pieces.astype(F32), axis=0) + bias
    return ((half_of(core, mask).astype(F32) * total).astype(BF),)


def kept_grads(core, pieces, mask):
    return ((half_of(core, mask).astype(F32) * jnp.sum(pieces.astype(F32), axis=0)).astype(BF),)


def decode(cut, codes, decoders):
    codes = split_codes(codes, cut)
    first, second = [dot(decoders[core], codes, (1, 1)) for core in range(N_CORE)]
    return (to_slices(first, second).astype(BF),)


def near_sums(core, got):
    tokens = got.shape[-1]
    got = got.astype(F32).reshape(N_Y, NEAR, ROWS, tokens)
    return ([jnp.sum(got, axis=1).astype(BF)] * N_FAR,)


def suffixes(late, got, base):
    got = got.astype(F32)
    half = base.shape[1] // 2

    def other_half(x):
        return pltpu.roll(x, half, 1)

    run = base
    errors = []
    for y in range(N_Y):
        run = run + ((got[0, y] + got[1, y]) + other_half(got[2, y]))
        errors.append(run)
        part = got[2, y] + got[3, y]
        run = run + (part + other_half(got[0, y + 1]) if y + 1 < N_Y else part)
        errors.append(run)
    tail = jnp.zeros_like(base)
    suffix = []
    for error in reversed(errors):
        tail = tail + error
        suffix.append(tail / GROUPS)
    suffix = suffix[::-1]
    row = lax.broadcasted_iota(jnp.int32, base.shape, 0)
    lane = lax.broadcasted_iota(jnp.int32, base.shape, 1)
    token_sum = jnp.sum(jnp.where(lane < half, 0.0, suffix[0]), axis=1, keepdims=True)
    token_row = jnp.sum(jnp.where(row == lane, token_sum, 0.0), axis=0, keepdims=True)
    token_high = token_row.astype(BF).astype(F32)
    tag_row = lax.broadcasted_iota(jnp.int32, (TAG_ROWS, base.shape[1]), 0)
    tags = jnp.where(tag_row == 0, token_high, jnp.where(tag_row == 1, token_row - token_high, 0.0))
    out = []
    for y in range(N_Y):
        own = jnp.where(late == 1, suffix[2 * y + 1], suffix[2 * y])
        previous = jnp.where(late == 1, suffix[2 * y], suffix[max(2 * y - 1, 0)])
        pair = jnp.where(lane < half, other_half(previous), own)
        out += [jnp.concatenate([pair, tags], axis=0).astype(BF)] * NEAR
    return (out,)


def back(cut, got, decoders):
    parts = [dot(from_slices(got, core).astype(BF), decoders[core], (0, 0)) for core in range(N_CORE)]
    total = parts[0] + parts[1]
    half = total.shape[0] // 2
    below = lax.broadcasted_iota(jnp.int32, (half, total.shape[1]), 1) < cut
    return ([jnp.where(below, total[:half], total[half:]).astype(BF)] * N_X,)


def decoder_grads(core, cut, got, codes):
    total = 0.0
    for half in range(N_CORE):
        suffix = jnp.where(core == 0, from_slices(got[half], 0), from_slices(got[half], 1))
        total = total + dot(suffix.astype(BF), split_codes(codes[half], cut), (1, 0))
    return (total.astype(BF),)


def encoder_grads(_, grads, activations):
    grads = jnp.concatenate([grads[0], grads[1]], axis=0)
    bias = jnp.sum(grads.astype(F32), axis=0, keepdims=True)
    return dot(activations, grads, (1, 0)).astype(BF), bias


def both_cores(x):
    return lax.all_gather(x, "wid", axis_index_groups=CORE_GROUPS)


def body(activations, encoder, encoder_bias, decoder, decoder_bias, kept_mask, boundaries):
    tokens, width = activations.shape
    latents = encoder.shape[1]
    place = lax.axis_index("lat")
    core = lax.axis_index("wid") % N_CORE
    span = lax.axis_size("lat") // GROUPS
    group = place // span
    y, z = place // N_Z, place % N_Z
    late = z // NEAR >= N_FAR // 2
    my_slice = NEAR * y + (z - jnp.where(late, NEAR // 2, 0)) % NEAR
    half = (tokens // N_CORE, latents)
    half_low = [(half, BF)]
    many = [((N_X,) + half, BF)]

    has_cut = (place % span == 0) & (group > 0)
    cut = jnp.where(has_cut, boundaries[jnp.maximum(group - 1, 0)] - place * latents, 0)
    rows_act = activations.T

    (turned_act,) = call(turned, [((tokens, width), BF)], [], rows_act)
    (enc_part,) = call(encode, [((tokens, latents), F32)], [], turned_act, encoder)
    (total,) = call(pair_sum, many, [core], both_cores(enc_part))
    decoder_rows, total = lax.optimization_barrier((decoder.T, total))
    pieces = swap(total, "wid", CHIP_GROUPS)
    decoders = both_cores(decoder_rows)
    (my_codes,) = call(kept_codes, half_low, [core], pieces, kept_mask, encoder_bias[None])

    target = lax.dynamic_index_in_dim(rows_act.reshape(SLICES, PIECE, tokens), my_slice, 0, False).astype(F32)
    base = lax.dynamic_index_in_dim(decoder_bias.reshape(SLICES, PIECE, 1), my_slice, 0, False) - target
    base = both_cores(base).reshape(ROWS, tokens)
    base = jnp.where(core == 0, jnp.roll(base, half[0], axis=1), base)

    (got,) = call(decode, [((SLICES, ROWS, tokens), BF)], [cut], my_codes, decoders)
    got = swap(got, "lat", NEAR_GROUPS)
    (got,) = call(near_sums, [((N_FAR, N_Y, ROWS, tokens), BF)], [core], got)
    got = swap(got, "lat", FAR_GROUPS)
    got, codes = lax.optimization_barrier((got, both_cores(my_codes)))
    (got,) = call(suffixes, [((SLICES, ROWS + TAG_ROWS, tokens), BF)], [late], got, base)
    got = swap(got, "lat", NEAR_GROUPS)

    (total,) = call(back, many, [cut], got, decoders)
    got, total = lax.optimization_barrier((got, total))
    pieces = swap(total, "wid", CHIP_GROUPS)
    got = both_cores(got)
    (decoder_grad,) = call(decoder_grads, [((width, latents), BF)], [core, cut], got, codes)
    tags = lax.dynamic_slice_in_dim(got[:, :, ROWS : ROWS + 2], core * PIECE, PIECE, 3)
    decoder_bias_grad = jnp.sum(tags.astype(F32), axis=(0, 2)).reshape(width)
    (my_grads,) = call(kept_grads, half_low, [core], pieces, kept_mask)
    encoder_grad, encoder_bias_grad = call(
        encoder_grads, [((width, latents), BF), ((1, latents), F32)], [], both_cores(my_grads), rows_act
    )
    return (encoder_grad, encoder_bias_grad.reshape(latents), decoder_grad.T, decoder_bias_grad)


def solution(mesh):
    placed = (
        P(None, "wid"),
        P("wid", "lat"),
        P("lat"),
        P("lat", "wid"),
        P("wid"),
        P(None, "lat"),
        P(),
    )
    return jax.shard_map(
        body,
        mesh=mesh,
        in_specs=placed,
        out_specs=(P("wid", "lat"), P("lat"), P("lat", "wid"), P("wid")),
        check_vma=False,
    )
```

time: 98 us -> 93.9 us (0.958)
  starting transfers between devices: 32.9 us -> 29.6 us
  Pallas kernels: 9.11 us -> 7.71 us
    all_to_all x5, starting transfers between devices: 32.9 us -> 29.6 us  [swap(): return lax.all_to_all(x, axis, 0, 0, axis_index_groups=groups, tiled=False)]
    pallas_call x9 -> x11, Pallas kernels: 8.45 us -> 7.71 us  [call(): pl.pallas_call(kernel, out_shape=[jax.ShapeDtypeStruct(shape, dtype) for...]
where the time goes in v5:
time: 93.9 us; the launch traced here: 93.2 us
  starting transfers between devices  29.6 us (32%)
  blocking collectives  27.7 us (29%)
  waiting for transfers between devices  21.5 us (23%)
  Pallas kernels  7.71 us (8%)
  local copies, waits for them, and re-layouts  4.72 us (5%)
  between operations  1.56 us (2%)
    all_to_all x5, starting transfers between devices, swap(): return lax.all_to_all(x, axis, 0, 0, axis_index_groups=groups, tiled=False)  29.6 us
    all_gather x6, blocking collectives, both_cores(): return lax.all_gather(x, 'wid', axis_index_groups=CORE_GROUPS)  27.7 us
    all_to_all x5, waiting for transfers between devices, swap(): return lax.all_to_all(x, axis, 0, 0, axis_index_groups=groups, tiled=False)  21.5 us
    pallas_call x11, Pallas kernels, call(): pl.pallas_call(kernel, out_shape=[jax.ShapeDtypeStruct(shape, dtype) for...  7.71 us
    unnamed x16, local copies, waits for them, and re-layouts  3.25 us
  transfers between devices with their start and end apart: 5, of which 4 were waited for; matrix products, arithmetic and copies ran while one was open for 2% of the time, Pallas kernels for 2%

profile of v5, /device:TPU:1, one launch (start us, length us, event | category | flops | bytes accessed | tf_op | source)
XLA Modules:
  0.0 93.2 jit_solution(2546080864223944396)
XLA Ops:
  0.6 0.0 copy-start.1
  0.7 0.9 copy-done.1
  1.5 0.1 turned.1.refs_0_
  1.7 0.0 copy-start.3
  1.7 1.0 %copy-done.3 = bf16[448,512]{1,0:T(8,128)(2,1)S(1)} copy-done((bf16[448,512]{1,0:T(8,128)(2,1)S(1)}, bf16[448,512]{1,0:T(8,128)(2,1)}, u32[]{:S(2)}) %copy-start.3) | copy-done | bytes 458776
  2.7 0.2 encode.1
  2.9 8.7 %all-gather = f32[256,512]{1,0:T(8,128)S(1)} all-gather(f32[128,512]{1,0:T(8,128)S(1)} %encode.1), channel_id=2, replica_groups={{0,1},{2,3},{4,5},{6,7},{8,9},{10,11},{12,13},{14,15},{16,17},{18,19},{..., dimensions={0}, use_global_device_ids=true | all-gather | bytes 786432 | tf_op jit(solution)/shard_map/all_gather | solution.py:183
  11.6 0.7 pair_sum.1
  12.3 0.0 copy-start.5
  12.4 3.5 %all-to-all-start = ((bf16[4,64,512]{2,1,0:T(8,128)(2,1)}), bf16[4,64,512]{2,1,0:T(8,128)(2,1)S(1)}, u32[]{:S(2)}, u32[]{:S(2)}) async-start(bf16[4,64,512]{2,1,0:T(8,128)(2,1)} %pair_sum.1), calls=%async_computation | async-start | bytes 524288 | tf_op jit(solution)/shard_map/all_to_all | solution.py:33
  15.9 0.0 copy-start.7
  15.9 0.6 copy-done.7
  16.6 0.6 dynamic_slice.14
  17.8 0.0 copy-done.5
  17.8 0.0 copy-start
  17.8 0.0 copy-start.4
  17.9 2.6 %all-gather.1 = bf16[896,512]{1,0:T(8,128)(2,1)S(1)} all-gather(bf16[448,512]{1,0:T(8,128)(2,1)S(1)} %bitcast.28), channel_id=3, replica_groups={{0,1},{2,3},{4,5},{6,7},{8,9},{10,11},{12,13},{14,15},{16,17},{18,19},{..., dimensions={0}, use_global_device_ids=true | all-gather | bytes 1376256 | tf_op jit(solution)/shard_map/all_gather | solution.py:183
  20.5 1.5 %all-to-all-done.refs_0_ = bf16[4,64,512]{2,1,0:T(8,128)(2,1)S(1)} async-done(((bf16[4,64,512]{2,1,0:T(8,128)(2,1)}), bf16[4,64,512]{2,1,0:T(8,128)(2,1)S(1)}, u32[]{:S(2)}, u32[]{:S(2)}) %all-to-all-start) | async-done | bytes 262176 | tf_op jit(solution)/shard_map/all_to_all | solution.py:33
  22.0 0.0 copy-done
  22.0 0.0 copy-done.4
  22.0 0.1 kept_codes.1.refs_0_
  22.1 1.1 %decode.1 = bf16[16,56,128]{2,1,0:T(8,128)(2,1)} custom-call(s32[1]{0:T(128)} %bitcast.3.scalar_ref, bf16[64,512]{1,0:T(8,128)(2,1)S(1)} %kept_codes.1.refs_0_, bf16[2,448,512]{2,1,0:T(8,128)(2,1)S(1)} %bitcast.16), custom_call_target="tpu_custom_call" | custom-call | tf_op jit(solution)/shard_map/decode/pallas_call | solution.py:69
  23.2 0.0 copy-start.2
  23.2 3.7 %all-to-all-start.1 = ((bf16[16,56,128]{2,1,0:T(8,128)(2,1)}), bf16[16,56,128]{2,1,0:T(8,128)(2,1)S(1)}, u32[]{:S(2)}, u32[]{:S(2)}) async-start(bf16[16,56,128]{2,1,0:T(8,128)(2,1)} %decode.1), calls=%async_computation.1 | async-start | bytes 458752 | tf_op jit(solution)/shard_map/all_to_all | solution.py:33
  26.9 0.0 copy-done.2
  26.9 0.0 copy-start.6
  26.9 0.7 copy-done.6
  27.6 0.1 reshape.31
  27.7 6.8 %all-to-all-done.1.refs_0_ = bf16[16,56,128]{2,1,0:T(8,128)(2,1)S(1)} async-done(((bf16[16,56,128]{2,1,0:T(8,128)(2,1)}), bf16[16,56,128]{2,1,0:T(8,128)(2,1)S(1)}, u32[]{:S(2)}, u32[]{:S(2)}) %all-to-all-start.1) | async-done | bytes 229408 | tf_op jit(solution)/shard_map/all_to_all | solution.py:33
  34.5 0.7 near_sums.1
  35.2 10.2 %all-to-all-start.2 = ((bf16[4,4,56,128]{3,2,1,0:T(8,128)(2,1)}), bf16[4,4,56,128]{3,2,1,0:T(8,128)(2,1)S(1)}, u32[]{:S(2)}, u32[]{:S(2)}) async-start(bf16[4,4,56,128]{3,2,1,0:T(8,128)(2,1)} %near_sums.1), calls=%async_computation.2 | async-start | bytes 458752 | tf_op jit(solution)/shard_map/all_to_all | solution.py:33
  45.4 0.1 convert_subtract_fusion
  45.5 5.0 %all_gather.40 = f32[2,28,128]{2,1,0:T(8,128)S(1)} all-gather(f32[1,28,128]{2,1,0:T(8,128)S(1)} %convert_subtract_fusion), channel_id=1, replica_groups={{0,1},{2,3},{4,5},{6,7},{8,9},{10,11},{12,13},{14,15},{16,17},{18,19},{..., dimensions={0}, use_global_device_ids=true | all-gather | bytes 43008 | tf_op jit(solution)/shard_map/all_gather | solution.py:183
  50.5 0.1 fusion.1
  50.6 0.1 maximum_select_fusion.refs_1_
  50.7 1.9 %all-gather.2 = bf16[128,512]{1,0:T(8,128)(2,1)S(1)} all-gather(bf16[64,512]{1,0:T(8,128)(2,1)S(1)} %kept_codes.1.refs_0_), channel_id=4, replica_groups={{0,1},{2,3},{4,5},{6,7},{8,9},{10,11},{12,13},{14,15},{16,17},{18,19},{..., dimensions={0}, use_global_device_ids=true | all-gather | bytes 196608 | tf_op jit(solution)/shard_map/all_gather | solution.py:183
  52.6 5.3 %all-to-all-done.2.refs_0_ = bf16[4,4,56,128]{3,2,1,0:T(8,128)(2,1)S(1)} async-done(((bf16[4,4,56,128]{3,2,1,0:T(8,128)(2,1)}), bf16[4,4,56,128]{3,2,1,0:T(8,128)(2,1)S(1)}, u32[]{:S(2)}, u32[]{:S(2)}) %all-to-all-start.2) | async-done | bytes 229408 | tf_op jit(solution)/shard_map/all_to_all | solution.py:33
  57.8 0.9 %suffixes.1 = bf16[16,64,128]{2,1,0:T(8,128)(2,1)} custom-call(s32[1]{0:T(128)} %bitcast.1.scalar_ref, bf16[4,4,56,128]{3,2,1,0:T(8,128)(2,1)S(1)} %all-to-all-done.2.refs_0_, f32[56,128]{1,0:T(8,128)S(1)} %maximum_select_fusion.refs_1_), custom_call_target="tpu_custom_call" | custom-call | tf_op jit(solution)/shard_map/suffixes/pallas_call | solution.py:69
  58.8 5.9 %all-to-all-start.3 = ((bf16[16,64,128]{2,1,0:T(8,128)(2,1)}), bf16[16,64,128]{2,1,0:T(8,128)(2,1)S(1)}, u32[]{:S(2)}, u32[]{:S(2)}) async-start(bf16[16,64,128]{2,1,0:T(8,128)(2,1)} %suffixes.1), calls=%async_computation.3 | async-start | bytes 524288 | tf_op jit(solution)/shard_map/all_to_all | solution.py:33
  64.7 8.0 %all-to-all-done.3.refs_0_ = bf16[16,64,128]{2,1,0:T(8,128)(2,1)S(1)} async-done(((bf16[16,64,128]{2,1,0:T(8,128)(2,1)}), bf16[16,64,128]{2,1,0:T(8,128)(2,1)S(1)}, u32[]{:S(2)}, u32[]{:S(2)}) %all-to-all-start.3) | async-done | bytes 262176 | tf_op jit(solution)/shard_map/all_to_all | solution.py:33
  72.7 1.0 %back.1 = bf16[4,64,512]{2,1,0:T(8,128)(2,1)} custom-call(s32[1]{0:T(128)} %bitcast.3.scalar_ref, bf16[16,64,128]{2,1,0:T(8,128)(2,1)S(1)} %all-to-all-done.3.refs_0_, bf16[2,448,512]{2,1,0:T(8,128)(2,1)S(1)} %bitcast.17), custom_call_target="tpu_custom_call" | custom-call | tf_op jit(solution)/shard_map/back/pallas_call | solution.py:69
  73.7 6.3 %all-to-all-start.4 = ((bf16[4,64,512]{2,1,0:T(8,128)(2,1)}), bf16[4,64,512]{2,1,0:T(8,128)(2,1)S(1)}, u32[]{:S(2)}, u32[]{:S(2)}) async-start(bf16[4,64,512]{2,1,0:T(8,128)(2,1)} %back.1), calls=%async_computation.4 | async-start | bytes 524288 | tf_op jit(solution)/shard_map/all_to_all | solution.py:33
  80.0 0.1 pad_add_fusion.scalar_ref
  80.1 5.7 %all-gather.4 = bf16[32,64,128]{2,1,0:T(8,128)(2,1)S(1)} all-gather(bf16[16,64,128]{2,1,0:T(8,128)(2,1)S(1)} %all-to-all-done.3.refs_0_), channel_id=6, replica_groups={{0,1},{2,3},{4,5},{6,7},{8,9},{10,11},{12,13},{14,15},{16,17},{18,19},{..., dimensions={0}, use_global_device_ids=true | all-gather | bytes 786432 | tf_op jit(solution)/shard_map/all_gather | solution.py:183
  85.7 0.1 convert_reduce_fusion
  85.9 0.7 reshape.35
  86.5 1.7 %decoder_grads.1 = bf16[448,512]{1,0:T(8,128)(2,1)} custom-call(s32[2]{0:T(128)S(1)} %pad_add_fusion.scalar_ref, bf16[2,16,64,128]{3,2,1,0:T(8,128)(2,1)S(1)} %bitcast.19, bf16[2,64,512]{2,1,0:T(8,128)(2,1)S(1)} %bitcast.25), custom_call_target="tpu_custom_call" | custom-call | tf_op jit(solution)/shard_map/decoder_grads/pallas_call | solution.py:69
  88.2 0.0 all-to-all-done.4.refs_0_
  88.2 0.1 kept_grads.1
  88.3 3.8 %all-gather.3 = bf16[128,512]{1,0:T(8,128)(2,1)S(1)} all-gather(bf16[64,512]{1,0:T(8,128)(2,1)S(1)} %kept_grads.1), channel_id=5, replica_groups={{0,1},{2,3},{4,5},{6,7},{8,9},{10,11},{12,13},{14,15},{16,17},{18,19},{..., dimensions={0}, use_global_device_ids=true | all-gather | bytes 196608 | tf_op jit(solution)/shard_map/all_gather | solution.py:183
  92.1 1.0 %encoder_grads.1 = (bf16[448,512]{1,0:T(8,128)(2,1)}, f32[1,512]{1,0:T(1,128)}) custom-call(s32[1]{0:T(128)} %constant.83.clone.1.scalar_ref, bf16[2,64,512]{2,1,0:T(8,128)(2,1)S(1)} %bitcast.24, bf16[448,128]{1,0:T(8,128)(2,1)S(1)} %bitcast.23), custom_call_target="tpu_custom_call" | custom-call | tf_op jit(solution)/shard_map/encoder_grads/pallas_call | solution.py:69
  (4 shorter events, 0.1 us)
Async XLA Ops:
  0.6 0.9 copy-start.1
  1.7 1.0 %copy-start.3 = (bf16[448,512]{1,0:T(8,128)(2,1)S(1)}, bf16[448,512]{1,0:T(8,128)(2,1)}, u32[]{:S(2)}) copy-start(bf16[448,512]{1,0:T(8,128)(2,1)} %refs_1_.3) | copy-start | bytes 1376260
  12.3 5.5 %copy-start.5 = (bf16[512,448]{0,1:T(8,128)(2,1)S(1)}, bf16[512,448]{0,1:T(8,128)(2,1)}, u32[]{:S(2)}) copy-start(bf16[512,448]{0,1:T(8,128)(2,1)} %param.10) | copy-start | bytes 1376260
  12.4 9.6 %all-to-all-start = ((bf16[4,64,512]{2,1,0:T(8,128)(2,1)}), bf16[4,64,512]{2,1,0:T(8,128)(2,1)S(1)}, u32[]{:S(2)}, u32[]{:S(2)}) async-start(bf16[4,64,512]{2,1,0:T(8,128)(2,1)} %pair_sum.1), calls=%async_computation | async-start | bytes 524288 | tf_op jit(solution)/shard_map/all_to_all | solution.py:33
  15.9 0.7 copy-start.7
  17.8 4.2 %copy-start = (s32[128,512]{1,0:T(8,128)S(1)}, s32[128,512]{1,0:T(8,128)}, u32[]{:S(2)}) copy-start(s32[128,512]{1,0:T(8,128)} %refs_1_.5) | copy-start | bytes 786436
  17.8 4.1 %copy-start.4 = (f32[512]{0:T(512)S(1)}, f32[512]{0:T(512)}, u32[]{:S(2)}) copy-start(f32[512]{0:T(512)} %param.9) | copy-start | bytes 6148
  23.2 3.7 %copy-start.2 = (bf16[128,448]{0,1:T(8,128)(2,1)S(1)}, bf16[128,448]{0,1:T(8,128)(2,1)}, u32[]{:S(2)}) copy-start(bf16[128,448]{0,1:T(8,128)(2,1)} %param.7) | copy-start | bytes 344068
  23.2 11.3 %all-to-all-start.1 = ((bf16[16,56,128]{2,1,0:T(8,128)(2,1)}), bf16[16,56,128]{2,1,0:T(8,128)(2,1)S(1)}, u32[]{:S(2)}, u32[]{:S(2)}) async-start(bf16[16,56,128]{2,1,0:T(8,128)(2,1)} %decode.1), calls=%async_computation.1 | async-start | bytes 458752 | tf_op jit(solution)/shard_map/all_to_all | solution.py:33
  26.9 0.7 copy-start.6
  35.2 22.6 %all-to-all-start.2 = ((bf16[4,4,56,128]{3,2,1,0:T(8,128)(2,1)}), bf16[4,4,56,128]{3,2,1,0:T(8,128)(2,1)S(1)}, u32[]{:S(2)}, u32[]{:S(2)}) async-start(bf16[4,4,56,128]{3,2,1,0:T(8,128)(2,1)} %near_sums.1), calls=%async_computation.2 | async-start | bytes 458752 | tf_op jit(solution)/shard_map/all_to_all | solution.py:33
  58.8 13.9 %all-to-all-start.3 = ((bf16[16,64,128]{2,1,0:T(8,128)(2,1)}), bf16[16,64,128]{2,1,0:T(8,128)(2,1)S(1)}, u32[]{:S(2)}, u32[]{:S(2)}) async-start(bf16[16,64,128]{2,1,0:T(8,128)(2,1)} %suffixes.1), calls=%async_computation.3 | async-start | bytes 524288 | tf_op jit(solution)/shard_map/all_to_all | solution.py:33
  73.7 14.5 %all-to-all-start.4 = ((bf16[4,64,512]{2,1,0:T(8,128)(2,1)}), bf16[4,64,512]{2,1,0:T(8,128)(2,1)S(1)}, u32[]{:S(2)}, u32[]{:S(2)}) async-start(bf16[4,64,512]{2,1,0:T(8,128)(2,1)} %back.1), calls=%async_computation.4 | async-start | bytes 524288 | tf_op jit(solution)/shard_map/all_to_all | solution.py:33

commit v6 on v5

--- a/solution.py
+++ b/solution.py
@@ -1,3 +1,5 @@
+import collections
+
 import jax
 import jax.numpy as jnp
 from jax import lax
@@ -29,6 +31,9 @@
 CHIP_GROUPS = [[N_CORE * x + c for x in range(N_X)] for c in range(N_CORE)]
 
 
+Scalars = collections.namedtuple('Scalars', ['core', 'late', 'cut', 'my_slice'], defaults=(None, None, None))
+
+
 def swap(x, axis, groups=None):
     return lax.all_to_all(x, axis, 0, 0, axis_index_groups=groups, tiled=False)
 
@@ -53,11 +58,10 @@
 
 def call(stage, shapes, scalars, *arrays):
     n_in = len(arrays)
-    scalars = scalars or [0]
 
     def kernel(scalar_ref, *refs):
-        values = [scalar_ref[i] for i in range(len(scalars))]
-        outs = stage(*values, *[ref[...] for ref in refs[:n_in]])
+        at = Scalars(*[scalar_ref[i] for i in range(scalars.shape[0])])
+        outs = stage(at, *[ref[...] for ref in refs[:n_in]])
         for ref, out in zip(refs[n_in:], outs, strict=True):
             if isinstance(out, list):
                 for i, one in enumerate(out):
@@ -73,7 +77,7 @@
         out_specs=[vmem] * len(shapes),
         compiler_params=pltpu.CompilerParams(vmem_limit_bytes=32 * 1024 * 1024),
         name=stage.__name__,
-    )(jnp.stack([jnp.asarray(v, jnp.int32) for v in scalars]), *arrays)
+    )(scalars, *arrays)
 
 
 def half_of(core, x):
@@ -87,46 +91,72 @@
     return jnp.concatenate([jnp.where(below, codes, 0.0), jnp.where(below, 0.0, codes)], axis=0).astype(BF)
 
 
-def turned(_, activations):
-    return (activations.astype(F32).T.astype(BF),)
-
-
-def encode(_, activations, encoder):
-    return (dot(activations, encoder, (1, 0)),)
-
-
-def pair_sum(core, parts):
-    return ([(half_of(core, parts[0]) + half_of(core, parts[1])).astype(BF)] * N_X,)
-
-
-def kept_codes(core, pieces, mask, bias):
+def encode_kernel(act_hbm, enc_hbm, out_ref, act, enc, sems):
+    copies = [pltpu.make_async_copy(act_hbm, act, sems.at[0]), pltpu.make_async_copy(enc_hbm, enc, sems.at[1])]
+    for copy in copies:
+        copy.start()
+    for copy in copies:
+        copy.wait()
+    out_ref[...] = dot(act[...], enc[...], (0, 0))
+
+
+def encode(activations, encoder):
+    hbm = pl.BlockSpec(memory_space=pltpu.HBM)
+    return pl.pallas_call(
+        encode_kernel,
+        out_shape=jax.ShapeDtypeStruct((activations.shape[1], encoder.shape[1]), F32),
+        in_specs=[hbm, hbm],
+        out_specs=pl.BlockSpec(memory_space=pltpu.VMEM),
+        scratch_shapes=[
+            pltpu.VMEM(activations.shape, BF),
+            pltpu.VMEM(encoder.shape, BF),
+            pltpu.SemaphoreType.DMA((2,)),
+        ],
+        compiler_params=pltpu.CompilerParams(vmem_limit_bytes=56 * 1024 * 1024),
+        name="encode",
+    )(activations, encoder)
+
+
+def pair_sum(at, parts):
+    return ([(half_of(at.core, parts[0]) + half_of(at.core, parts[1])).astype(BF)] * N_X,)
+
+
+def kept_codes(at, pieces, mask, bias):
     total = jnp.sum(pieces.astype(F32), axis=0) + bias
-    return ((half_of(core, mask).astype(F32) * total).astype(BF),)
-
-
-def kept_grads(core, pieces, mask):
-    return ((half_of(core, mask).astype(F32) * jnp.sum(pieces.astype(F32), axis=0)).astype(BF),)
-
-
-def decode(cut, codes, decoders):
-    codes = split_codes(codes, cut)
+    return ((half_of(at.core, mask).astype(F32) * total).astype(BF),)
+
+
+def kept_grads(at, pieces, mask):
+    return ((half_of(at.core, mask).astype(F32) * jnp.sum(pieces.astype(F32), axis=0)).astype(BF),)
+
+
+def decode(at, codes, decoders):
+    codes = split_codes(codes, at.cut)
     first, second = [dot(decoders[core], codes, (1, 1)) for core in range(N_CORE)]
     return (to_slices(first, second).astype(BF),)
 
 
-def near_sums(core, got):
+def near_sums(_, got):
     tokens = got.shape[-1]
     got = got.astype(F32).reshape(N_Y, NEAR, ROWS, tokens)
     return ([jnp.sum(got, axis=1).astype(BF)] * N_FAR,)
 
 
-def suffixes(late, got, base):
+def own_base(at, activations, bias):
+    base = bias - activations.astype(F32)
+    pieces = [jnp.where(at.my_slice == i, base[PIECE * i : PIECE * (i + 1)], 0.0) for i in range(SLICES)]
+    return (sum(pieces),)
+
+
+def suffixes(at, got, bases):
     got = got.astype(F32)
+    base = jnp.concatenate([bases[0], bases[1]], axis=0)
     half = base.shape[1] // 2
 
     def other_half(x):
         return pltpu.roll(x, half, 1)
 
+    base = jnp.where(at.core == 0, other_half(base), base)
     run = base
     errors = []
     for y in range(N_Y):
@@ -150,27 +180,29 @@
     tags = jnp.where(tag_row == 0, token_high, jnp.where(tag_row == 1, token_row - token_high, 0.0))
     out = []
     for y in range(N_Y):
-        own = jnp.where(late == 1, suffix[2 * y + 1], suffix[2 * y])
-        previous = jnp.where(late == 1, suffix[2 * y], suffix[max(2 * y - 1, 0)])
+        own = jnp.where(at.late == 1, suffix[2 * y + 1], suffix[2 * y])
+        previous = jnp.where(at.late == 1, suffix[2 * y], suffix[max(2 * y - 1, 0)])
         pair = jnp.where(lane < half, other_half(previous), own)
         out += [jnp.concatenate([pair, tags], axis=0).astype(BF)] * NEAR
     return (out,)
 
 
-def back(cut, got, decoders):
+def back(at, got, decoders):
     parts = [dot(from_slices(got, core).astype(BF), decoders[core], (0, 0)) for core in range(N_CORE)]
     total = parts[0] + parts[1]
     half = total.shape[0] // 2
-    below = lax.broadcasted_iota(jnp.int32, (half, total.shape[1]), 1) < cut
+    below = lax.broadcasted_iota(jnp.int32, (half, total.shape[1]), 1) < at.cut
     return ([jnp.where(below, total[:half], total[half:]).astype(BF)] * N_X,)
 
 
-def decoder_grads(core, cut, got, codes):
-    total = 0.0
+def decoder_grads(at, got, codes):
+    total, tags = 0.0, 0.0
     for half in range(N_CORE):
-        suffix = jnp.where(core == 0, from_slices(got[half], 0), from_slices(got[half], 1))
-        total = total + dot(suffix.astype(BF), split_codes(codes[half], cut), (1, 0))
-    return (total.astype(BF),)
+        suffix = jnp.where(at.core == 0, from_slices(got[half], 0), from_slices(got[half], 1))
+        total = total + dot(suffix.astype(BF), split_codes(codes[half], at.cut), (1, 0))
+        tags = tags + jnp.sum(got[half, :, ROWS:].astype(F32), axis=1)
+    tags = jnp.where(at.core == 0, tags, pltpu.roll(tags, tags.shape[1] - PIECE, 1))
+    return total.astype(BF), tags
 
 
 def encoder_grads(_, grads, activations):
@@ -196,42 +228,40 @@
     half = (tokens // N_CORE, latents)
     half_low = [(half, BF)]
     many = [((N_X,) + half, BF)]
+    rows_act = activations.T
+
+    (total,) = call(pair_sum, many, core.reshape(1), both_cores(encode(rows_act, encoder)))
+    decoder_rows, boundaries, total = lax.optimization_barrier((decoder.T, boundaries, total))
 
     has_cut = (place % span == 0) & (group > 0)
     cut = jnp.where(has_cut, boundaries[jnp.maximum(group - 1, 0)] - place * latents, 0)
-    rows_act = activations.T
-
-    (turned_act,) = call(turned, [((tokens, width), BF)], [], rows_act)
-    (enc_part,) = call(encode, [((tokens, latents), F32)], [], turned_act, encoder)
-    (total,) = call(pair_sum, many, [core], both_cores(enc_part))
-    decoder_rows, total = lax.optimization_barrier((decoder.T, total))
+    at = jnp.stack(Scalars(core, late.astype(jnp.int32), cut, my_slice))
+
     pieces = swap(total, "wid", CHIP_GROUPS)
     decoders = both_cores(decoder_rows)
-    (my_codes,) = call(kept_codes, half_low, [core], pieces, kept_mask, encoder_bias[None])
-
-    target = lax.dynamic_index_in_dim(rows_act.reshape(SLICES, PIECE, tokens), my_slice, 0, False).astype(F32)
-    base = lax.dynamic_index_in_dim(decoder_bias.reshape(SLICES, PIECE, 1), my_slice, 0, False) - target
-    base = both_cores(base).reshape(ROWS, tokens)
-    base = jnp.where(core == 0, jnp.roll(base, half[0], axis=1), base)
-
-    (got,) = call(decode, [((SLICES, ROWS, tokens), BF)], [cut], my_codes, decoders)
+    (my_codes,) = call(kept_codes, half_low, at, pieces, kept_mask, encoder_bias[None])
+
+    (got,) = call(decode, [((SLICES, ROWS, tokens), BF)], at, my_codes, decoders)
     got = swap(got, "lat", NEAR_GROUPS)
-    (got,) = call(near_sums, [((N_FAR, N_Y, ROWS, tokens), BF)], [core], got)
+    (got,) = call(near_sums, [((N_FAR, N_Y, ROWS, tokens), BF)], at, got)
+    later_act, later_bias, later_codes, got = lax.optimization_barrier((rows_act, decoder_bias, my_codes, got))
     got = swap(got, "lat", FAR_GROUPS)
-    got, codes = lax.optimization_barrier((got, both_cores(my_codes)))
-    (got,) = call(suffixes, [((SLICES, ROWS + TAG_ROWS, tokens), BF)], [late], got, base)
+    (base,) = call(own_base, [((PIECE, tokens), F32)], at, later_act, later_bias[:, None])
+    base, codes = both_cores(base), both_cores(later_codes)
+    got, base, codes = lax.optimization_barrier((got, base, codes))
+    (got,) = call(suffixes, [((SLICES, ROWS + TAG_ROWS, tokens), BF)], at, got, base)
     got = swap(got, "lat", NEAR_GROUPS)
 
-    (total,) = call(back, many, [cut], got, decoders)
+    (total,) = call(back, many, at, got, decoders)
     got, total = lax.optimization_barrier((got, total))
     pieces = swap(total, "wid", CHIP_GROUPS)
-    got = both_cores(got)
-    (decoder_grad,) = call(decoder_grads, [((width, latents), BF)], [core, cut], got, codes)
-    tags = lax.dynamic_slice_in_dim(got[:, :, ROWS : ROWS + 2], core * PIECE, PIECE, 3)
-    decoder_bias_grad = jnp.sum(tags.astype(F32), axis=(0, 2)).reshape(width)
-    (my_grads,) = call(kept_grads, half_low, [core], pieces, kept_mask)
+    decoder_grad, tags = call(
+        decoder_grads, [((width, latents), BF), ((SLICES, tokens), F32)], at, both_cores(got), codes
+    )
+    decoder_bias_grad = tags[:, :PIECE].reshape(width)
+    (my_grads,) = call(kept_grads, half_low, at, pieces, kept_mask)
     encoder_grad, encoder_bias_grad = call(
-        encoder_grads, [((width, latents), BF), ((1, latents), F32)], [], both_cores(my_grads), rows_act
+        encoder_grads, [((width, latents), BF), ((1, latents), F32)], at, both_cores(my_grads), rows_act
     )
     return (encoder_grad, encoder_bias_grad.reshape(latents), decoder_grad.T, decoder_bias_grad)
 

time: 93.9 us -> 96.1 us (1.023)
  blocking collectives: 27.7 us -> 52.4 us
  waiting for transfers between devices: 21.5 us -> 5.33 us
  starting transfers between devices: 29.6 us -> 20.9 us
  Pallas kernels: 7.71 us -> 12.5 us
  local copies, waits for them, and re-layouts: 4.72 us -> 2.8 us
    all_to_all x0 -> x2, blocking collectives: none -> 24.6 us  [swap(): return lax.all_to_all(x, axis, 0, 0, axis_index_groups=groups, tiled=False)]
    all_to_all x5 -> x3, waiting for transfers between devices: 21.5 us -> 5.33 us  [swap(): return lax.all_to_all(x, axis, 0, 0, axis_index_groups=groups, tiled=False)]
    all_to_all x5 -> x3, starting transfers between devices: 29.6 us -> 20.9 us  [swap(): return lax.all_to_all(x, axis, 0, 0, axis_index_groups=groups, tiled=False)]
    pallas_call x11 -> x10, Pallas kernels: 7.71 us -> 10.4 us  [call(): pl.pallas_call(kernel, out_shape=[jax.ShapeDtypeStruct(shape, dtype) for...]
    pallas_call x0 -> x1, Pallas kernels: none -> 2.05 us  [encode(): pl.pallas_call(encode_kernel, out_shape=jax.ShapeDtypeStruct((activations...]
    unnamed x16 -> x12, local copies, waits for them, and re-layouts: 3.25 us -> 1.42 us
  transfers between devices with their start and end apart: 5 -> 3, of which waited for: 4 -> 2; matrix products, arithmetic and copies ran while one was open for 2% -> 2% of each run, Pallas kernels for 2% -> 2%
where the time goes in v6:
time: 96.1 us; the launch traced here: 95.5 us
  blocking collectives  52.4 us (55%)
  starting transfers between devices  20.9 us (22%)
  Pallas kernels  12.5 us (13%)
  waiting for transfers between devices  5.33 us (6%)
  local copies, waits for them, and re-layouts  2.8 us (3%)
  between operations  1.47 us (2%)
    all_gather x6, blocking collectives, both_cores(): return lax.all_gather(x, 'wid', axis_index_groups=CORE_GROUPS)  27.8 us
    all_to_all x2, blocking collectives, swap(): return lax.all_to_all(x, axis, 0, 0, axis_index_groups=groups, tiled=False)  24.6 us
    all_to_all x3, starting transfers between devices, swap(): return lax.all_to_all(x, axis, 0, 0, axis_index_groups=groups, tiled=False)  20.9 us
    pallas_call x10, Pallas kernels, call(): pl.pallas_call(kernel, out_shape=[jax.ShapeDtypeStruct(shape, dtype) for...  10.4 us
    all_to_all x3, waiting for transfers between devices, swap(): return lax.all_to_all(x, axis, 0, 0, axis_index_groups=groups, tiled=False)  5.33 us
    pallas_call x1, Pallas kernels, encode(): pl.pallas_call(encode_kernel, out_shape=jax.ShapeDtypeStruct((activations...  2.05 us
  transfers between devices with their start and end apart: 3, of which 2 were waited for; matrix products, arithmetic and copies ran while one was open for 2% of the time, Pallas kernels for 2%

profile of v6, /device:TPU:1, one launch (start us, length us, event | category | flops | bytes accessed | tf_op | source)
XLA Modules:
  0.0 95.5 jit_solution(1864880991206780830)
XLA Ops:
  0.6 2.1 %encode.1 = f32[128,512]{1,0:T(8,128)} custom-call(bf16[448,128]{1,0:T(8,128)(2,1)} %bitcast.22, bf16[448,512]{1,0:T(8,128)(2,1)} %enc_hbm.1), custom_call_target="tpu_custom_call" | custom-call | tf_op jit(solution)/shard_map/encode/pallas_call | solution.py:105
  2.7 8.9 %all-gather = f32[256,512]{1,0:T(8,128)S(1)} all-gather(f32[128,512]{1,0:T(8,128)} %encode.1), channel_id=2, replica_groups={{0,1},{2,3},{4,5},{6,7},{8,9},{10,11},{12,13},{14,15},{16,17},{18,19},{..., dimensions={0}, use_global_device_ids=true | all-gather | bytes 786432 | tf_op jit(solution)/shard_map/all_gather | solution.py:215
  11.6 0.7 pair_sum.1
  12.3 0.0 copy-start.3
  12.3 3.5 %all-to-all-start = ((bf16[4,64,512]{2,1,0:T(8,128)(2,1)}), bf16[4,64,512]{2,1,0:T(8,128)(2,1)S(1)}, u32[]{:S(2)}, u32[]{:S(2)}) async-start(bf16[4,64,512]{2,1,0:T(8,128)(2,1)} %pair_sum.1), calls=%async_computation | async-start | bytes 524288 | tf_op jit(solution)/shard_map/all_to_all | solution.py:38
  16.0 0.0 copy-start.5
  16.0 0.6 copy-done.5
  16.6 0.6 dynamic_slice.3
  17.9 0.1 pad_add_fusion.scalar_ref
  18.0 0.0 copy-done.3
  18.0 0.0 copy-start
  18.0 0.0 copy-start.2
  18.0 2.6 %all-gather.1 = bf16[896,512]{1,0:T(8,128)(2,1)S(1)} all-gather(bf16[448,512]{1,0:T(8,128)(2,1)S(1)} %bitcast.30), channel_id=3, replica_groups={{0,1},{2,3},{4,5},{6,7},{8,9},{10,11},{12,13},{14,15},{16,17},{18,19},{..., dimensions={0}, use_global_device_ids=true | all-gather | bytes 1376256 | tf_op jit(solution)/shard_map/all_gather | solution.py:215
  20.6 1.4 %all-to-all-done.refs_0_ = bf16[4,64,512]{2,1,0:T(8,128)(2,1)S(1)} async-done(((bf16[4,64,512]{2,1,0:T(8,128)(2,1)}), bf16[4,64,512]{2,1,0:T(8,128)(2,1)S(1)}, u32[]{:S(2)}, u32[]{:S(2)}) %all-to-all-start) | async-done | bytes 262176 | tf_op jit(solution)/shard_map/all_to_all | solution.py:38
  22.0 0.0 copy-done
  22.0 0.0 copy-done.2
  22.0 0.6 kept_codes.1.refs_0_
  22.6 0.9 decode.1
  23.5 10.9 %all_to_all.25.refs_0_ = bf16[16,56,128]{2,1,0:T(8,128)(2,1)S(1)} all-to-all(bf16[16,56,128]{2,1,0:T(8,128)(2,1)S(1)} %decode.1), channel_id=1, replica_groups={{0,8,16,24,128,136,144,152,256,264,272,280,384,392,400,408},{32,40,48,5..., dimensions={0} | all-to-all | bytes 458752 | tf_op jit(solution)/shard_map/all_to_all | solution.py:38
  34.4 1.3 %near_sums.1 = bf16[4,4,56,128]{3,2,1,0:T(8,128)(2,1)} custom-call(s32[4]{0:T(128)S(1)} %pad_add_fusion.scalar_ref, bf16[16,56,128]{2,1,0:T(8,128)(2,1)S(1)} %all_to_all.25.refs_0_), custom_call_target="tpu_custom_call" | custom-call | tf_op jit(solution)/shard_map/near_sums/pallas_call | solution.py:73
  35.7 0.0 copy-start.4
  35.7 10.5 %all-to-all-start.2 = ((bf16[4,4,56,128]{3,2,1,0:T(8,128)(2,1)}), bf16[4,4,56,128]{3,2,1,0:T(8,128)(2,1)S(1)}, u32[]{:S(2)}, u32[]{:S(2)}) async-start(bf16[4,4,56,128]{3,2,1,0:T(8,128)(2,1)} %near_sums.1), calls=%async_computation.2 | async-start | bytes 458752 | tf_op jit(solution)/shard_map/all_to_all | solution.py:38
  46.1 0.0 copy-done.4
  46.1 0.0 copy-start.1
  46.1 0.1 copy.12.refs_1_
  46.3 0.8 copy-done.1
  47.0 0.7 own_base.1
  47.7 5.0 %all-gather.6.refs_1_ = f32[2,28,128]{2,1,0:T(8,128)S(1)} all-gather(f32[1,28,128]{2,1,0:T(8,128)S(1)} %bitcast.27), channel_id=4, replica_groups={{0,1},{2,3},{4,5},{6,7},{8,9},{10,11},{12,13},{14,15},{16,17},{18,19},{..., dimensions={0}, use_global_device_ids=true | all-gather | bytes 43008 | tf_op jit(solution)/shard_map/all_gather | solution.py:215
  52.7 1.9 %all-gather.3 = bf16[128,512]{1,0:T(8,128)(2,1)S(1)} all-gather(bf16[64,512]{1,0:T(8,128)(2,1)S(1)} %kept_codes.1.refs_0_), channel_id=5, replica_groups={{0,1},{2,3},{4,5},{6,7},{8,9},{10,11},{12,13},{14,15},{16,17},{18,19},{..., dimensions={0}, use_global_device_ids=true | all-gather | bytes 196608 | tf_op jit(solution)/shard_map/all_gather | solution.py:215
  54.6 3.9 %all-to-all-done.2.refs_0_ = bf16[4,4,56,128]{3,2,1,0:T(8,128)(2,1)S(1)} async-done(((bf16[4,4,56,128]{3,2,1,0:T(8,128)(2,1)}), bf16[4,4,56,128]{3,2,1,0:T(8,128)(2,1)S(1)}, u32[]{:S(2)}, u32[]{:S(2)}) %all-to-all-start.2) | async-done | bytes 229408 | tf_op jit(solution)/shard_map/all_to_all | solution.py:38
  58.5 0.8 suffixes.1
  59.3 13.7 %all_to_all.26.refs_0_ = bf16[16,64,128]{2,1,0:T(8,128)(2,1)S(1)} all-to-all(bf16[16,64,128]{2,1,0:T(8,128)(2,1)S(1)} %suffixes.1), channel_id=1, replica_groups={{0,8,16,24,128,136,144,152,256,264,272,280,384,392,400,408},{32,40,48,5..., dimensions={0} | all-to-all | bytes 524288 | tf_op jit(solution)/shard_map/all_to_all | solution.py:38
  73.0 1.6 %back.1 = bf16[4,64,512]{2,1,0:T(8,128)(2,1)} custom-call(s32[4]{0:T(128)S(1)} %pad_add_fusion.scalar_ref, bf16[16,64,128]{2,1,0:T(8,128)(2,1)S(1)} %all_to_all.26.refs_0_, bf16[2,448,512]{2,1,0:T(8,128)(2,1)S(1)} %bitcast.19), custom_call_target="tpu_custom_call" | custom-call | tf_op jit(solution)/shard_map/back/pallas_call | solution.py:73
  74.6 6.9 %all-to-all-start.4 = ((bf16[4,64,512]{2,1,0:T(8,128)(2,1)}), bf16[4,64,512]{2,1,0:T(8,128)(2,1)S(1)}, u32[]{:S(2)}, u32[]{:S(2)}) async-start(bf16[4,64,512]{2,1,0:T(8,128)(2,1)} %back.1), calls=%async_computation.4 | async-start | bytes 524288 | tf_op jit(solution)/shard_map/all_to_all | solution.py:38
  81.5 5.4 %all-gather.5 = bf16[32,64,128]{2,1,0:T(8,128)(2,1)S(1)} all-gather(bf16[16,64,128]{2,1,0:T(8,128)(2,1)S(1)} %all_to_all.26.refs_0_), channel_id=7, replica_groups={{0,1},{2,3},{4,5},{6,7},{8,9},{10,11},{12,13},{14,15},{16,17},{18,19},{..., dimensions={0}, use_global_device_ids=true | all-gather | bytes 786432 | tf_op jit(solution)/shard_map/all_gather | solution.py:215
  86.9 1.7 %decoder_grads.1 = (bf16[448,512]{1,0:T(8,128)(2,1)}, f32[16,128]{1,0:T(8,128)S(1)}) custom-call(s32[4]{0:T(128)S(1)} %pad_add_fusion.scalar_ref, bf16[2,16,64,128]{3,2,1,0:T(8,128)(2,1)S(1)} %bitcast.21, bf16[2,64,512]{2,1,0:T(8,128)(2,1)S(1)} %bitcast.26), custom_call_target="tpu_custom_call" | custom-call | tf_op jit(solution)/shard_map/decoder_grads/pallas_call | solution.py:73
  88.6 0.7 reshape.16
  89.3 0.0 all-to-all-done.4.refs_0_
  89.3 0.6 kept_grads.1
  89.9 4.1 %all-gather.4 = bf16[128,512]{1,0:T(8,128)(2,1)S(1)} all-gather(bf16[64,512]{1,0:T(8,128)(2,1)S(1)} %kept_grads.1), channel_id=6, replica_groups={{0,1},{2,3},{4,5},{6,7},{8,9},{10,11},{12,13},{14,15},{16,17},{18,19},{..., dimensions={0}, use_global_device_ids=true | all-gather | bytes 196608 | tf_op jit(solution)/shard_map/all_gather | solution.py:215
  93.9 1.6 %encoder_grads.1 = (bf16[448,512]{1,0:T(8,128)(2,1)}, f32[1,512]{1,0:T(1,128)}) custom-call(s32[4]{0:T(128)S(1)} %pad_add_fusion.scalar_ref, bf16[2,64,512]{2,1,0:T(8,128)(2,1)S(1)} %bitcast.25, bf16[448,128]{1,0:T(8,128)(2,1)S(1)} %bitcast.24), custom_call_target="tpu_custom_call" | custom-call | tf_op jit(solution)/shard_map/encoder_grads/pallas_call | solution.py:73
Async XLA Ops:
  12.3 5.6 %copy-start.3 = (bf16[512,448]{0,1:T(8,128)(2,1)S(1)}, bf16[512,448]{0,1:T(8,128)(2,1)}, u32[]{:S(2)}) copy-start(bf16[512,448]{0,1:T(8,128)(2,1)} %param.10) | copy-start | bytes 1376260
  12.3 9.6 %all-to-all-start = ((bf16[4,64,512]{2,1,0:T(8,128)(2,1)}), bf16[4,64,512]{2,1,0:T(8,128)(2,1)S(1)}, u32[]{:S(2)}, u32[]{:S(2)}) async-start(bf16[4,64,512]{2,1,0:T(8,128)(2,1)} %pair_sum.1), calls=%async_computation | async-start | bytes 524288 | tf_op jit(solution)/shard_map/all_to_all | solution.py:38
  16.0 0.7 copy-start.5
  18.0 4.0 %copy-start = (s32[128,512]{1,0:T(8,128)S(1)}, s32[128,512]{1,0:T(8,128)}, u32[]{:S(2)}) copy-start(s32[128,512]{1,0:T(8,128)} %refs_1_.3) | copy-start | bytes 786436
  18.0 4.0 %copy-start.2 = (f32[512]{0:T(512)S(1)}, f32[512]{0:T(512)}, u32[]{:S(2)}) copy-start(f32[512]{0:T(512)} %param.9) | copy-start | bytes 6148
  35.7 10.5 %copy-start.4 = (f32[448]{0:T(512)S(1)}, f32[448]{0:T(512)}, u32[]{:S(2)}) copy-start(f32[448]{0:T(512)} %param.11) | copy-start | bytes 5380
  35.7 22.9 %all-to-all-start.2 = ((bf16[4,4,56,128]{3,2,1,0:T(8,128)(2,1)}), bf16[4,4,56,128]{3,2,1,0:T(8,128)(2,1)S(1)}, u32[]{:S(2)}, u32[]{:S(2)}) async-start(bf16[4,4,56,128]{3,2,1,0:T(8,128)(2,1)} %near_sums.1), calls=%async_computation.2 | async-start | bytes 458752 | tf_op jit(solution)/shard_map/all_to_all | solution.py:38
  46.1 0.9 copy-start.1
  74.6 14.7 %all-to-all-start.4 = ((bf16[4,64,512]{2,1,0:T(8,128)(2,1)}), bf16[4,64,512]{2,1,0:T(8,128)(2,1)S(1)}, u32[]{:S(2)}, u32[]{:S(2)}) async-start(bf16[4,64,512]{2,1,0:T(8,128)(2,1)} %back.1), calls=%async_computation.4 | async-start | bytes 524288 | tf_op jit(solution)/shard_map/all_to_all | solution.py:38

commit v7 on v6

--- a/solution.py
+++ b/solution.py
@@ -31,7 +31,7 @@
 CHIP_GROUPS = [[N_CORE * x + c for x in range(N_X)] for c in range(N_CORE)]
 
 
-Scalars = collections.namedtuple('Scalars', ['core', 'late', 'cut', 'my_slice'], defaults=(None, None, None))
+Scalars = collections.namedtuple('Scalars', ['core', 'late', 'cut', 'my_slice'], defaults=(None,) * 4)
 
 
 def swap(x, axis, groups=None):
@@ -57,12 +57,13 @@
 
 
 def call(stage, shapes, scalars, *arrays):
-    n_in = len(arrays)
-
-    def kernel(scalar_ref, *refs):
-        at = Scalars(*[scalar_ref[i] for i in range(scalars.shape[0])])
-        outs = stage(at, *[ref[...] for ref in refs[:n_in]])
-        for ref, out in zip(refs[n_in:], outs, strict=True):
+    names = list(scalars)
+    n_out = len(shapes)
+
+    def kernel(*refs):
+        at = Scalars(**{name: ref[0] for name, ref in zip(names, refs)})
+        outs = stage(at, *[ref[...] for ref in refs[len(names) : -n_out]])
+        for ref, out in zip(refs[-n_out:], outs, strict=True):
             if isinstance(out, list):
                 for i, one in enumerate(out):
                     ref[i] = one
@@ -73,11 +74,11 @@
     return pl.pallas_call(
         kernel,
         out_shape=[jax.ShapeDtypeStruct(shape, dtype) for shape, dtype in shapes],
-        in_specs=[pl.BlockSpec(memory_space=pltpu.SMEM)] + [vmem] * n_in,
-        out_specs=[vmem] * len(shapes),
+        in_specs=[pl.BlockSpec(memory_space=pltpu.SMEM)] * len(names) + [vmem] * len(arrays),
+        out_specs=[vmem] * n_out,
         compiler_params=pltpu.CompilerParams(vmem_limit_bytes=32 * 1024 * 1024),
         name=stage.__name__,
-    )(scalars, *arrays)
+    )(*[scalars[name].reshape(1) for name in names], *arrays)
 
 
 def half_of(core, x):
@@ -91,30 +92,8 @@
     return jnp.concatenate([jnp.where(below, codes, 0.0), jnp.where(below, 0.0, codes)], axis=0).astype(BF)
 
 
-def encode_kernel(act_hbm, enc_hbm, out_ref, act, enc, sems):
-    copies = [pltpu.make_async_copy(act_hbm, act, sems.at[0]), pltpu.make_async_copy(enc_hbm, enc, sems.at[1])]
-    for copy in copies:
-        copy.start()
-    for copy in copies:
-        copy.wait()
-    out_ref[...] = dot(act[...], enc[...], (0, 0))
-
-
-def encode(activations, encoder):
-    hbm = pl.BlockSpec(memory_space=pltpu.HBM)
-    return pl.pallas_call(
-        encode_kernel,
-        out_shape=jax.ShapeDtypeStruct((activations.shape[1], encoder.shape[1]), F32),
-        in_specs=[hbm, hbm],
-        out_specs=pl.BlockSpec(memory_space=pltpu.VMEM),
-        scratch_shapes=[
-            pltpu.VMEM(activations.shape, BF),
-            pltpu.VMEM(encoder.shape, BF),
-            pltpu.SemaphoreType.DMA((2,)),
-        ],
-        compiler_params=pltpu.CompilerParams(vmem_limit_bytes=56 * 1024 * 1024),
-        name="encode",
-    )(activations, encoder)
+def encode(_, activations, encoder):
+    return (dot(activations, encoder, (0, 0)),)
 
 
 def pair_sum(at, parts):
@@ -230,38 +209,41 @@
     many = [((N_X,) + half, BF)]
     rows_act = activations.T
 
-    (total,) = call(pair_sum, many, core.reshape(1), both_cores(encode(rows_act, encoder)))
+    on_core = {'core': core}
+    (enc_part,) = call(encode, [((tokens, latents), F32)], {}, rows_act, encoder)
+    (total,) = call(pair_sum, many, on_core, both_cores(enc_part))
     decoder_rows, boundaries, total = lax.optimization_barrier((decoder.T, boundaries, total))
 
     has_cut = (place % span == 0) & (group > 0)
     cut = jnp.where(has_cut, boundaries[jnp.maximum(group - 1, 0)] - place * latents, 0)
-    at = jnp.stack(Scalars(core, late.astype(jnp.int32), cut, my_slice))
+    late = late.astype(jnp.int32)
+    at_cut = {'cut': cut}
 
     pieces = swap(total, "wid", CHIP_GROUPS)
     decoders = both_cores(decoder_rows)
-    (my_codes,) = call(kept_codes, half_low, at, pieces, kept_mask, encoder_bias[None])
-
-    (got,) = call(decode, [((SLICES, ROWS, tokens), BF)], at, my_codes, decoders)
+    (my_codes,) = call(kept_codes, half_low, on_core, pieces, kept_mask, encoder_bias[None])
+
+    (got,) = call(decode, [((SLICES, ROWS, tokens), BF)], at_cut, my_codes, decoders)
     got = swap(got, "lat", NEAR_GROUPS)
-    (got,) = call(near_sums, [((N_FAR, N_Y, ROWS, tokens), BF)], at, got)
+    (got,) = call(near_sums, [((N_FAR, N_Y, ROWS, tokens), BF)], {}, got)
     later_act, later_bias, later_codes, got = lax.optimization_barrier((rows_act, decoder_bias, my_codes, got))
     got = swap(got, "lat", FAR_GROUPS)
-    (base,) = call(own_base, [((PIECE, tokens), F32)], at, later_act, later_bias[:, None])
+    (base,) = call(own_base, [((PIECE, tokens), F32)], {'my_slice': my_slice}, later_act, later_bias[:, None])
     base, codes = both_cores(base), both_cores(later_codes)
     got, base, codes = lax.optimization_barrier((got, base, codes))
-    (got,) = call(suffixes, [((SLICES, ROWS + TAG_ROWS, tokens), BF)], at, got, base)
+    (got,) = call(suffixes, [((SLICES, ROWS + TAG_ROWS, tokens), BF)], {'core': core, 'late': late}, got, base)
     got = swap(got, "lat", NEAR_GROUPS)
 
-    (total,) = call(back, many, at, got, decoders)
+    (total,) = call(back, many, at_cut, got, decoders)
     got, total = lax.optimization_barrier((got, total))
     pieces = swap(total, "wid", CHIP_GROUPS)
     decoder_grad, tags = call(
-        decoder_grads, [((width, latents), BF), ((SLICES, tokens), F32)], at, both_cores(got), codes
+        decoder_grads, [((width, latents), BF), ((SLICES, tokens), F32)], {'core': core, 'cut': cut}, both_cores(got), codes
     )
     decoder_bias_grad = tags[:, :PIECE].reshape(width)
-    (my_grads,) = call(kept_grads, half_low, at, pieces, kept_mask)
+    (my_grads,) = call(kept_grads, half_low, on_core, pieces, kept_mask)
     encoder_grad, encoder_bias_grad = call(
-        encoder_grads, [((width, latents), BF), ((1, latents), F32)], at, both_cores(my_grads), rows_act
+        encoder_grads, [((width, latents), BF), ((1, latents), F32)], {}, both_cores(my_grads), rows_act
     )
     return (encoder_grad, encoder_bias_grad.reshape(latents), decoder_grad.T, decoder_bias_grad)
 

time: 96.1 us -> 91.7 us (0.954)
  Pallas kernels: 12.5 us -> 5.78 us
  local copies, waits for them, and re-layouts: 2.8 us -> 5.4 us
    pallas_call x10 -> x11, Pallas kernels: 10.4 us -> 5.78 us  [call(): pl.pallas_call(kernel, out_shape=[jax.ShapeDtypeStruct(shape, dtype) for...]
    unnamed x12 -> x16, local copies, waits for them, and re-layouts: 1.42 us -> 4.01 us
    pallas_call x1 -> x0, Pallas kernels: 2.05 us -> none  [encode(): pl.pallas_call(encode_kernel, out_shape=jax.ShapeDtypeStruct((activations...]
  transfers between devices with their start and end apart: 3 -> 3, of which waited for: 2 -> 2; matrix products, arithmetic and copies ran while one was open for 2% -> 2% of each run, Pallas kernels for 2% -> 1%
where the time goes in v7:
time: 91.7 us; the launch traced here: 91.1 us
  blocking collectives  53 us (58%)
  starting transfers between devices  20.1 us (22%)
  Pallas kernels  5.78 us (6%)
  local copies, waits for them, and re-layouts  5.4 us (6%)
  waiting for transfers between devices  5.31 us (6%)
  between operations  1.43 us (2%)
    all_gather x6, blocking collectives, both_cores(): return lax.all_gather(x, 'wid', axis_index_groups=CORE_GROUPS)  28.4 us
    all_to_all x2, blocking collectives, swap(): return lax.all_to_all(x, axis, 0, 0, axis_index_groups=groups, tiled=False)  24.6 us
    all_to_all x3, starting transfers between devices, swap(): return lax.all_to_all(x, axis, 0, 0, axis_index_groups=groups, tiled=False)  20.1 us
    pallas_call x11, Pallas kernels, call(): pl.pallas_call(kernel, out_shape=[jax.ShapeDtypeStruct(shape, dtype) for...  5.78 us
    all_to_all x3, waiting for transfers between devices, swap(): return lax.all_to_all(x, axis, 0, 0, axis_index_groups=groups, tiled=False)  5.31 us
    unnamed x16, local copies, waits for them, and re-layouts  4.01 us
  transfers between devices with their start and end apart: 3, of which 2 were waited for; matrix products, arithmetic and copies ran while one was open for 2% of the time, Pallas kernels for 1%

profile of v7, /device:TPU:1, one launch (start us, length us, event | category | flops | bytes accessed | tf_op | source)
XLA Modules:
  0.0 91.1 jit_solution(617636599069995718)
XLA Ops:
  0.6 0.0 copy-start.1
  0.7 0.9 copy-done.1
  1.5 0.0 copy-start.3
  1.5 1.0 %copy-done.3 = bf16[448,512]{1,0:T(8,128)(2,1)S(1)} copy-done((bf16[448,512]{1,0:T(8,128)(2,1)S(1)}, bf16[448,512]{1,0:T(8,128)(2,1)}, u32[]{:S(2)}) %copy-start.3) | copy-done | bytes 458776
  2.6 0.2 encode.1
  2.8 8.7 %all-gather = f32[256,512]{1,0:T(8,128)S(1)} all-gather(f32[128,512]{1,0:T(8,128)S(1)} %encode.1), channel_id=2, replica_groups={{0,1},{2,3},{4,5},{6,7},{8,9},{10,11},{12,13},{14,15},{16,17},{18,19},{..., dimensions={0}, use_global_device_ids=true | all-gather | bytes 786432 | tf_op jit(solution)/shard_map/all_gather | solution.py:194
  11.5 0.7 pair_sum.1
  12.2 0.0 copy-start.5
  12.2 3.5 %all-to-all-start = ((bf16[4,64,512]{2,1,0:T(8,128)(2,1)}), bf16[4,64,512]{2,1,0:T(8,128)(2,1)S(1)}, u32[]{:S(2)}, u32[]{:S(2)}) async-start(bf16[4,64,512]{2,1,0:T(8,128)(2,1)} %pair_sum.1), calls=%async_computation | async-start | bytes 524288 | tf_op jit(solution)/shard_map/all_to_all | solution.py:38
  15.8 0.0 copy-start.7
  15.8 0.6 copy-done.7
  16.5 0.6 dynamic_slice.3
  17.7 0.0 copy-done.5
  17.7 0.0 copy-start
  17.7 0.0 copy-start.4
  17.7 2.6 %all-gather.1 = bf16[896,512]{1,0:T(8,128)(2,1)S(1)} all-gather(bf16[448,512]{1,0:T(8,128)(2,1)S(1)} %bitcast.30), channel_id=3, replica_groups={{0,1},{2,3},{4,5},{6,7},{8,9},{10,11},{12,13},{14,15},{16,17},{18,19},{..., dimensions={0}, use_global_device_ids=true | all-gather | bytes 1376256 | tf_op jit(solution)/shard_map/all_gather | solution.py:194
  20.3 1.5 %all-to-all-done.refs_1_ = bf16[4,64,512]{2,1,0:T(8,128)(2,1)S(1)} async-done(((bf16[4,64,512]{2,1,0:T(8,128)(2,1)}), bf16[4,64,512]{2,1,0:T(8,128)(2,1)S(1)}, u32[]{:S(2)}, u32[]{:S(2)}) %all-to-all-start) | async-done | bytes 262176 | tf_op jit(solution)/shard_map/all_to_all | solution.py:38
  21.9 0.0 copy-done
  21.9 0.0 copy-done.4
  21.9 0.1 kept_codes.1.refs_1_
  21.9 0.4 decode.1
  22.3 10.9 %all_to_all.25.refs_0_ = bf16[16,56,128]{2,1,0:T(8,128)(2,1)S(1)} all-to-all(bf16[16,56,128]{2,1,0:T(8,128)(2,1)S(1)} %decode.1), channel_id=1, replica_groups={{0,8,16,24,128,136,144,152,256,264,272,280,384,392,400,408},{32,40,48,5..., dimensions={0} | all-to-all | bytes 458752 | tf_op jit(solution)/shard_map/all_to_all | solution.py:38
  33.2 0.7 near_sums.1
  33.9 10.4 %all-to-all-start.2 = ((bf16[4,4,56,128]{3,2,1,0:T(8,128)(2,1)}), bf16[4,4,56,128]{3,2,1,0:T(8,128)(2,1)S(1)}, u32[]{:S(2)}, u32[]{:S(2)}) async-start(bf16[4,4,56,128]{3,2,1,0:T(8,128)(2,1)} %near_sums.1), calls=%async_computation.2 | async-start | bytes 458752 | tf_op jit(solution)/shard_map/all_to_all | solution.py:38
  44.3 0.0 copy-start.6
  44.3 0.7 copy-done.6
  45.0 0.0 copy-start.2
  45.0 0.1 copy.12.refs_2_
  45.1 0.8 copy-done.2
  45.9 0.1 own_base.1
  46.0 5.0 %all-gather.6.refs_3_ = f32[2,28,128]{2,1,0:T(8,128)S(1)} all-gather(f32[1,28,128]{2,1,0:T(8,128)S(1)} %bitcast.27), channel_id=4, replica_groups={{0,1},{2,3},{4,5},{6,7},{8,9},{10,11},{12,13},{14,15},{16,17},{18,19},{..., dimensions={0}, use_global_device_ids=true | all-gather | bytes 43008 | tf_op jit(solution)/shard_map/all_gather | solution.py:194
  51.0 1.9 %all-gather.3 = bf16[128,512]{1,0:T(8,128)(2,1)S(1)} all-gather(bf16[64,512]{1,0:T(8,128)(2,1)S(1)} %kept_codes.1.refs_1_), channel_id=5, replica_groups={{0,1},{2,3},{4,5},{6,7},{8,9},{10,11},{12,13},{14,15},{16,17},{18,19},{..., dimensions={0}, use_global_device_ids=true | all-gather | bytes 196608 | tf_op jit(solution)/shard_map/all_gather | solution.py:194
  52.9 3.8 %all-to-all-done.2.refs_2_ = bf16[4,4,56,128]{3,2,1,0:T(8,128)(2,1)S(1)} async-done(((bf16[4,4,56,128]{3,2,1,0:T(8,128)(2,1)}), bf16[4,4,56,128]{3,2,1,0:T(8,128)(2,1)S(1)}, u32[]{:S(2)}, u32[]{:S(2)}) %all-to-all-start.2) | async-done | bytes 229408 | tf_op jit(solution)/shard_map/all_to_all | solution.py:38
  56.7 0.2 suffixes.1
  56.9 13.7 %all_to_all.26.refs_1_ = bf16[16,64,128]{2,1,0:T(8,128)(2,1)S(1)} all-to-all(bf16[16,64,128]{2,1,0:T(8,128)(2,1)S(1)} %suffixes.1), channel_id=1, replica_groups={{0,8,16,24,128,136,144,152,256,264,272,280,384,392,400,408},{32,40,48,5..., dimensions={0} | all-to-all | bytes 524288 | tf_op jit(solution)/shard_map/all_to_all | solution.py:38
  70.6 1.0 %back.1 = bf16[4,64,512]{2,1,0:T(8,128)(2,1)} custom-call(s32[1]{0:T(128)} %bitcast.7.refs_0_.refs_1_, bf16[16,64,128]{2,1,0:T(8,128)(2,1)S(1)} %all_to_all.26.refs_1_, bf16[2,448,512]{2,1,0:T(8,128)(2,1)S(1)} %bitcast.19), custom_call_target="tpu_custom_call" | custom-call | tf_op jit(solution)/shard_map/back/pallas_call | solution.py:74
  71.7 6.2 %all-to-all-start.4 = ((bf16[4,64,512]{2,1,0:T(8,128)(2,1)}), bf16[4,64,512]{2,1,0:T(8,128)(2,1)S(1)}, u32[]{:S(2)}, u32[]{:S(2)}) async-start(bf16[4,64,512]{2,1,0:T(8,128)(2,1)} %back.1), calls=%async_computation.4 | async-start | bytes 524288 | tf_op jit(solution)/shard_map/all_to_all | solution.py:38
  77.9 5.6 %all-gather.5 = bf16[32,64,128]{2,1,0:T(8,128)(2,1)S(1)} all-gather(bf16[16,64,128]{2,1,0:T(8,128)(2,1)S(1)} %all_to_all.26.refs_1_), channel_id=7, replica_groups={{0,1},{2,3},{4,5},{6,7},{8,9},{10,11},{12,13},{14,15},{16,17},{18,19},{..., dimensions={0}, use_global_device_ids=true | all-gather | bytes 786432 | tf_op jit(solution)/shard_map/all_gather | solution.py:194
  83.6 1.2 %decoder_grads.1 = (bf16[448,512]{1,0:T(8,128)(2,1)}, f32[16,128]{1,0:T(8,128)S(1)}) custom-call(s32[1]{0:T(128)} %bitcast.refs_0_, s32[1]{0:T(128)} %bitcast.7.refs_0_.refs_1_, bf16[2,16,64,128]{3,2,1,0:T(8,128)(2,1)S(1)} %bitcast.20, bf16[2,64,512]{2,1,0:T(8,128)(2,1)S(1)} %bitcast.25), custom_call_target="tpu_custom_call" | custom-call | tf_op jit(solution)/shard_map/decoder_grads/pallas_call | solution.py:74
  84.7 0.7 reshape.40
  85.4 0.0 all-to-all-done.4.refs_1_
  85.4 0.1 kept_grads.1
  85.4 4.6 %all-gather.4 = bf16[128,512]{1,0:T(8,128)(2,1)S(1)} all-gather(bf16[64,512]{1,0:T(8,128)(2,1)S(1)} %kept_grads.1), channel_id=6, replica_groups={{0,1},{2,3},{4,5},{6,7},{8,9},{10,11},{12,13},{14,15},{16,17},{18,19},{..., dimensions={0}, use_global_device_ids=true | all-gather | bytes 196608 | tf_op jit(solution)/shard_map/all_gather | solution.py:194
  90.1 1.0 %encoder_grads.1 = (bf16[448,512]{1,0:T(8,128)(2,1)}, f32[1,512]{1,0:T(1,128)}) custom-call(bf16[2,64,512]{2,1,0:T(8,128)(2,1)S(1)} %bitcast.26, bf16[448,128]{1,0:T(8,128)(2,1)S(1)} %bitcast.24), custom_call_target="tpu_custom_call" | custom-call | tf_op jit(solution)/shard_map/encoder_grads/pallas_call | solution.py:74
Async XLA Ops:
  0.6 0.9 copy-start.1
  1.5 1.0 %copy-start.3 = (bf16[448,512]{1,0:T(8,128)(2,1)S(1)}, bf16[448,512]{1,0:T(8,128)(2,1)}, u32[]{:S(2)}) copy-start(bf16[448,512]{1,0:T(8,128)(2,1)} %refs_1_.1) | copy-start | bytes 1376260
  12.2 5.5 %copy-start.5 = (bf16[512,448]{0,1:T(8,128)(2,1)S(1)}, bf16[512,448]{0,1:T(8,128)(2,1)}, u32[]{:S(2)}) copy-start(bf16[512,448]{0,1:T(8,128)(2,1)} %param.10) | copy-start | bytes 1376260
  12.2 9.6 %all-to-all-start = ((bf16[4,64,512]{2,1,0:T(8,128)(2,1)}), bf16[4,64,512]{2,1,0:T(8,128)(2,1)S(1)}, u32[]{:S(2)}, u32[]{:S(2)}) async-start(bf16[4,64,512]{2,1,0:T(8,128)(2,1)} %pair_sum.1), calls=%async_computation | async-start | bytes 524288 | tf_op jit(solution)/shard_map/all_to_all | solution.py:38
  15.8 0.7 copy-start.7
  17.7 4.2 %copy-start = (s32[128,512]{1,0:T(8,128)S(1)}, s32[128,512]{1,0:T(8,128)}, u32[]{:S(2)}) copy-start(s32[128,512]{1,0:T(8,128)} %refs_2_.3) | copy-start | bytes 786436
  17.7 4.1 %copy-start.4 = (f32[512]{0:T(512)S(1)}, f32[512]{0:T(512)}, u32[]{:S(2)}) copy-start(f32[512]{0:T(512)} %param.9) | copy-start | bytes 6148
  33.9 22.8 %all-to-all-start.2 = ((bf16[4,4,56,128]{3,2,1,0:T(8,128)(2,1)}), bf16[4,4,56,128]{3,2,1,0:T(8,128)(2,1)S(1)}, u32[]{:S(2)}, u32[]{:S(2)}) async-start(bf16[4,4,56,128]{3,2,1,0:T(8,128)(2,1)} %near_sums.1), calls=%async_computation.2 | async-start | bytes 458752 | tf_op jit(solution)/shard_map/all_to_all | solution.py:38
  44.3 0.7 copy-start.6
  45.0 0.9 copy-start.2
  71.7 13.7 %all-to-all-start.4 = ((bf16[4,64,512]{2,1,0:T(8,128)(2,1)}), bf16[4,64,512]{2,1,0:T(8,128)(2,1)S(1)}, u32[]{:S(2)}, u32[]{:S(2)}) async-start(bf16[4,64,512]{2,1,0:T(8,128)(2,1)} %back.1), calls=%async_computation.4 | async-start | bytes 524288 | tf_op jit(solution)/shard_map/all_to_all | solution.py:38

commit v8 on v7

--- a/solution.py
+++ b/solution.py
@@ -92,12 +92,21 @@
     return jnp.concatenate([jnp.where(below, codes, 0.0), jnp.where(below, 0.0, codes)], axis=0).astype(BF)
 
 
-def encode(_, activations, encoder):
-    return (dot(activations, encoder, (0, 0)),)
-
-
-def pair_sum(at, parts):
-    return ([(half_of(at.core, parts[0]) + half_of(at.core, parts[1])).astype(BF)] * N_X,)
+def lanes_of(core, x):
+    half = x.shape[1] // N_CORE
+    return jnp.where(core == 0, x[:, :half], x[:, half:])
+
+
+def encode(at, sides, activations):
+    half = activations.shape[1] // N_CORE
+    latents = sides.shape[2] - half
+    mine = lanes_of(at.core, activations.astype(F32))
+    part = 0.0
+    for core in range(N_CORE):
+        theirs = sides[core, :, latents:].astype(F32)
+        rows = jnp.where(at.core == core, mine, theirs).astype(BF)
+        part = part + dot(rows, sides[core, :, :latents], (0, 0))
+    return ([part.astype(BF)] * N_X,)
 
 
 def kept_codes(at, pieces, mask, bias):
@@ -210,8 +219,8 @@
     rows_act = activations.T
 
     on_core = {'core': core}
-    (enc_part,) = call(encode, [((tokens, latents), F32)], {}, rows_act, encoder)
-    (total,) = call(pair_sum, many, on_core, both_cores(enc_part))
+    sides = both_cores(jnp.concatenate([encoder, lanes_of(1 - core, rows_act)], axis=1))
+    (total,) = call(encode, many, on_core, sides, rows_act)
     decoder_rows, boundaries, total = lax.optimization_barrier((decoder.T, boundaries, total))
 
     has_cut = (place % span == 0) & (group > 0)

time: 91.7 us -> 91.5 us (level)
  local copies, waits for them, and re-layouts: 5.4 us -> 1.42 us
  waiting for transfers between devices: 5.31 us -> 7.55 us
  other arithmetic: 0 us -> 2.15 us
  starting transfers between devices: 20.1 us -> 18.5 us
    unnamed x16 -> x12, local copies, waits for them, and re-layouts: 4.01 us -> 0.03 us
    all_to_all x3, waiting for transfers between devices: 5.31 us -> 7.55 us  [swap(): return lax.all_to_all(x, axis, 0, 0, axis_index_groups=groups, tiled=False)]
    all_to_all x3, starting transfers between devices: 20.1 us -> 18.5 us  [swap(): return lax.all_to_all(x, axis, 0, 0, axis_index_groups=groups, tiled=False)]
    select_n x0 -> x1, other arithmetic: none -> 1.07 us  [lanes_of(): return jnp.where(core == 0, x[:, :half], x[:, half:])]
    concatenate x0 -> x1, other arithmetic: none -> 1.07 us  [body(): jnp.concatenate([encoder, lanes_of(1 - core, rows_act)], axis=1)]
    pallas_call x11 -> x10, Pallas kernels: 5.78 us -> 5.93 us  [call(): pl.pallas_call(kernel, out_shape=[jax.ShapeDtypeStruct(shape, dtype) for...]
where the time goes in v8:
time: 91.5 us; the launch traced here: 90.9 us
  blocking collectives  53.9 us (59%)
  starting transfers between devices  18.5 us (20%)
  waiting for transfers between devices  7.55 us (8%)
  Pallas kernels  5.93 us (6%)
  other arithmetic  2.15 us (2%)
  between operations  1.43 us (2%)
  local copies, waits for them, and re-layouts  1.42 us (2%)
    all_gather x6, blocking collectives, both_cores(): return lax.all_gather(x, 'wid', axis_index_groups=CORE_GROUPS)  29.3 us
    all_to_all x2, blocking collectives, swap(): return lax.all_to_all(x, axis, 0, 0, axis_index_groups=groups, tiled=False)  24.6 us
    all_to_all x3, starting transfers between devices, swap(): return lax.all_to_all(x, axis, 0, 0, axis_index_groups=groups, tiled=False)  18.5 us
    all_to_all x3, waiting for transfers between devices, swap(): return lax.all_to_all(x, axis, 0, 0, axis_index_groups=groups, tiled=False)  7.55 us
    pallas_call x10, Pallas kernels, call(): pl.pallas_call(kernel, out_shape=[jax.ShapeDtypeStruct(shape, dtype) for...  5.93 us
  transfers between devices with their start and end apart: 3, of which 2 were waited for; matrix products, arithmetic and copies ran while one was open for 2% of the time, Pallas kernels for 1%

profile of v8, /device:TPU:1, one launch (start us, length us, event | category | flops | bytes accessed | tf_op | source)
XLA Modules:
  0.0 90.9 jit_solution(11561618683091823246)
XLA Ops:
  0.6 1.1 %slice_select_fusion = bf16[448,64]{1,0:T(8,128)(2,1)S(1)} fusion(bf16[448,128]{1,0:T(8,128)(2,1)} %bitcast.21, pred[]{:T(512)S(6)} %eq.11), kind=kLoop, calls=%fused_computation.1 | loop fusion | flops 28672 | bytes 172033 | tf_op jit(solution)/shard_map/jit(_where)/select_n | solution.py:97
  1.7 1.1 %pad_maximum_fusion = bf16[448,576]{1,0:T(8,128)(2,1)S(1)} fusion(bf16[448,64]{1,0:T(8,128)(2,1)S(1)} %slice_select_fusion, bf16[448,512]{1,0:T(8,128)(2,1)} %param.8), kind=kLoop, calls=%fused_computation | loop fusion | flops 1032192 | bytes 1032192 | tf_op jit(solution)/shard_map/concatenate | solution.py:222
  2.8 0.0 copy-start
  2.8 9.3 %all-gather = bf16[896,576]{1,0:T(8,128)(2,1)S(1)} all-gather(bf16[448,576]{1,0:T(8,128)(2,1)S(1)} %pad_maximum_fusion), channel_id=2, replica_groups={{0,1},{2,3},{4,5},{6,7},{8,9},{10,11},{12,13},{14,15},{16,17},{18,19},{..., dimensions={0}, use_global_device_ids=true | all-gather | bytes 1548288 | tf_op jit(solution)/shard_map/all_gather | solution.py:203
  12.1 0.0 copy-start.5
  12.1 0.0 copy-start.3
  12.1 0.0 copy-done
  12.1 1.1 %encode.1 = bf16[4,64,512]{2,1,0:T(8,128)(2,1)} custom-call(s32[1]{0:T(128)} %bitcast.refs_0_, bf16[2,448,576]{2,1,0:T(8,128)(2,1)S(1)} %bitcast.20, bf16[448,128]{1,0:T(8,128)(2,1)S(1)} %bitcast.22), custom_call_target="tpu_custom_call" | custom-call | tf_op jit(solution)/shard_map/encode/pallas_call | solution.py:74
  13.2 0.0 copy-start.1
  13.2 0.0 copy-start.2
  13.2 3.5 %all-to-all-start = ((bf16[4,64,512]{2,1,0:T(8,128)(2,1)}), bf16[4,64,512]{2,1,0:T(8,128)(2,1)S(1)}, u32[]{:S(2)}, u32[]{:S(2)}) async-start(bf16[4,64,512]{2,1,0:T(8,128)(2,1)} %encode.1), calls=%async_computation | async-start | bytes 524288 | tf_op jit(solution)/shard_map/all_to_all | solution.py:38
  16.8 0.0 copy-done.5
  16.8 0.6 dynamic_slice.3
  18.0 0.0 copy-done.3
  18.0 2.5 %all-gather.1 = bf16[896,512]{1,0:T(8,128)(2,1)S(1)} all-gather(bf16[448,512]{1,0:T(8,128)(2,1)S(1)} %bitcast.31), channel_id=3, replica_groups={{0,1},{2,3},{4,5},{6,7},{8,9},{10,11},{12,13},{14,15},{16,17},{18,19},{..., dimensions={0}, use_global_device_ids=true | all-gather | bytes 1376256 | tf_op jit(solution)/shard_map/all_gather | solution.py:203
  20.5 2.3 %all-to-all-done.refs_1_ = bf16[4,64,512]{2,1,0:T(8,128)(2,1)S(1)} async-done(((bf16[4,64,512]{2,1,0:T(8,128)(2,1)}), bf16[4,64,512]{2,1,0:T(8,128)(2,1)S(1)}, u32[]{:S(2)}, u32[]{:S(2)}) %all-to-all-start) | async-done | bytes 262176 | tf_op jit(solution)/shard_map/all_to_all | solution.py:38
  22.8 0.0 copy-done.1
  22.8 0.0 copy-done.2
  22.8 0.1 kept_codes.1.refs_1_
  22.9 0.0 copy-start.4
  22.9 0.4 decode.1
  23.3 10.9 %all_to_all.25.refs_0_ = bf16[16,56,128]{2,1,0:T(8,128)(2,1)S(1)} all-to-all(bf16[16,56,128]{2,1,0:T(8,128)(2,1)S(1)} %decode.1), channel_id=1, replica_groups={{0,8,16,24,128,136,144,152,256,264,272,280,384,392,400,408},{32,40,48,5..., dimensions={0} | all-to-all | bytes 458752 | tf_op jit(solution)/shard_map/all_to_all | solution.py:38
  34.2 0.7 near_sums.1
  34.9 10.4 %all-to-all-start.2 = ((bf16[4,4,56,128]{3,2,1,0:T(8,128)(2,1)}), bf16[4,4,56,128]{3,2,1,0:T(8,128)(2,1)S(1)}, u32[]{:S(2)}, u32[]{:S(2)}) async-start(bf16[4,4,56,128]{3,2,1,0:T(8,128)(2,1)} %near_sums.1), calls=%async_computation.2 | async-start | bytes 458752 | tf_op jit(solution)/shard_map/all_to_all | solution.py:38
  45.3 0.0 copy-done.4
  45.3 0.1 copy.12.refs_2_
  45.4 0.1 own_base.1
  45.5 5.0 %all-gather.6.refs_3_ = f32[2,28,128]{2,1,0:T(8,128)S(1)} all-gather(f32[1,28,128]{2,1,0:T(8,128)S(1)} %bitcast.28), channel_id=4, replica_groups={{0,1},{2,3},{4,5},{6,7},{8,9},{10,11},{12,13},{14,15},{16,17},{18,19},{..., dimensions={0}, use_global_device_ids=true | all-gather | bytes 43008 | tf_op jit(solution)/shard_map/all_gather | solution.py:203
  50.5 1.9 %all-gather.3 = bf16[128,512]{1,0:T(8,128)(2,1)S(1)} all-gather(bf16[64,512]{1,0:T(8,128)(2,1)S(1)} %kept_codes.1.refs_1_), channel_id=5, replica_groups={{0,1},{2,3},{4,5},{6,7},{8,9},{10,11},{12,13},{14,15},{16,17},{18,19},{..., dimensions={0}, use_global_device_ids=true | all-gather | bytes 196608 | tf_op jit(solution)/shard_map/all_gather | solution.py:203
  52.4 5.2 %all-to-all-done.2.refs_2_ = bf16[4,4,56,128]{3,2,1,0:T(8,128)(2,1)S(1)} async-done(((bf16[4,4,56,128]{3,2,1,0:T(8,128)(2,1)}), bf16[4,4,56,128]{3,2,1,0:T(8,128)(2,1)S(1)}, u32[]{:S(2)}, u32[]{:S(2)}) %all-to-all-start.2) | async-done | bytes 229408 | tf_op jit(solution)/shard_map/all_to_all | solution.py:38
  57.6 0.2 suffixes.1
  57.9 13.8 %all_to_all.26.refs_1_ = bf16[16,64,128]{2,1,0:T(8,128)(2,1)S(1)} all-to-all(bf16[16,64,128]{2,1,0:T(8,128)(2,1)S(1)} %suffixes.1), channel_id=1, replica_groups={{0,8,16,24,128,136,144,152,256,264,272,280,384,392,400,408},{32,40,48,5..., dimensions={0} | all-to-all | bytes 524288 | tf_op jit(solution)/shard_map/all_to_all | solution.py:38
  71.6 1.0 %back.1 = bf16[4,64,512]{2,1,0:T(8,128)(2,1)} custom-call(s32[1]{0:T(128)} %bitcast.7.refs_0_.refs_1_, bf16[16,64,128]{2,1,0:T(8,128)(2,1)S(1)} %all_to_all.26.refs_1_, bf16[2,448,512]{2,1,0:T(8,128)(2,1)S(1)} %bitcast.19), custom_call_target="tpu_custom_call" | custom-call | tf_op jit(solution)/shard_map/back/pallas_call | solution.py:74
  72.7 4.6 %all-to-all-start.4 = ((bf16[4,64,512]{2,1,0:T(8,128)(2,1)}), bf16[4,64,512]{2,1,0:T(8,128)(2,1)S(1)}, u32[]{:S(2)}, u32[]{:S(2)}) async-start(bf16[4,64,512]{2,1,0:T(8,128)(2,1)} %back.1), calls=%async_computation.4 | async-start | bytes 524288 | tf_op jit(solution)/shard_map/all_to_all | solution.py:38
  77.3 6.1 %all-gather.5 = bf16[32,64,128]{2,1,0:T(8,128)(2,1)S(1)} all-gather(bf16[16,64,128]{2,1,0:T(8,128)(2,1)S(1)} %all_to_all.26.refs_1_), channel_id=7, replica_groups={{0,1},{2,3},{4,5},{6,7},{8,9},{10,11},{12,13},{14,15},{16,17},{18,19},{..., dimensions={0}, use_global_device_ids=true | all-gather | bytes 786432 | tf_op jit(solution)/shard_map/all_gather | solution.py:203
  83.5 1.2 %decoder_grads.1 = (bf16[448,512]{1,0:T(8,128)(2,1)}, f32[16,128]{1,0:T(8,128)S(1)}) custom-call(s32[1]{0:T(128)} %bitcast.refs_0_, s32[1]{0:T(128)} %bitcast.7.refs_0_.refs_1_, bf16[2,16,64,128]{3,2,1,0:T(8,128)(2,1)S(1)} %bitcast.25, bf16[2,64,512]{2,1,0:T(8,128)(2,1)S(1)} %bitcast.26), custom_call_target="tpu_custom_call" | custom-call | tf_op jit(solution)/shard_map/decoder_grads/pallas_call | solution.py:74
  84.6 0.7 reshape.40
  85.3 0.0 all-to-all-done.4.refs_1_
  85.3 0.1 kept_grads.1
  85.3 4.6 %all-gather.4 = bf16[128,512]{1,0:T(8,128)(2,1)S(1)} all-gather(bf16[64,512]{1,0:T(8,128)(2,1)S(1)} %kept_grads.1), channel_id=6, replica_groups={{0,1},{2,3},{4,5},{6,7},{8,9},{10,11},{12,13},{14,15},{16,17},{18,19},{..., dimensions={0}, use_global_device_ids=true | all-gather | bytes 196608 | tf_op jit(solution)/shard_map/all_gather | solution.py:203
  89.9 1.0 %encoder_grads.1 = (bf16[448,512]{1,0:T(8,128)(2,1)}, f32[1,512]{1,0:T(1,128)}) custom-call(bf16[2,64,512]{2,1,0:T(8,128)(2,1)S(1)} %bitcast.27, bf16[448,128]{1,0:T(8,128)(2,1)S(1)} %bitcast.24), custom_call_target="tpu_custom_call" | custom-call | tf_op jit(solution)/shard_map/encoder_grads/pallas_call | solution.py:74
Async XLA Ops:
  2.8 9.3 %copy-start = (bf16[128,448]{0,1:T(8,128)(2,1)S(1)}, bf16[128,448]{0,1:T(8,128)(2,1)}, u32[]{:S(2)}) copy-start(bf16[128,448]{0,1:T(8,128)(2,1)} %param.7) | copy-start | bytes 344068
  12.1 4.7 %copy-start.5 = (s32[8]{0:T(128)S(1)}, s32[8]{0:T(128)}, u32[]{:S(2)}) copy-start(s32[8]{0:T(128)} %param.13) | copy-start | bytes 100
  12.1 5.9 %copy-start.3 = (bf16[512,448]{0,1:T(8,128)(2,1)S(1)}, bf16[512,448]{0,1:T(8,128)(2,1)}, u32[]{:S(2)}) copy-start(bf16[512,448]{0,1:T(8,128)(2,1)} %param.10) | copy-start | bytes 1376260
  13.2 9.6 %copy-start.1 = (s32[128,512]{1,0:T(8,128)S(1)}, s32[128,512]{1,0:T(8,128)}, u32[]{:S(2)}) copy-start(s32[128,512]{1,0:T(8,128)} %refs_2_.3) | copy-start | bytes 786436
  13.2 9.6 %copy-start.2 = (f32[512]{0:T(512)S(1)}, f32[512]{0:T(512)}, u32[]{:S(2)}) copy-start(f32[512]{0:T(512)} %param.9) | copy-start | bytes 6148
  13.2 9.6 %all-to-all-start = ((bf16[4,64,512]{2,1,0:T(8,128)(2,1)}), bf16[4,64,512]{2,1,0:T(8,128)(2,1)S(1)}, u32[]{:S(2)}, u32[]{:S(2)}) async-start(bf16[4,64,512]{2,1,0:T(8,128)(2,1)} %encode.1), calls=%async_computation | async-start | bytes 524288 | tf_op jit(solution)/shard_map/all_to_all | solution.py:38
  22.9 22.4 %copy-start.4 = (f32[448]{0:T(512)S(1)}, f32[448]{0:T(512)}, u32[]{:S(2)}) copy-start(f32[448]{0:T(512)} %param.11) | copy-start | bytes 5380
  34.9 22.8 %all-to-all-start.2 = ((bf16[4,4,56,128]{3,2,1,0:T(8,128)(2,1)}), bf16[4,4,56,128]{3,2,1,0:T(8,128)(2,1)S(1)}, u32[]{:S(2)}, u32[]{:S(2)}) async-start(bf16[4,4,56,128]{3,2,1,0:T(8,128)(2,1)} %near_sums.1), calls=%async_computation.2 | async-start | bytes 458752 | tf_op jit(solution)/shard_map/all_to_all | solution.py:38
  72.7 12.6 %all-to-all-start.4 = ((bf16[4,64,512]{2,1,0:T(8,128)(2,1)}), bf16[4,64,512]{2,1,0:T(8,128)(2,1)S(1)}, u32[]{:S(2)}, u32[]{:S(2)}) async-start(bf16[4,64,512]{2,1,0:T(8,128)(2,1)} %back.1), calls=%async_computation.4 | async-start | bytes 524288 | tf_op jit(solution)/shard_map/all_to_all | solution.py:38

commit v9 on v7

--- a/solution.py
+++ b/solution.py
@@ -21,17 +21,18 @@
     return N_Z * y + NEAR * q + (s + TURN[q]) % NEAR
 
 
-NEAR_GROUPS = [[at(y, q, s) for y in range(N_Y) for s in range(NEAR)] for q in range(N_FAR)]
-FAR_GROUPS = [[at(y, q, s) for q in range(N_FAR)] for y in range(N_Y) for s in range(NEAR)]
+NEAR_ORDER = [(3, 2), (0, 1), (0, 3), (3, 3), (2, 0), (0, 0), (1, 3), (2, 1), (1, 2), (1, 0), (3, 1), (1, 1), (2, 3), (0, 2), (3, 0), (2, 2)]
+NEAR_GROUPS = [[at(y, q, s) for y, s in NEAR_ORDER] for q in range(N_FAR)]
+FAR_GROUPS = [[at(y, q, s) for q in range(N_FAR)] for y, s in NEAR_ORDER]
 PIECE = 28
 ROWS = 2 * PIECE
 TAG_ROWS = 8
 N_CORE, N_X = 2, 4
 CORE_GROUPS = [[N_CORE * x + c for c in range(N_CORE)] for x in range(N_X)]
-CHIP_GROUPS = [[N_CORE * x + c for x in range(N_X)] for c in range(N_CORE)]
-
-
-Scalars = collections.namedtuple('Scalars', ['core', 'late', 'cut', 'my_slice'], defaults=(None,) * 4)
+CHIP_GROUPS = [[N_CORE * x + c for x in (0, 2, 1, 3)] for c in range(N_CORE)]
+
+
+Scalars = collections.namedtuple('Scalars', ['core', 'late', 'cut', 'my_place'], defaults=(None,) * 4)
 
 
 def swap(x, axis, groups=None):
@@ -116,14 +117,16 @@
 
 
 def near_sums(_, got):
-    tokens = got.shape[-1]
-    got = got.astype(F32).reshape(N_Y, NEAR, ROWS, tokens)
-    return ([jnp.sum(got, axis=1).astype(BF)] * N_FAR,)
+    got = got.astype(F32)
+    sums = [sum(got[i] for i, (at_y, _) in enumerate(NEAR_ORDER) if at_y == y) for y in range(N_Y)]
+    return ([jnp.stack(sums).astype(BF)] * N_FAR,)
 
 
 def own_base(at, activations, bias):
     base = bias - activations.astype(F32)
-    pieces = [jnp.where(at.my_slice == i, base[PIECE * i : PIECE * (i + 1)], 0.0) for i in range(SLICES)]
+    pieces = [
+        jnp.where(at.my_place == NEAR * y + s, base[PIECE * i : PIECE * (i + 1)], 0.0) for i, (y, s) in enumerate(NEAR_ORDER)
+    ]
     return (sum(pieces),)
 
 
@@ -162,8 +165,8 @@
         own = jnp.where(at.late == 1, suffix[2 * y + 1], suffix[2 * y])
         previous = jnp.where(at.late == 1, suffix[2 * y], suffix[max(2 * y - 1, 0)])
         pair = jnp.where(lane < half, other_half(previous), own)
-        out += [jnp.concatenate([pair, tags], axis=0).astype(BF)] * NEAR
-    return (out,)
+        out.append(jnp.concatenate([pair, tags], axis=0).astype(BF))
+    return ([out[y] for y, _ in NEAR_ORDER],)
 
 
 def back(at, got, decoders):
@@ -203,7 +206,7 @@
     group = place // span
     y, z = place // N_Z, place % N_Z
     late = z // NEAR >= N_FAR // 2
-    my_slice = NEAR * y + (z - jnp.where(late, NEAR // 2, 0)) % NEAR
+    my_place = NEAR * y + (z - jnp.where(late, NEAR // 2, 0)) % NEAR
     half = (tokens // N_CORE, latents)
     half_low = [(half, BF)]
     many = [((N_X,) + half, BF)]
@@ -228,7 +231,7 @@
     (got,) = call(near_sums, [((N_FAR, N_Y, ROWS, tokens), BF)], {}, got)
     later_act, later_bias, later_codes, got = lax.optimization_barrier((rows_act, decoder_bias, my_codes, got))
     got = swap(got, "lat", FAR_GROUPS)
-    (base,) = call(own_base, [((PIECE, tokens), F32)], {'my_slice': my_slice}, later_act, later_bias[:, None])
+    (base,) = call(own_base, [((PIECE, tokens), F32)], {'my_place': my_place}, later_act, later_bias[:, None])
     base, codes = both_cores(base), both_cores(later_codes)
     got, base, codes = lax.optimization_barrier((got, base, codes))
     (got,) = call(suffixes, [((SLICES, ROWS + TAG_ROWS, tokens), BF)], {'core': core, 'late': late}, got, base)

time: 91.7 us -> 91.8 us (level)
  blocking collectives: 53 us -> 48.1 us
  waiting for transfers between devices: 5.31 us -> 9.08 us
  starting transfers between devices: 20.1 us -> 21.3 us
    all_to_all x3, waiting for transfers between devices: 5.31 us -> 9.08 us  [swap(): return lax.all_to_all(x, axis, 0, 0, axis_index_groups=groups, tiled=False)]
    all_gather x6, blocking collectives: 28.4 us -> 25.1 us  [both_cores(): return lax.all_gather(x, 'wid', axis_index_groups=CORE_GROUPS)]
    all_to_all x2, blocking collectives: 24.6 us -> 23 us  [swap(): return lax.all_to_all(x, axis, 0, 0, axis_index_groups=groups, tiled=False)]
    all_to_all x3, starting transfers between devices: 20.1 us -> 21.3 us  [swap(): return lax.all_to_all(x, axis, 0, 0, axis_index_groups=groups, tiled=False)]
where the time goes in v9:
time: 91.8 us; the launch traced here: 91.1 us
  blocking collectives  48.1 us (52%)
  starting transfers between devices  21.3 us (23%)
  waiting for transfers between devices  9.08 us (10%)
  Pallas kernels  5.79 us (6%)
  local copies, waits for them, and re-layouts  5.4 us (6%)
  between operations  1.43 us (2%)
    all_gather x6, blocking collectives, both_cores(): return lax.all_gather(x, 'wid', axis_index_groups=CORE_GROUPS)  25.1 us
    all_to_all x2, blocking collectives, swap(): return lax.all_to_all(x, axis, 0, 0, axis_index_groups=groups, tiled=False)  23 us
    all_to_all x3, starting transfers between devices, swap(): return lax.all_to_all(x, axis, 0, 0, axis_index_groups=groups, tiled=False)  21.3 us
    all_to_all x3, waiting for transfers between devices, swap(): return lax.all_to_all(x, axis, 0, 0, axis_index_groups=groups, tiled=False)  9.08 us
    pallas_call x11, Pallas kernels, call(): pl.pallas_call(kernel, out_shape=[jax.ShapeDtypeStruct(shape, dtype) for...  5.79 us
    unnamed x16, local copies, waits for them, and re-layouts  4.01 us
  transfers between devices with their start and end apart: 3, of which 2 were waited for; matrix products, arithmetic and copies ran while one was open for 2% of the time, Pallas kernels for 1%

profile of v9, /device:TPU:1, one launch (start us, length us, event | category | flops | bytes accessed | tf_op | source)
XLA Modules:
  0.0 91.1 jit_solution(3204798083866975443)
XLA Ops:
  0.6 0.0 copy-start.1
  0.7 0.9 copy-done.1
  1.5 0.0 copy-start.3
  1.5 1.0 %copy-done.3 = bf16[448,512]{1,0:T(8,128)(2,1)S(1)} copy-done((bf16[448,512]{1,0:T(8,128)(2,1)S(1)}, bf16[448,512]{1,0:T(8,128)(2,1)}, u32[]{:S(2)}) %copy-start.3) | copy-done | bytes 458776
  2.6 0.2 encode.1
  2.8 8.7 %all-gather = f32[256,512]{1,0:T(8,128)S(1)} all-gather(f32[128,512]{1,0:T(8,128)S(1)} %encode.1), channel_id=2, replica_groups={{0,1},{2,3},{4,5},{6,7},{8,9},{10,11},{12,13},{14,15},{16,17},{18,19},{..., dimensions={0}, use_global_device_ids=true | all-gather | bytes 786432 | tf_op jit(solution)/shard_map/all_gather | solution.py:197
  11.5 0.7 pair_sum.1
  12.2 0.0 copy-start.5
  12.2 3.5 %all-to-all-start = ((bf16[4,64,512]{2,1,0:T(8,128)(2,1)}), bf16[4,64,512]{2,1,0:T(8,128)(2,1)S(1)}, u32[]{:S(2)}, u32[]{:S(2)}) async-start(bf16[4,64,512]{2,1,0:T(8,128)(2,1)} %pair_sum.1), calls=%async_computation | async-start | bytes 524288 | tf_op jit(solution)/shard_map/all_to_all | solution.py:39
  15.8 0.0 copy-start.7
  15.8 0.6 copy-done.7
  16.5 0.6 dynamic_slice.3
  17.7 0.0 copy-done.5
  17.7 0.0 copy-start
  17.7 0.0 copy-start.4
  17.7 2.6 %all-gather.1 = bf16[896,512]{1,0:T(8,128)(2,1)S(1)} all-gather(bf16[448,512]{1,0:T(8,128)(2,1)S(1)} %bitcast.30), channel_id=3, replica_groups={{0,1},{2,3},{4,5},{6,7},{8,9},{10,11},{12,13},{14,15},{16,17},{18,19},{..., dimensions={0}, use_global_device_ids=true | all-gather | bytes 1376256 | tf_op jit(solution)/shard_map/all_gather | solution.py:197
  20.3 2.0 %all-to-all-done.refs_1_ = bf16[4,64,512]{2,1,0:T(8,128)(2,1)S(1)} async-done(((bf16[4,64,512]{2,1,0:T(8,128)(2,1)}), bf16[4,64,512]{2,1,0:T(8,128)(2,1)S(1)}, u32[]{:S(2)}, u32[]{:S(2)}) %all-to-all-start) | async-done | bytes 262176 | tf_op jit(solution)/shard_map/all_to_all | solution.py:39
  22.3 0.0 copy-done
  22.3 0.0 copy-done.4
  22.3 0.1 kept_codes.1.refs_1_
  22.4 0.4 decode.1
  22.8 10.1 %all_to_all.25.refs_0_ = bf16[16,56,128]{2,1,0:T(8,128)(2,1)S(1)} all-to-all(bf16[16,56,128]{2,1,0:T(8,128)(2,1)S(1)} %decode.1), channel_id=1, replica_groups={{400,8,24,408,256,0,152,264,144,128,392,136,280,16,384,272},{432,40,56,..., dimensions={0} | all-to-all | bytes 458752 | tf_op jit(solution)/shard_map/all_to_all | solution.py:39
  32.9 0.7 near_sums.1
  33.6 11.7 %all-to-all-start.2 = ((bf16[4,4,56,128]{3,2,1,0:T(8,128)(2,1)}), bf16[4,4,56,128]{3,2,1,0:T(8,128)(2,1)S(1)}, u32[]{:S(2)}, u32[]{:S(2)}) async-start(bf16[4,4,56,128]{3,2,1,0:T(8,128)(2,1)} %near_sums.1), calls=%async_computation.2 | async-start | bytes 458752 | tf_op jit(solution)/shard_map/all_to_all | solution.py:39
  45.3 0.0 copy-start.6
  45.3 0.7 copy-done.6
  46.0 0.0 copy-start.2
  46.0 0.1 copy.12.refs_2_
  46.1 0.8 copy-done.2
  46.9 0.1 own_base.1
  47.0 3.0 %all-gather.6.refs_3_ = f32[2,28,128]{2,1,0:T(8,128)S(1)} all-gather(f32[1,28,128]{2,1,0:T(8,128)S(1)} %bitcast.27), channel_id=4, replica_groups={{0,1},{2,3},{4,5},{6,7},{8,9},{10,11},{12,13},{14,15},{16,17},{18,19},{..., dimensions={0}, use_global_device_ids=true | all-gather | bytes 43008 | tf_op jit(solution)/shard_map/all_gather | solution.py:197
  50.0 1.9 %all-gather.3 = bf16[128,512]{1,0:T(8,128)(2,1)S(1)} all-gather(bf16[64,512]{1,0:T(8,128)(2,1)S(1)} %kept_codes.1.refs_1_), channel_id=5, replica_groups={{0,1},{2,3},{4,5},{6,7},{8,9},{10,11},{12,13},{14,15},{16,17},{18,19},{..., dimensions={0}, use_global_device_ids=true | all-gather | bytes 196608 | tf_op jit(solution)/shard_map/all_gather | solution.py:197
  51.9 7.1 %all-to-all-done.2.refs_2_ = bf16[4,4,56,128]{3,2,1,0:T(8,128)(2,1)S(1)} async-done(((bf16[4,4,56,128]{3,2,1,0:T(8,128)(2,1)}), bf16[4,4,56,128]{3,2,1,0:T(8,128)(2,1)S(1)}, u32[]{:S(2)}, u32[]{:S(2)}) %all-to-all-start.2) | async-done | bytes 229408 | tf_op jit(solution)/shard_map/all_to_all | solution.py:39
  59.0 0.2 suffixes.1
  59.2 12.9 %all_to_all.26.refs_1_ = bf16[16,64,128]{2,1,0:T(8,128)(2,1)S(1)} all-to-all(bf16[16,64,128]{2,1,0:T(8,128)(2,1)S(1)} %suffixes.1), channel_id=1, replica_groups={{400,8,24,408,256,0,152,264,144,128,392,136,280,16,384,272},{432,40,56,..., dimensions={0} | all-to-all | bytes 524288 | tf_op jit(solution)/shard_map/all_to_all | solution.py:39
  72.1 1.0 %back.1 = bf16[4,64,512]{2,1,0:T(8,128)(2,1)} custom-call(s32[1]{0:T(128)} %bitcast.7.refs_0_.refs_1_, bf16[16,64,128]{2,1,0:T(8,128)(2,1)S(1)} %all_to_all.26.refs_1_, bf16[2,448,512]{2,1,0:T(8,128)(2,1)S(1)} %bitcast.19), custom_call_target="tpu_custom_call" | custom-call | tf_op jit(solution)/shard_map/back/pallas_call | solution.py:75
  73.2 6.2 %all-to-all-start.4 = ((bf16[4,64,512]{2,1,0:T(8,128)(2,1)}), bf16[4,64,512]{2,1,0:T(8,128)(2,1)S(1)}, u32[]{:S(2)}, u32[]{:S(2)}) async-start(bf16[4,64,512]{2,1,0:T(8,128)(2,1)} %back.1), calls=%async_computation.4 | async-start | bytes 524288 | tf_op jit(solution)/shard_map/all_to_all | solution.py:39
  79.3 4.6 %all-gather.5 = bf16[32,64,128]{2,1,0:T(8,128)(2,1)S(1)} all-gather(bf16[16,64,128]{2,1,0:T(8,128)(2,1)S(1)} %all_to_all.26.refs_1_), channel_id=7, replica_groups={{0,1},{2,3},{4,5},{6,7},{8,9},{10,11},{12,13},{14,15},{16,17},{18,19},{..., dimensions={0}, use_global_device_ids=true | all-gather | bytes 786432 | tf_op jit(solution)/shard_map/all_gather | solution.py:197
  83.9 1.2 %decoder_grads.1 = (bf16[448,512]{1,0:T(8,128)(2,1)}, f32[16,128]{1,0:T(8,128)S(1)}) custom-call(s32[1]{0:T(128)} %bitcast.refs_0_, s32[1]{0:T(128)} %bitcast.7.refs_0_.refs_1_, bf16[2,16,64,128]{3,2,1,0:T(8,128)(2,1)S(1)} %bitcast.20, bf16[2,64,512]{2,1,0:T(8,128)(2,1)S(1)} %bitcast.25), custom_call_target="tpu_custom_call" | custom-call | tf_op jit(solution)/shard_map/decoder_grads/pallas_call | solution.py:75
  85.1 0.7 reshape.40
  85.7 0.0 all-to-all-done.4.refs_1_
  85.7 0.1 kept_grads.1
  85.8 4.3 %all-gather.4 = bf16[128,512]{1,0:T(8,128)(2,1)S(1)} all-gather(bf16[64,512]{1,0:T(8,128)(2,1)S(1)} %kept_grads.1), channel_id=6, replica_groups={{0,1},{2,3},{4,5},{6,7},{8,9},{10,11},{12,13},{14,15},{16,17},{18,19},{..., dimensions={0}, use_global_device_ids=true | all-gather | bytes 196608 | tf_op jit(solution)/shard_map/all_gather | solution.py:197
  90.1 1.0 %encoder_grads.1 = (bf16[448,512]{1,0:T(8,128)(2,1)}, f32[1,512]{1,0:T(1,128)}) custom-call(bf16[2,64,512]{2,1,0:T(8,128)(2,1)S(1)} %bitcast.26, bf16[448,128]{1,0:T(8,128)(2,1)S(1)} %bitcast.24), custom_call_target="tpu_custom_call" | custom-call | tf_op jit(solution)/shard_map/encoder_grads/pallas_call | solution.py:75
Async XLA Ops:
  0.6 0.9 copy-start.1
  1.5 1.0 %copy-start.3 = (bf16[448,512]{1,0:T(8,128)(2,1)S(1)}, bf16[448,512]{1,0:T(8,128)(2,1)}, u32[]{:S(2)}) copy-start(bf16[448,512]{1,0:T(8,128)(2,1)} %refs_1_.1) | copy-start | bytes 1376260
  12.2 5.5 %copy-start.5 = (bf16[512,448]{0,1:T(8,128)(2,1)S(1)}, bf16[512,448]{0,1:T(8,128)(2,1)}, u32[]{:S(2)}) copy-start(bf16[512,448]{0,1:T(8,128)(2,1)} %param.10) | copy-start | bytes 1376260
  12.2 10.1 %all-to-all-start = ((bf16[4,64,512]{2,1,0:T(8,128)(2,1)}), bf16[4,64,512]{2,1,0:T(8,128)(2,1)S(1)}, u32[]{:S(2)}, u32[]{:S(2)}) async-start(bf16[4,64,512]{2,1,0:T(8,128)(2,1)} %pair_sum.1), calls=%async_computation | async-start | bytes 524288 | tf_op jit(solution)/shard_map/all_to_all | solution.py:39
  15.8 0.7 copy-start.7
  17.7 4.6 %copy-start = (s32[128,512]{1,0:T(8,128)S(1)}, s32[128,512]{1,0:T(8,128)}, u32[]{:S(2)}) copy-start(s32[128,512]{1,0:T(8,128)} %refs_2_.3) | copy-start | bytes 786436
  17.7 4.6 %copy-start.4 = (f32[512]{0:T(512)S(1)}, f32[512]{0:T(512)}, u32[]{:S(2)}) copy-start(f32[512]{0:T(512)} %param.9) | copy-start | bytes 6148
  33.6 25.4 %all-to-all-start.2 = ((bf16[4,4,56,128]{3,2,1,0:T(8,128)(2,1)}), bf16[4,4,56,128]{3,2,1,0:T(8,128)(2,1)S(1)}, u32[]{:S(2)}, u32[]{:S(2)}) async-start(bf16[4,4,56,128]{3,2,1,0:T(8,128)(2,1)} %near_sums.1), calls=%async_computation.2 | async-start | bytes 458752 | tf_op jit(solution)/shard_map/all_to_all | solution.py:39
  45.3 0.7 copy-start.6
  46.0 0.9 copy-start.2
  73.2 12.6 %all-to-all-start.4 = ((bf16[4,64,512]{2,1,0:T(8,128)(2,1)}), bf16[4,64,512]{2,1,0:T(8,128)(2,1)S(1)}, u32[]{:S(2)}, u32[]{:S(2)}) async-start(bf16[4,64,512]{2,1,0:T(8,128)(2,1)} %back.1), calls=%async_computation.4 | async-start | bytes 524288 | tf_op jit(solution)/shard_map/all_to_all | solution.py:39

commit v10 on v7

--- a/solution.py
+++ b/solution.py
@@ -90,10 +90,6 @@
     codes = codes.astype(F32)
     below = lax.broadcasted_iota(jnp.int32, codes.shape, 1) < cut
     return jnp.concatenate([jnp.where(below, codes, 0.0), jnp.where(below, 0.0, codes)], axis=0).astype(BF)
-
-
-def encode(_, activations, encoder):
-    return (dot(activations, encoder, (0, 0)),)
 
 
 def pair_sum(at, parts):
@@ -210,7 +206,7 @@
     rows_act = activations.T
 
     on_core = {'core': core}
-    (enc_part,) = call(encode, [((tokens, latents), F32)], {}, rows_act, encoder)
+    enc_part = dot(activations, encoder, (1, 0))
     (total,) = call(pair_sum, many, on_core, both_cores(enc_part))
     decoder_rows, boundaries, total = lax.optimization_barrier((decoder.T, boundaries, total))
 

time: 91.7 us -> 91.7 us (level)
  matrix products: 0 us -> 1.14 us
    dot_general x0 -> x1, matrix products: none -> 1.14 us  [dot(): lax.dot_general(a, b, (((over[0],), (over[1],)), ((), ())), preferred_ele...]
    unnamed x16 -> x14, local copies, waits for them, and re-layouts: 4.01 us -> 3.11 us
    pallas_call x11 -> x10, Pallas kernels: 5.78 us -> 5.55 us  [call(): pl.pallas_call(kernel, out_shape=[jax.ShapeDtypeStruct(shape, dtype) for...]
where the time goes in v10:
time: 91.7 us; the launch traced here: 91.1 us
  blocking collectives  53 us (58%)
  starting transfers between devices  20.2 us (22%)
  Pallas kernels  5.55 us (6%)
  waiting for transfers between devices  5.31 us (6%)
  local copies, waits for them, and re-layouts  4.49 us (5%)
  between operations  1.43 us (2%)
  matrix products  1.14 us (1%)
    all_gather x6, blocking collectives, both_cores(): return lax.all_gather(x, 'wid', axis_index_groups=CORE_GROUPS)  28.5 us
    all_to_all x2, blocking collectives, swap(): return lax.all_to_all(x, axis, 0, 0, axis_index_groups=groups, tiled=False)  24.6 us
    all_to_all x3, starting transfers between devices, swap(): return lax.all_to_all(x, axis, 0, 0, axis_index_groups=groups, tiled=False)  20.2 us
    pallas_call x10, Pallas kernels, call(): pl.pallas_call(kernel, out_shape=[jax.ShapeDtypeStruct(shape, dtype) for...  5.55 us
    all_to_all x3, waiting for transfers between devices, swap(): return lax.all_to_all(x, axis, 0, 0, axis_index_groups=groups, tiled=False)  5.31 us
    unnamed x14, local copies, waits for them, and re-layouts  3.11 us
  transfers between devices with their start and end apart: 3, of which 2 were waited for; matrix products, arithmetic and copies ran while one was open for 2% of the time, Pallas kernels for 1%

profile of v10, /device:TPU:1, one launch (start us, length us, event | category | flops | bytes accessed | tf_op | source)
XLA Modules:
  0.0 91.1 jit_solution(18251144684358280240)
XLA Ops:
  0.6 0.0 copy-start
  0.7 1.0 %copy-done = bf16[448,512]{1,0:T(8,128)(2,1)S(1)} copy-done((bf16[448,512]{1,0:T(8,128)(2,1)S(1)}, bf16[448,512]{1,0:T(8,128)(2,1)}, u32[]{:S(2)}) %copy-start) | copy-done | bytes 458776
  1.7 1.1 %fusion = f32[128,512]{1,0:T(8,128)S(1)} fusion(bf16[128,448]{0,1:T(8,128)(2,1)} %param.7, bf16[448,512]{1,0:T(8,128)(2,1)S(1)} %copy-done), kind=kOutput, calls=%fused_computation | convolution fusion | flops 58720256 | bytes 835584 | tf_op jit(solution)/shard_map/dot_general | solution.py:46
  2.8 8.7 %all-gather = f32[256,512]{1,0:T(8,128)S(1)} all-gather(f32[128,512]{1,0:T(8,128)S(1)} %fusion), channel_id=2, replica_groups={{0,1},{2,3},{4,5},{6,7},{8,9},{10,11},{12,13},{14,15},{16,17},{18,19},{..., dimensions={0}, use_global_device_ids=true | all-gather | bytes 786432 | tf_op jit(solution)/shard_map/all_gather | solution.py:190
  11.5 0.7 pair_sum.1
  12.2 0.0 copy-start.4
  12.2 3.5 %all-to-all-start = ((bf16[4,64,512]{2,1,0:T(8,128)(2,1)}), bf16[4,64,512]{2,1,0:T(8,128)(2,1)S(1)}, u32[]{:S(2)}, u32[]{:S(2)}) async-start(bf16[4,64,512]{2,1,0:T(8,128)(2,1)} %pair_sum.1), calls=%async_computation | async-start | bytes 524288 | tf_op jit(solution)/shard_map/all_to_all | solution.py:38
  15.8 0.0 copy-start.6
  15.8 0.6 copy-done.6
  16.5 0.6 dynamic_slice.3
  17.7 0.0 copy-done.4
  17.7 0.0 copy-start.1
  17.7 0.0 copy-start.3
  17.7 2.6 %all-gather.1 = bf16[896,512]{1,0:T(8,128)(2,1)S(1)} all-gather(bf16[448,512]{1,0:T(8,128)(2,1)S(1)} %bitcast.31), channel_id=3, replica_groups={{0,1},{2,3},{4,5},{6,7},{8,9},{10,11},{12,13},{14,15},{16,17},{18,19},{..., dimensions={0}, use_global_device_ids=true | all-gather | bytes 1376256 | tf_op jit(solution)/shard_map/all_gather | solution.py:190
  20.3 1.5 %all-to-all-done.refs_1_ = bf16[4,64,512]{2,1,0:T(8,128)(2,1)S(1)} async-done(((bf16[4,64,512]{2,1,0:T(8,128)(2,1)}), bf16[4,64,512]{2,1,0:T(8,128)(2,1)S(1)}, u32[]{:S(2)}, u32[]{:S(2)}) %all-to-all-start) | async-done | bytes 262176 | tf_op jit(solution)/shard_map/all_to_all | solution.py:38
  21.9 0.0 copy-done.1
  21.9 0.0 copy-done.3
  21.9 0.1 kept_codes.1.refs_1_
  21.9 0.4 decode.1
  22.3 10.9 %all_to_all.25.refs_0_ = bf16[16,56,128]{2,1,0:T(8,128)(2,1)S(1)} all-to-all(bf16[16,56,128]{2,1,0:T(8,128)(2,1)S(1)} %decode.1), channel_id=1, replica_groups={{0,8,16,24,128,136,144,152,256,264,272,280,384,392,400,408},{32,40,48,5..., dimensions={0} | all-to-all | bytes 458752 | tf_op jit(solution)/shard_map/all_to_all | solution.py:38
  33.2 0.7 near_sums.1
  33.9 10.4 %all-to-all-start.2 = ((bf16[4,4,56,128]{3,2,1,0:T(8,128)(2,1)}), bf16[4,4,56,128]{3,2,1,0:T(8,128)(2,1)S(1)}, u32[]{:S(2)}, u32[]{:S(2)}) async-start(bf16[4,4,56,128]{3,2,1,0:T(8,128)(2,1)} %near_sums.1), calls=%async_computation.2 | async-start | bytes 458752 | tf_op jit(solution)/shard_map/all_to_all | solution.py:38
  44.3 0.0 copy-start.5
  44.3 0.7 copy-done.5
  44.9 0.0 copy-start.2
  44.9 0.1 copy.12.refs_2_
  45.1 0.8 copy-done.2
  45.8 0.1 own_base.1
  46.0 5.0 %all-gather.6.refs_3_ = f32[2,28,128]{2,1,0:T(8,128)S(1)} all-gather(f32[1,28,128]{2,1,0:T(8,128)S(1)} %bitcast.28), channel_id=4, replica_groups={{0,1},{2,3},{4,5},{6,7},{8,9},{10,11},{12,13},{14,15},{16,17},{18,19},{..., dimensions={0}, use_global_device_ids=true | all-gather | bytes 43008 | tf_op jit(solution)/shard_map/all_gather | solution.py:190
  51.0 1.9 %all-gather.3 = bf16[128,512]{1,0:T(8,128)(2,1)S(1)} all-gather(bf16[64,512]{1,0:T(8,128)(2,1)S(1)} %kept_codes.1.refs_1_), channel_id=5, replica_groups={{0,1},{2,3},{4,5},{6,7},{8,9},{10,11},{12,13},{14,15},{16,17},{18,19},{..., dimensions={0}, use_global_device_ids=true | all-gather | bytes 196608 | tf_op jit(solution)/shard_map/all_gather | solution.py:190
  52.9 3.8 %all-to-all-done.2.refs_2_ = bf16[4,4,56,128]{3,2,1,0:T(8,128)(2,1)S(1)} async-done(((bf16[4,4,56,128]{3,2,1,0:T(8,128)(2,1)}), bf16[4,4,56,128]{3,2,1,0:T(8,128)(2,1)S(1)}, u32[]{:S(2)}, u32[]{:S(2)}) %all-to-all-start.2) | async-done | bytes 229408 | tf_op jit(solution)/shard_map/all_to_all | solution.py:38
  56.7 0.2 suffixes.1
  56.9 13.7 %all_to_all.26.refs_1_ = bf16[16,64,128]{2,1,0:T(8,128)(2,1)S(1)} all-to-all(bf16[16,64,128]{2,1,0:T(8,128)(2,1)S(1)} %suffixes.1), channel_id=1, replica_groups={{0,8,16,24,128,136,144,152,256,264,272,280,384,392,400,408},{32,40,48,5..., dimensions={0} | all-to-all | bytes 524288 | tf_op jit(solution)/shard_map/all_to_all | solution.py:38
  70.6 1.0 %back.1 = bf16[4,64,512]{2,1,0:T(8,128)(2,1)} custom-call(s32[1]{0:T(128)} %bitcast.7.refs_0_.refs_1_, bf16[16,64,128]{2,1,0:T(8,128)(2,1)S(1)} %all_to_all.26.refs_1_, bf16[2,448,512]{2,1,0:T(8,128)(2,1)S(1)} %bitcast.21), custom_call_target="tpu_custom_call" | custom-call | tf_op jit(solution)/shard_map/back/pallas_call | solution.py:74
  71.6 6.3 %all-to-all-start.4 = ((bf16[4,64,512]{2,1,0:T(8,128)(2,1)}), bf16[4,64,512]{2,1,0:T(8,128)(2,1)S(1)}, u32[]{:S(2)}, u32[]{:S(2)}) async-start(bf16[4,64,512]{2,1,0:T(8,128)(2,1)} %back.1), calls=%async_computation.4 | async-start | bytes 524288 | tf_op jit(solution)/shard_map/all_to_all | solution.py:38
  77.9 5.7 %all-gather.5 = bf16[32,64,128]{2,1,0:T(8,128)(2,1)S(1)} all-gather(bf16[16,64,128]{2,1,0:T(8,128)(2,1)S(1)} %all_to_all.26.refs_1_), channel_id=7, replica_groups={{0,1},{2,3},{4,5},{6,7},{8,9},{10,11},{12,13},{14,15},{16,17},{18,19},{..., dimensions={0}, use_global_device_ids=true | all-gather | bytes 786432 | tf_op jit(solution)/shard_map/all_gather | solution.py:190
  83.6 1.2 %decoder_grads.1 = (bf16[448,512]{1,0:T(8,128)(2,1)}, f32[16,128]{1,0:T(8,128)S(1)}) custom-call(s32[1]{0:T(128)} %bitcast.refs_0_, s32[1]{0:T(128)} %bitcast.7.refs_0_.refs_1_, bf16[2,16,64,128]{3,2,1,0:T(8,128)(2,1)S(1)} %bitcast.22, bf16[2,64,512]{2,1,0:T(8,128)(2,1)S(1)} %bitcast.26), custom_call_target="tpu_custom_call" | custom-call | tf_op jit(solution)/shard_map/decoder_grads/pallas_call | solution.py:74
  84.8 0.7 reshape.40
  85.4 0.0 all-to-all-done.4.refs_1_
  85.4 0.1 kept_grads.1
  85.5 4.6 %all-gather.4 = bf16[128,512]{1,0:T(8,128)(2,1)S(1)} all-gather(bf16[64,512]{1,0:T(8,128)(2,1)S(1)} %kept_grads.1), channel_id=6, replica_groups={{0,1},{2,3},{4,5},{6,7},{8,9},{10,11},{12,13},{14,15},{16,17},{18,19},{..., dimensions={0}, use_global_device_ids=true | all-gather | bytes 196608 | tf_op jit(solution)/shard_map/all_gather | solution.py:190
  90.1 1.0 %encoder_grads.1 = (bf16[448,512]{1,0:T(8,128)(2,1)}, f32[1,512]{1,0:T(1,128)}) custom-call(bf16[2,64,512]{2,1,0:T(8,128)(2,1)S(1)} %bitcast.27, bf16[448,128]{1,0:T(8,128)(2,1)S(1)} %bitcast.25), custom_call_target="tpu_custom_call" | custom-call | tf_op jit(solution)/shard_map/encoder_grads/pallas_call | solution.py:74
Async XLA Ops:
  0.6 1.0 %copy-start = (bf16[448,512]{1,0:T(8,128)(2,1)S(1)}, bf16[448,512]{1,0:T(8,128)(2,1)}, u32[]{:S(2)}) copy-start(bf16[448,512]{1,0:T(8,128)(2,1)} %param.8) | copy-start | bytes 1376260
  12.2 5.5 %copy-start.4 = (bf16[512,448]{0,1:T(8,128)(2,1)S(1)}, bf16[512,448]{0,1:T(8,128)(2,1)}, u32[]{:S(2)}) copy-start(bf16[512,448]{0,1:T(8,128)(2,1)} %param.10) | copy-start | bytes 1376260
  12.2 9.6 %all-to-all-start = ((bf16[4,64,512]{2,1,0:T(8,128)(2,1)}), bf16[4,64,512]{2,1,0:T(8,128)(2,1)S(1)}, u32[]{:S(2)}, u32[]{:S(2)}) async-start(bf16[4,64,512]{2,1,0:T(8,128)(2,1)} %pair_sum.1), calls=%async_computation | async-start | bytes 524288 | tf_op jit(solution)/shard_map/all_to_all | solution.py:38
  15.8 0.7 copy-start.6
  17.7 4.2 %copy-start.1 = (s32[128,512]{1,0:T(8,128)S(1)}, s32[128,512]{1,0:T(8,128)}, u32[]{:S(2)}) copy-start(s32[128,512]{1,0:T(8,128)} %refs_2_.3) | copy-start | bytes 786436
  17.7 4.1 %copy-start.3 = (f32[512]{0:T(512)S(1)}, f32[512]{0:T(512)}, u32[]{:S(2)}) copy-start(f32[512]{0:T(512)} %param.9) | copy-start | bytes 6148
  33.9 22.7 %all-to-all-start.2 = ((bf16[4,4,56,128]{3,2,1,0:T(8,128)(2,1)}), bf16[4,4,56,128]{3,2,1,0:T(8,128)(2,1)S(1)}, u32[]{:S(2)}, u32[]{:S(2)}) async-start(bf16[4,4,56,128]{3,2,1,0:T(8,128)(2,1)} %near_sums.1), calls=%async_computation.2 | async-start | bytes 458752 | tf_op jit(solution)/shard_map/all_to_all | solution.py:38
  44.3 0.7 copy-start.5
  44.9 0.9 copy-start.2
  71.6 13.8 %all-to-all-start.4 = ((bf16[4,64,512]{2,1,0:T(8,128)(2,1)}), bf16[4,64,512]{2,1,0:T(8,128)(2,1)S(1)}, u32[]{:S(2)}, u32[]{:S(2)}) async-start(bf16[4,64,512]{2,1,0:T(8,128)(2,1)} %back.1), calls=%async_computation.4 | async-start | bytes 524288 | tf_op jit(solution)/shard_map/all_to_all | solution.py:38

commit v11 on v10

--- a/solution.py
+++ b/solution.py
@@ -105,10 +105,11 @@
     return ((half_of(at.core, mask).astype(F32) * jnp.sum(pieces.astype(F32), axis=0)).astype(BF),)
 
 
-def decode(at, codes, decoders):
-    codes = split_codes(codes, at.cut)
+def decode(at, pieces, mask, bias, decoders):
+    (my_codes,) = kept_codes(at, pieces, mask, bias)
+    codes = split_codes(my_codes, at.cut)
     first, second = [dot(decoders[core], codes, (1, 1)) for core in range(N_CORE)]
-    return (to_slices(first, second).astype(BF),)
+    return to_slices(first, second).astype(BF), my_codes
 
 
 def near_sums(_, got):
@@ -217,9 +218,10 @@
 
     pieces = swap(total, "wid", CHIP_GROUPS)
     decoders = both_cores(decoder_rows)
-    (my_codes,) = call(kept_codes, half_low, on_core, pieces, kept_mask, encoder_bias[None])
-
-    (got,) = call(decode, [((SLICES, ROWS, tokens), BF)], at_cut, my_codes, decoders)
+
+    got, my_codes = call(
+        decode, [((SLICES, ROWS, tokens), BF)] + half_low, on_core | at_cut, pieces, kept_mask, encoder_bias[None], decoders
+    )
     got = swap(got, "lat", NEAR_GROUPS)
     (got,) = call(near_sums, [((N_FAR, N_Y, ROWS, tokens), BF)], {}, got)
     later_act, later_bias, later_codes, got = lax.optimization_barrier((rows_act, decoder_bias, my_codes, got))

time: 91.7 us -> 92.4 us (level)
    pallas_call x10 -> x9, Pallas kernels: 5.55 us -> 5.51 us  [call(): pl.pallas_call(kernel, out_shape=[jax.ShapeDtypeStruct(shape, dtype) for...]
where the time goes in v11:
time: 92.4 us; the launch traced here: 91.7 us
  blocking collectives  53 us (57%)
  starting transfers between devices  20.2 us (22%)
  Pallas kernels  5.51 us (6%)
  waiting for transfers between devices  5.32 us (6%)
  local copies, waits for them, and re-layouts  5.17 us (6%)
  between operations  1.42 us (2%)
  matrix products  1.14 us (1%)
    all_gather x6, blocking collectives, both_cores(): return lax.all_gather(x, 'wid', axis_index_groups=CORE_GROUPS)  28.4 us
    all_to_all x2, blocking collectives, swap(): return lax.all_to_all(x, axis, 0, 0, axis_index_groups=groups, tiled=False)  24.6 us
    all_to_all x3, starting transfers between devices, swap(): return lax.all_to_all(x, axis, 0, 0, axis_index_groups=groups, tiled=False)  20.2 us
    pallas_call x9, Pallas kernels, call(): pl.pallas_call(kernel, out_shape=[jax.ShapeDtypeStruct(shape, dtype) for...  5.51 us
    all_to_all x3, waiting for transfers between devices, swap(): return lax.all_to_all(x, axis, 0, 0, axis_index_groups=groups, tiled=False)  5.32 us
    unnamed x14, local copies, waits for them, and re-layouts  3.78 us
  transfers between devices with their start and end apart: 3, of which 2 were waited for; matrix products, arithmetic and copies ran while one was open for 2% of the time, Pallas kernels for 1%

profile of v11, /device:TPU:1, one launch (start us, length us, event | category | flops | bytes accessed | tf_op | source)
XLA Modules:
  0.0 91.7 jit_solution(11239054208544430087)
XLA Ops:
  0.6 0.0 copy-start
  0.7 1.0 %copy-done = bf16[448,512]{1,0:T(8,128)(2,1)S(1)} copy-done((bf16[448,512]{1,0:T(8,128)(2,1)S(1)}, bf16[448,512]{1,0:T(8,128)(2,1)}, u32[]{:S(2)}) %copy-start) | copy-done | bytes 458776
  1.7 1.1 %fusion = f32[128,512]{1,0:T(8,128)S(1)} fusion(bf16[128,448]{0,1:T(8,128)(2,1)} %param.7, bf16[448,512]{1,0:T(8,128)(2,1)S(1)} %copy-done), kind=kOutput, calls=%fused_computation | convolution fusion | flops 58720256 | bytes 835584 | tf_op jit(solution)/shard_map/dot_general | solution.py:46
  2.8 8.7 %all-gather = f32[256,512]{1,0:T(8,128)S(1)} all-gather(f32[128,512]{1,0:T(8,128)S(1)} %fusion), channel_id=2, replica_groups={{0,1},{2,3},{4,5},{6,7},{8,9},{10,11},{12,13},{14,15},{16,17},{18,19},{..., dimensions={0}, use_global_device_ids=true | all-gather | bytes 786432 | tf_op jit(solution)/shard_map/all_gather | solution.py:191
  11.5 0.7 pair_sum.1
  12.2 0.0 copy-start.4
  12.2 3.5 %all-to-all-start = ((bf16[4,64,512]{2,1,0:T(8,128)(2,1)}), bf16[4,64,512]{2,1,0:T(8,128)(2,1)S(1)}, u32[]{:S(2)}, u32[]{:S(2)}) async-start(bf16[4,64,512]{2,1,0:T(8,128)(2,1)} %pair_sum.1), calls=%async_computation | async-start | bytes 524288 | tf_op jit(solution)/shard_map/all_to_all | solution.py:38
  15.8 0.0 copy-start.6
  15.8 0.6 copy-done.6
  16.5 0.6 dynamic_slice.3
  17.7 0.0 copy-done.4
  17.7 0.0 copy-start.1
  17.7 2.6 %all-gather.1 = bf16[896,512]{1,0:T(8,128)(2,1)S(1)} all-gather(bf16[448,512]{1,0:T(8,128)(2,1)S(1)} %bitcast.31), channel_id=3, replica_groups={{0,1},{2,3},{4,5},{6,7},{8,9},{10,11},{12,13},{14,15},{16,17},{18,19},{..., dimensions={0}, use_global_device_ids=true | all-gather | bytes 1376256 | tf_op jit(solution)/shard_map/all_gather | solution.py:191
  20.3 1.5 %all-to-all-done.refs_2_ = bf16[4,64,512]{2,1,0:T(8,128)(2,1)S(1)} async-done(((bf16[4,64,512]{2,1,0:T(8,128)(2,1)}), bf16[4,64,512]{2,1,0:T(8,128)(2,1)S(1)}, u32[]{:S(2)}, u32[]{:S(2)}) %all-to-all-start) | async-done | bytes 262176 | tf_op jit(solution)/shard_map/all_to_all | solution.py:38
  21.9 0.0 copy-start.3
  21.9 0.0 copy-done.1
  21.9 0.7 copy-done.3
  22.5 0.4 decode.1
  23.0 10.9 %all_to_all.25.refs_0_ = bf16[16,56,128]{2,1,0:T(8,128)(2,1)S(1)} all-to-all(bf16[16,56,128]{2,1,0:T(8,128)(2,1)S(1)} %get-tuple-element.26), channel_id=1, replica_groups={{0,8,16,24,128,136,144,152,256,264,272,280,384,392,400,408},{32,40,48,5..., dimensions={0} | all-to-all | bytes 458752 | tf_op jit(solution)/shard_map/all_to_all | solution.py:38
  33.8 0.7 near_sums.1
  34.5 10.3 %all-to-all-start.2 = ((bf16[4,4,56,128]{3,2,1,0:T(8,128)(2,1)}), bf16[4,4,56,128]{3,2,1,0:T(8,128)(2,1)S(1)}, u32[]{:S(2)}, u32[]{:S(2)}) async-start(bf16[4,4,56,128]{3,2,1,0:T(8,128)(2,1)} %near_sums.1), calls=%async_computation.2 | async-start | bytes 458752 | tf_op jit(solution)/shard_map/all_to_all | solution.py:38
  44.9 0.0 copy-start.5
  44.9 0.7 copy-done.5
  45.6 0.0 copy-start.2
  45.6 0.1 copy.12.refs_2_
  45.7 0.8 copy-done.2
  46.5 0.1 own_base.1
  46.6 5.0 %all-gather.6.refs_3_ = f32[2,28,128]{2,1,0:T(8,128)S(1)} all-gather(f32[1,28,128]{2,1,0:T(8,128)S(1)} %bitcast.28), channel_id=4, replica_groups={{0,1},{2,3},{4,5},{6,7},{8,9},{10,11},{12,13},{14,15},{16,17},{18,19},{..., dimensions={0}, use_global_device_ids=true | all-gather | bytes 43008 | tf_op jit(solution)/shard_map/all_gather | solution.py:191
  51.6 1.9 %all-gather.3 = bf16[128,512]{1,0:T(8,128)(2,1)S(1)} all-gather(bf16[64,512]{1,0:T(8,128)(2,1)S(1)} %get-tuple-element.30), channel_id=5, replica_groups={{0,1},{2,3},{4,5},{6,7},{8,9},{10,11},{12,13},{14,15},{16,17},{18,19},{..., dimensions={0}, use_global_device_ids=true | all-gather | bytes 196608 | tf_op jit(solution)/shard_map/all_gather | solution.py:191
  53.5 3.8 %all-to-all-done.2.refs_2_ = bf16[4,4,56,128]{3,2,1,0:T(8,128)(2,1)S(1)} async-done(((bf16[4,4,56,128]{3,2,1,0:T(8,128)(2,1)}), bf16[4,4,56,128]{3,2,1,0:T(8,128)(2,1)S(1)}, u32[]{:S(2)}, u32[]{:S(2)}) %all-to-all-start.2) | async-done | bytes 229408 | tf_op jit(solution)/shard_map/all_to_all | solution.py:38
  57.3 0.2 suffixes.1
  57.5 13.7 %all_to_all.26.refs_1_ = bf16[16,64,128]{2,1,0:T(8,128)(2,1)S(1)} all-to-all(bf16[16,64,128]{2,1,0:T(8,128)(2,1)S(1)} %suffixes.1), channel_id=1, replica_groups={{0,8,16,24,128,136,144,152,256,264,272,280,384,392,400,408},{32,40,48,5..., dimensions={0} | all-to-all | bytes 524288 | tf_op jit(solution)/shard_map/all_to_all | solution.py:38
  71.2 1.1 %back.1 = bf16[4,64,512]{2,1,0:T(8,128)(2,1)} custom-call(s32[1]{0:T(128)} %bitcast.6.refs_1_.refs_0_, bf16[16,64,128]{2,1,0:T(8,128)(2,1)S(1)} %all_to_all.26.refs_1_, bf16[2,448,512]{2,1,0:T(8,128)(2,1)S(1)} %bitcast.21), custom_call_target="tpu_custom_call" | custom-call | tf_op jit(solution)/shard_map/back/pallas_call | solution.py:74
  72.3 6.3 %all-to-all-start.4 = ((bf16[4,64,512]{2,1,0:T(8,128)(2,1)}), bf16[4,64,512]{2,1,0:T(8,128)(2,1)S(1)}, u32[]{:S(2)}, u32[]{:S(2)}) async-start(bf16[4,64,512]{2,1,0:T(8,128)(2,1)} %back.1), calls=%async_computation.4 | async-start | bytes 524288 | tf_op jit(solution)/shard_map/all_to_all | solution.py:38
  78.6 5.6 %all-gather.5 = bf16[32,64,128]{2,1,0:T(8,128)(2,1)S(1)} all-gather(bf16[16,64,128]{2,1,0:T(8,128)(2,1)S(1)} %all_to_all.26.refs_1_), channel_id=7, replica_groups={{0,1},{2,3},{4,5},{6,7},{8,9},{10,11},{12,13},{14,15},{16,17},{18,19},{..., dimensions={0}, use_global_device_ids=true | all-gather | bytes 786432 | tf_op jit(solution)/shard_map/all_gather | solution.py:191
  84.2 1.2 %decoder_grads.1 = (bf16[448,512]{1,0:T(8,128)(2,1)}, f32[16,128]{1,0:T(8,128)S(1)}) custom-call(s32[1]{0:T(128)} %bitcast.refs_0_, s32[1]{0:T(128)} %bitcast.6.refs_1_.refs_0_, bf16[2,16,64,128]{3,2,1,0:T(8,128)(2,1)S(1)} %bitcast.22, bf16[2,64,512]{2,1,0:T(8,128)(2,1)S(1)} %bitcast.26), custom_call_target="tpu_custom_call" | custom-call | tf_op jit(solution)/shard_map/decoder_grads/pallas_call | solution.py:74
  85.4 0.7 reshape.40
  86.0 0.0 all-to-all-done.4.refs_1_
  86.0 0.1 kept_grads.1
  86.1 4.6 %all-gather.4 = bf16[128,512]{1,0:T(8,128)(2,1)S(1)} all-gather(bf16[64,512]{1,0:T(8,128)(2,1)S(1)} %kept_grads.1), channel_id=6, replica_groups={{0,1},{2,3},{4,5},{6,7},{8,9},{10,11},{12,13},{14,15},{16,17},{18,19},{..., dimensions={0}, use_global_device_ids=true | all-gather | bytes 196608 | tf_op jit(solution)/shard_map/all_gather | solution.py:191
  90.7 1.0 %encoder_grads.1 = (bf16[448,512]{1,0:T(8,128)(2,1)}, f32[1,512]{1,0:T(1,128)}) custom-call(bf16[2,64,512]{2,1,0:T(8,128)(2,1)S(1)} %bitcast.27, bf16[448,128]{1,0:T(8,128)(2,1)S(1)} %bitcast.25), custom_call_target="tpu_custom_call" | custom-call | tf_op jit(solution)/shard_map/encoder_grads/pallas_call | solution.py:74
Async XLA Ops:
  0.6 1.0 %copy-start = (bf16[448,512]{1,0:T(8,128)(2,1)S(1)}, bf16[448,512]{1,0:T(8,128)(2,1)}, u32[]{:S(2)}) copy-start(bf16[448,512]{1,0:T(8,128)(2,1)} %param.8) | copy-start | bytes 1376260
  12.2 5.5 %copy-start.4 = (bf16[512,448]{0,1:T(8,128)(2,1)S(1)}, bf16[512,448]{0,1:T(8,128)(2,1)}, u32[]{:S(2)}) copy-start(bf16[512,448]{0,1:T(8,128)(2,1)} %param.10) | copy-start | bytes 1376260
  12.2 9.6 %all-to-all-start = ((bf16[4,64,512]{2,1,0:T(8,128)(2,1)}), bf16[4,64,512]{2,1,0:T(8,128)(2,1)S(1)}, u32[]{:S(2)}, u32[]{:S(2)}) async-start(bf16[4,64,512]{2,1,0:T(8,128)(2,1)} %pair_sum.1), calls=%async_computation | async-start | bytes 524288 | tf_op jit(solution)/shard_map/all_to_all | solution.py:38
  15.8 0.7 copy-start.6
  17.7 4.2 %copy-start.1 = (s32[128,512]{1,0:T(8,128)S(1)}, s32[128,512]{1,0:T(8,128)}, u32[]{:S(2)}) copy-start(s32[128,512]{1,0:T(8,128)} %refs_2_.1) | copy-start | bytes 786436
  21.9 0.7 copy-start.3
  34.5 22.7 %all-to-all-start.2 = ((bf16[4,4,56,128]{3,2,1,0:T(8,128)(2,1)}), bf16[4,4,56,128]{3,2,1,0:T(8,128)(2,1)S(1)}, u32[]{:S(2)}, u32[]{:S(2)}) async-start(bf16[4,4,56,128]{3,2,1,0:T(8,128)(2,1)} %near_sums.1), calls=%async_computation.2 | async-start | bytes 458752 | tf_op jit(solution)/shard_map/all_to_all | solution.py:38
  44.9 0.7 copy-start.5
  45.6 0.9 copy-start.2
  72.3 13.7 %all-to-all-start.4 = ((bf16[4,64,512]{2,1,0:T(8,128)(2,1)}), bf16[4,64,512]{2,1,0:T(8,128)(2,1)S(1)}, u32[]{:S(2)}, u32[]{:S(2)}) async-start(bf16[4,64,512]{2,1,0:T(8,128)(2,1)} %back.1), calls=%async_computation.4 | async-start | bytes 524288 | tf_op jit(solution)/shard_map/all_to_all | solution.py:38
